TPU v7x, 512 devices: a whole 4x4x16 slice. The times are simulated.
512 devices in a mesh: dp: 32 (over z, y_lo), seq: 16 (over x, y_hi, core).
Axes of the slice: x: 4, y: 4 (y_hi: 2, y_lo: 2; y = y_hi * 2 + y_lo), z: 16, core: 2. Of those that a mesh axis runs over, the one named last changes fastest.
Arguments:
- inputs: bfloat16 [64, 8192, 768], P('dp', 'seq'), may hold values from -6 to 6
- conv_weight: bfloat16 [3, 768, 384], P(None, 'dp', 'seq'), may hold values from -0.125 to 0.125
- point_weight: bfloat16 [384, 768], P('seq', 'dp'), may hold values from -0.3125 to 0.3125
- cotangent: bfloat16 [64, 8192, 768], P('dp', 'seq'), may hold values from -6 to 6
Outputs:
- input_grad: bfloat16 [64, 8192, 768], P('dp', 'seq')
- conv_grad: float32 [3, 768, 384], P(None, 'dp', 'seq')
All inputs are finite; a program needn't handle non-finite values.
Results may differ from a plain program's by a relative error of at most 0.0054.
Values may be sent and summed in bfloat16 or wider, within the bound.
No kernel may reach another device: no remote copies, remote signals or barrier semaphores. Data moves between devices by JAX's collectives and lax.ppermute only.
A program may use at most 64 MiB of HBM per device.

v0:
```python
import jax
import jax.numpy as jnp
from jax import lax
from jax.sharding import PartitionSpec as P

SPAN = 2


EPSILON = 1e-06
GELU_SCALE = 0.7978845608028654
GELU_CUBIC = 0.044715


def from_behind(x, axis, by):
    peers = lax.axis_size(axis)
    pairs = [(i, i + by) for i in range(peers) if 0 <= i + by < peers]
    return lax.ppermute(x, axis, pairs)


def gelu_tanh(values):
    return (
        0.5
        * values
        * (1.0 + jnp.tanh(GELU_SCALE * (values + GELU_CUBIC * values * values * values)))
    )


def gelu_slope(values):
    tangent = jnp.tanh(GELU_SCALE * (values + GELU_CUBIC * values * values * values))
    return 0.5 * (1.0 + tangent) + 0.5 * values * (1.0 - tangent * tangent) * GELU_SCALE * (
        1.0 + 3.0 * GELU_CUBIC * values * values
    )


def product(left, right):
    return jnp.dot(left, right, preferred_element_type=jnp.float32)


def outer_sum(left, right):
    return jnp.einsum("rc,rf->cf", left, right, preferred_element_type=jnp.float32)


def to_half(values):
    return lax.optimization_barrier(values.astype(jnp.bfloat16))


def from_lower(array):
    moved = from_behind(array, "seq", SPAN)
    return moved


def from_upper(array):
    moved = from_behind(array, "seq", -SPAN)
    return moved


def body(inputs, conv_weight, point_weight, cotangent):
    samp_count, bin_count, width = inputs.shape
    row_count = samp_count * bin_count
    grad_scale = float(row_count * lax.axis_size("dp") * lax.axis_size("seq")) ** (-0.5)
    columns = (
        lax.all_gather(conv_weight, "seq", axis=2, tiled=True),
        lax.all_gather(point_weight, "seq", axis=0, tiled=True),
    )
    conv_full, point_full = (
        lax.all_gather(columns[0], "dp", axis=1, tiled=True),
        lax.all_gather(columns[1], "dp", axis=1, tiled=True),
    )
    hidden = conv_full.shape[2]
    floats = inputs.astype(jnp.float32)
    row_scale = lax.rsqrt(jnp.mean(floats * floats, axis=-1, keepdims=True) + EPSILON)
    normed = floats * row_scale
    acted = gelu_tanh(normed).astype(jnp.bfloat16)
    acted_flat = acted.reshape(row_count, width)
    lower_acts = from_lower(acted).reshape(row_count, width)
    upper_acts = from_upper(acted).reshape(row_count, width)
    shifted_low = to_half(product(lower_acts, conv_full[0])).astype(jnp.float32)
    shifted_high = to_half(product(upper_acts, conv_full[2])).astype(jnp.float32)
    preact = shifted_low + product(acted_flat, conv_full[1]) + shifted_high
    cot_flat = cotangent.reshape(row_count, width)
    grad_inner = product(cot_flat, point_full.T)
    grad_pre = (grad_inner * gelu_slope(preact)).astype(jnp.bfloat16)
    grad_blocks = grad_pre.reshape(samp_count, bin_count, hidden)
    grad_upper = from_upper(grad_blocks).reshape(row_count, hidden)
    grad_lower = from_lower(grad_blocks).reshape(row_count, hidden)
    grad_act = (
        product(grad_upper, conv_full[0].T)
        + product(grad_pre, conv_full[1].T)
        + product(grad_lower, conv_full[2].T)
    )
    normed_flat = normed.reshape(row_count, width)
    scale_flat = row_scale.reshape(row_count, 1)
    grad_norm = grad_act * gelu_slope(normed_flat)
    center = jnp.mean(grad_norm * normed_flat, axis=-1, keepdims=True)
    grad_input = cot_flat.astype(jnp.float32) + scale_flat * (grad_norm - normed_flat * center)
    input_grad = grad_input.astype(jnp.bfloat16).reshape(samp_count, bin_count, width)
    conv_terms = (
        jnp.stack(
            [
                outer_sum(acted_flat, grad_upper),
                outer_sum(acted_flat, grad_pre),
                outer_sum(acted_flat, grad_lower),
            ],
            axis=0,
        )
        * grad_scale
    )
    partial_terms = lax.psum_scatter(conv_terms, "dp", scatter_dimension=1, tiled=True)
    conv_grad = lax.psum_scatter(partial_terms, "seq", scatter_dimension=2, tiled=True)
    return (input_grad, conv_grad)


def solution(mesh):
    return jax.shard_map(
        body,
        mesh=mesh,
        in_specs=(P("dp", "seq", None), P(None, "dp", "seq"), P("seq", "dp"), P("dp", "seq", None)),
        out_specs=(P("dp", "seq", None), P(None, "dp", "seq")),
        check_vma=False,
    )
```

profile of v0, /device:TPU:1, one launch (start us, length us, event | category | flops | bytes accessed | tf_op | source)
XLA Modules:
  0.0 558.5 jit_solution(1335041176882694279)
XLA Ops:
  8.0 26.8 %all_gather.14 = bf16[3,24,384]{1,0,2:T(4,128)(2,1)S(1)} all-gather(bf16[3,24,24]{1,0,2:T(4,128)(2,1)S(1)} %copy.18), channel_id=1, replica_groups=mesh['dp'=32,'seq'=16] {'seq'}, dimensions={2}, use_global_device_ids=true | all-gather | bytes 58752 | tf_op jit(solution)/shard_map/all_gather | solution.py:62
  35.7 1.9 fusion
  37.7 2.4 fusion.5
  40.1 6.3 %collective-permute-start = (bf16[2,512,768]{2,1,0:T(8,128)(2,1)}, bf16[2,512,768]{2,1,0:T(8,128)(2,1)}, u32[]{:S(2)}, u32[]{:S(2)}) collective-permute-start(bf16[2,512,768]{2,1,0:T(8,128)(2,1)} %get-tuple-element.2), channel_id=1, source_target_pairs={{0,2},{1,3},{2,4},{3,5},{4,6},{5,7},{6,8},{7,9},{8,10},{9,11},{10,... | collective-permute-start | bytes 4718600 | tf_op jit(solution)/shard_map/ppermute | solution.py:17
  46.3 1.3 collective-permute-start.1
  47.6 96.7 %all_gather.12 = bf16[384,24]{1,0:T(8,128)(2,1)S(1)} all-gather(bf16[24,24]{1,0:T(8,128)(2,1)S(1)} %copy-done.7), channel_id=1, replica_groups=mesh['dp'=32,'seq'=16] {'seq'}, dimensions={0}, use_global_device_ids=true | all-gather | bytes 19584 | tf_op jit(solution)/shard_map/all_gather | solution.py:63
  144.4 58.0 %all_gather.13 = bf16[384,768]{0,1:T(8,128)(2,1)S(1)} all-gather(bf16[384,24]{0,1:T(8,128)(2,1)S(1)} %copy.17), channel_id=1, replica_groups=mesh['dp'=32,'seq'=16] {'dp'}, dimensions={1}, use_global_device_ids=true | all-gather | bytes 608256 | tf_op jit(solution)/shard_map/all_gather | solution.py:67
  202.4 3.6 fusion.31
  205.9 2.6 convolution_convert_fusion.1
  208.6 2.4 convolution_convert_fusion
  211.0 2.5 fusion.28
  214.7 4.5 collective-permute-start.3
  219.2 1.3 collective-permute-start.2
  220.5 2.4 convolution_bitcast_fusion.1
  223.0 24.0 %collective-permute-done.3 = bf16[2,512,384]{2,1,0:T(8,128)(2,1)S(1)} collective-permute-done((bf16[2,512,384]{2,1,0:T(8,128)(2,1)S(1)}, bf16[2,512,384]{2,1,0:T(8,128)(2,1)S(1)}, u32[]{:S(2)}, u32[]{:S(2)}) %collective-permute-start.3) | collective-permute-done | bytes 786464 | tf_op jit(solution)/shard_map/ppermute | solution.py:17
  247.0 2.7 convolution_bitcast_fusion
  250.6 2.4 convolution_bitcast_fusion.2
  253.0 2.1 maximum_multiply_fusion
  257.3 2.5 fusion.27
  260.9 4.6 fusion.16
  265.5 113.1 %reduce-scatter.3.cloned.1.call-done = f32[3,24,384]{2,1,0:T(8,128)} async-done(((f32[3,768,384]{2,1,0:T(8,128)}), f32[3,24,384]{2,1,0:T(8,128)}) %reduce-scatter.3.cloned.1.call-update) | async-done | bytes 110608 | tf_op jit(solution)/shard_map/reduce_scatter | solution.py:108
  378.7 4.2 fusion.15
  383.0 167.4 %all-reduce.3.cloned.1.call-done = f32[3,24,384]{2,1,0:T(8,128)} async-done(((f32[3,24,384]{2,1,0:T(8,128)}), f32[3,24,384]{2,1,0:T(8,128)}) %all-reduce.3.cloned.1.call-update) | async-done | bytes 110608
  550.4 1.6 constant_dynamic-slice_fusion
  (39 shorter events, 6.6 us)
Async XLA Ops:
  7.2 198.8 %all-gather.2.cloned.1.call-start = ((), (), s32[]{:S(2)}) async-start(), calls=%async_computation.1 | async-start | bytes 1824768 | tf_op jit(solution)/shard_map/all_gather | solution.py:66
  35.7 343.0 %reduce-scatter.3.cloned.1.call-start = ((), (), s32[]{:S(2)}) async-start(), calls=%async_computation.2 | async-start | bytes 3649536 | tf_op jit(solution)/shard_map/reduce_scatter | solution.py:108
  35.7 1.9 copy-start
  37.7 10.0 %copy-start.7 = (bf16[24,24]{1,0:T(8,128)(2,1)S(1)}, bf16[24,24]{1,0:T(8,128)(2,1)}, u32[]{:S(2)}) copy-start(bf16[24,24]{1,0:T(8,128)(2,1)} %param.6) | copy-start | bytes 3460
  40.1 165.9 %collective-permute-start = (bf16[2,512,768]{2,1,0:T(8,128)(2,1)}, bf16[2,512,768]{2,1,0:T(8,128)(2,1)}, u32[]{:S(2)}, u32[]{:S(2)}) collective-permute-start(bf16[2,512,768]{2,1,0:T(8,128)(2,1)} %get-tuple-element.2), channel_id=1, source_target_pairs={{0,2},{1,3},{2,4},{3,5},{4,6},{5,7},{6,8},{7,9},{8,10},{9,11},{10,... | collective-permute-start | bytes 4718600 | tf_op jit(solution)/shard_map/ppermute | solution.py:17
  46.3 162.2 %collective-permute-start.1 = (bf16[2,512,768]{2,1,0:T(8,128)(2,1)}, bf16[2,512,768]{2,1,0:T(8,128)(2,1)}, u32[]{:S(2)}, u32[]{:S(2)}) collective-permute-start(bf16[2,512,768]{2,1,0:T(8,128)(2,1)} %get-tuple-element.2), channel_id=1, source_target_pairs={{2,0},{3,1},{4,2},{5,3},{6,4},{7,5},{8,6},{9,7},{10,8},{11,9},{12,... | collective-permute-start | bytes 4718600 | tf_op jit(solution)/shard_map/ppermute | solution.py:17
  205.9 2.7 copy-start.3
  211.0 2.5 copy-start.2
  214.7 8.2 %copy-start.1 = (bf16[1024,384]{1,0:T(8,128)(2,1)}, bf16[1024,384]{1,0:T(8,128)(2,1)S(1)}, u32[]{:S(2)}) copy-start(bf16[1024,384]{1,0:T(8,128)(2,1)S(1)} %fusion.25) | copy-start | bytes 2359300
  214.7 32.3 %collective-permute-start.3 = (bf16[2,512,384]{2,1,0:T(8,128)(2,1)S(1)}, bf16[2,512,384]{2,1,0:T(8,128)(2,1)S(1)}, u32[]{:S(2)}, u32[]{:S(2)}) collective-permute-start(bf16[2,512,384]{2,1,0:T(8,128)(2,1)S(1)} %bitcast.77), channel_id=1, source_target_pairs={{0,2},{1,3},{2,4},{3,5},{4,6},{5,7},{6,8},{7,9},{8,10},{9,11},{10,... | collective-permute-start | bytes 2359304 | tf_op jit(solution)/shard_map/ppermute | solution.py:17
  219.2 30.5 %collective-permute-start.2 = (bf16[2,512,384]{2,1,0:T(8,128)(2,1)S(1)}, bf16[2,512,384]{2,1,0:T(8,128)(2,1)S(1)}, u32[]{:S(2)}, u32[]{:S(2)}) collective-permute-start(bf16[2,512,384]{2,1,0:T(8,128)(2,1)S(1)} %bitcast.78), channel_id=1, source_target_pairs={{2,0},{3,1},{4,2},{5,3},{6,4},{7,5},{8,6},{9,7},{10,8},{11,9},{12,... | collective-permute-start | bytes 2359304 | tf_op jit(solution)/shard_map/ppermute | solution.py:17
  247.0 2.7 copy-start.8
  249.7 0.9 copy-start.5
  255.1 295.2 %all-reduce.3.cloned.1.call-start = ((), (), s32[]{:S(2)}) async-start(), calls=%async_computation.3 | async-start | bytes 221184
  257.3 2.5 copy-start.4
  257.3 2.5 copy-start.6
  259.8 1.1 copy-start.9
Sparse Core Ops, SparseCore 0:
  35.8 147.5 all-gather.1
  255.2 123.4 reduce-scatter.2
  381.9 168.4 all-reduce.2
where the time goes:
time: 559 us; the launch traced here: 558 us
  waiting for transfers between devices  305 us (55%)
  blocking collectives  181 us (32%)
  matrix products  26.7 us (5%)
  between operations  14.6 us (3%)
  starting transfers between devices  13.6 us (2%)
  other arithmetic  11.8 us (2%)
  local copies, waits for them, and re-layouts  5.6 us (1%)
    unnamed x4, waiting for transfers between devices  167 us
    reduce_scatter x1, waiting for transfers between devices, body(): lax.psum_scatter(conv_terms, 'dp', scatter_dimension=1, tiled=True)  113 us
    all_gather x1, blocking collectives, body(): lax.all_gather(point_weight, 'seq', axis=0, tiled=True)  96.7 us
    all_gather x1, blocking collectives, body(): lax.all_gather(columns[1], 'dp', axis=1, tiled=True)  58 us
    all_gather x1, blocking collectives, body(): lax.all_gather(conv_weight, 'seq', axis=2, tiled=True)  26.8 us
    ppermute x4, waiting for transfers between devices, from_behind(): return lax.ppermute(x, axis, pairs)  24.1 us
    dot_general x7, matrix products, product(): return jnp.dot(left, right, preferred_element_type=jnp.float32)  19.1 us
    ppermute x4, starting transfers between devices, from_behind(): return lax.ppermute(x, axis, pairs)  13.3 us
  transfers between devices with their start and end apart: 7, of which 3 were waited for; matrix products, arithmetic and copies ran while one was open for 5% of the time, Pallas kernels for 0%

commit v1 on v0

v1 whole, which is shorter than its diff:
```python
import jax
import jax.numpy as jnp
from jax import lax
from jax.sharding import PartitionSpec as P

SPAN = 2
LANES = 128

EPSILON = 1e-06
GELU_SCALE = 0.7978845608028654
GELU_CUBIC = 0.044715


def from_behind(x, axis, by):
    peers = lax.axis_size(axis)
    pairs = [(i, i + by) for i in range(peers) if 0 <= i + by < peers]
    return lax.ppermute(x, axis, pairs)


def gelu_tanh(values):
    return (
        0.5
        * values
        * (1.0 + jnp.tanh(GELU_SCALE * (values + GELU_CUBIC * values * values * values)))
    )


def gelu_slope(values):
    tangent = jnp.tanh(GELU_SCALE * (values + GELU_CUBIC * values * values * values))
    return 0.5 * (1.0 + tangent) + 0.5 * values * (1.0 - tangent * tangent) * GELU_SCALE * (
        1.0 + 3.0 * GELU_CUBIC * values * values
    )


def product(left, right):
    return lax.dot_general(left, right, (((1,), (0,)), ((), ())), preferred_element_type=jnp.float32)


def product_nt(left, right):
    return lax.dot_general(left, right, (((1,), (1,)), ((), ())), preferred_element_type=jnp.float32)


def product_tn(left, right):
    return lax.dot_general(left, right, (((0,), (0,)), ((), ())), preferred_element_type=jnp.float32)


def to_half(values):
    return lax.optimization_barrier(values.astype(jnp.bfloat16))


def everywhere(shard, axis):
    peers = lax.axis_size(axis)
    copies = jnp.broadcast_to(shard[None], (peers,) + shard.shape)
    return lax.all_to_all(copies, axis, 0, 0)


def normalize(inputs):
    floats = inputs.astype(jnp.float32)
    row_scale = lax.rsqrt(jnp.mean(floats * floats, axis=-1, keepdims=True) + EPSILON)
    return floats * row_scale, row_scale


def body(inputs, conv_weight, point_weight, cotangent):
    samp_count, bin_count, width = inputs.shape
    row_count = samp_count * bin_count
    n_dp, n_seq = lax.axis_size("dp"), lax.axis_size("seq")
    grad_scale = float(row_count * n_dp * n_seq) ** (-0.5)
    taps, c_part, f_part = conv_weight.shape
    hidden = f_part * n_seq

    tap_lanes = (taps + 1) * f_part
    shard = jnp.concatenate(
        [conv_weight[tap] for tap in range(taps)] + [point_weight.T], axis=1
    )
    shard = jnp.pad(shard, ((0, 0), (0, LANES - tap_lanes)))
    by_channel = everywhere(shard, "dp").reshape(width, LANES)
    by_tap = by_channel.T[:tap_lanes]
    gathered = everywhere(by_tap, "seq").reshape(n_seq, taps + 1, f_part, width)
    weights = jnp.transpose(gathered, (1, 0, 2, 3)).reshape(taps + 1, hidden, width)

    lower_in = from_behind(inputs, "seq", SPAN)
    upper_in = from_behind(inputs, "seq", -SPAN)

    normed, row_scale = normalize(inputs)
    acted = gelu_tanh(normed).astype(jnp.bfloat16).reshape(row_count, width)
    lower_acts = gelu_tanh(normalize(lower_in)[0]).astype(jnp.bfloat16).reshape(row_count, width)
    upper_acts = gelu_tanh(normalize(upper_in)[0]).astype(jnp.bfloat16).reshape(row_count, width)
    cot_flat = cotangent.reshape(row_count, width)

    grad_inner = product_nt(cot_flat, weights[3])
    shifted_low = to_half(product_nt(lower_acts, weights[0])).astype(jnp.float32)
    shifted_high = to_half(product_nt(upper_acts, weights[2])).astype(jnp.float32)
    preact = shifted_low + product_nt(acted, weights[1]) + shifted_high
    grad_pre = (grad_inner * gelu_slope(preact)).astype(jnp.bfloat16)

    terms = [
        (product_tn(grad_pre, acts) * grad_scale).astype(jnp.bfloat16)
        for acts in (lower_acts, acted, upper_acts)
    ]
    sums = [
        jnp.sum(
            lax.all_to_all(term.reshape(n_seq, f_part, width), "seq", 0, 0).astype(jnp.float32),
            axis=0,
        )
        for term in terms
    ]
    by_lane = jnp.concatenate(sums, axis=0).T
    by_lane = jnp.pad(by_lane, ((0, 0), (0, LANES - taps * f_part))).astype(jnp.bfloat16)
    parts = lax.all_to_all(by_lane.reshape(n_dp, c_part, LANES), "dp", 0, 0)
    total = jnp.sum(parts.astype(jnp.float32), axis=0)
    conv_grad = jnp.stack([total[:, t * f_part : (t + 1) * f_part] for t in range(taps)], axis=0)

    grad_blocks = grad_pre.reshape(samp_count, bin_count, hidden)
    grad_upper = from_behind(grad_blocks, "seq", -SPAN).reshape(row_count, hidden)
    grad_lower = from_behind(grad_blocks, "seq", SPAN).reshape(row_count, hidden)
    grad_act = (
        product(grad_upper, weights[0])
        + product(grad_pre, weights[1])
        + product(grad_lower, weights[2])
    )
    normed_flat = normed.reshape(row_count, width)
    scale_flat = row_scale.reshape(row_count, 1)
    grad_norm = grad_act * gelu_slope(normed_flat)
    center = jnp.mean(grad_norm * normed_flat, axis=-1, keepdims=True)
    grad_input = cot_flat.astype(jnp.float32) + scale_flat * (grad_norm - normed_flat * center)
    input_grad = grad_input.astype(jnp.bfloat16).reshape(samp_count, bin_count, width)
    return (input_grad, conv_grad)


def solution(mesh):
    return jax.shard_map(
        body,
        mesh=mesh,
        in_specs=(P("dp", "seq", None), P(None, "dp", "seq"), P("seq", "dp"), P("dp", "seq", None)),
        out_specs=(P("dp", "seq", None), P(None, "dp", "seq")),
        check_vma=False,
    )
```

time: 559 us -> 237 us (0.42)
  the two profiles are of different devices: /device:TPU:1 before, /device:TPU:4 now
where the time goes in v1:
time: 237 us; the launch traced here: 236 us
  starting transfers between devices  108 us (46%)
  waiting for transfers between devices  72.1 us (30%)
  other arithmetic  27.6 us (12%)
  matrix products  15.9 us (7%)
  local copies, waits for them, and re-layouts  11.3 us (5%)
    all_to_all x2, starting transfers between devices, everywhere(): return lax.all_to_all(copies, axis, 0, 0)  54.5 us
    all_to_all x3, waiting for transfers between devices, body(): lax.all_to_all(term.reshape(n_seq, f_part, width), 'seq', 0, 0)  35.5 us
    all_to_all x2, waiting for transfers between devices, everywhere(): return lax.all_to_all(copies, axis, 0, 0)  28.3 us
    all_to_all x3, starting transfers between devices, body(): lax.all_to_all(term.reshape(n_seq, f_part, width), 'seq', 0, 0)  20.6 us
    ppermute x4, starting transfers between devices, from_behind(): return lax.ppermute(x, axis, pairs)  17.1 us
    all_to_all x1, starting transfers between devices, body(): parts = lax.all_to_all(by_lane.reshape(n_dp, c_part, LANES), 'dp', 0, 0)  15.5 us
    all_to_all x1, waiting for transfers between devices, body(): parts = lax.all_to_all(by_lane.reshape(n_dp, c_part, LANES), 'dp', 0, 0)  8.36 us
    dot_general x3, matrix products, product_tn(): lax.dot_general(left, right, (((0,), (0,)), ((), ())), preferred_element_...  6.41 us
  transfers between devices with their start and end apart: 10, of which 5 were waited for; matrix products, arithmetic and copies ran while one was open for 19% of the time, Pallas kernels for 0%

profile of v1, /device:TPU:4, one launch (start us, length us, event | category | flops | bytes accessed | tf_op | source)
XLA Modules:
  0.0 235.6 jit_solution(10067381851368016522)
XLA Ops:
  0.6 5.1 %collective-permute-start.1 = (bf16[2,512,768]{2,1,0:T(8,128)(2,1)}, bf16[2,512,768]{2,1,0:T(8,128)(2,1)}, u32[]{:S(2)}, u32[]{:S(2)}) collective-permute-start(bf16[2,512,768]{2,1,0:T(8,128)(2,1)} %param.4), channel_id=1, source_target_pairs={{2,0},{3,1},{4,2},{5,3},{6,4},{7,5},{8,6},{9,7},{10,8},{11,9},{12,... | collective-permute-start | bytes 4718600 | tf_op jit(solution)/shard_map/ppermute | solution.py:17
  8.0 15.6 %all-to-all-start = ((bf16[32,24,128]{2,1,0:T(8,128)(2,1)}), bf16[32,24,128]{2,1,0:T(8,128)(2,1)S(1)}, u32[]{:S(2)}, u32[]{:S(2)}) async-start(bf16[32,24,128]{2,1,0:T(8,128)(2,1)} %broadcast_in_dim.4), calls=%async_computation | async-start | bytes 393216 | tf_op jit(solution)/shard_map/all_to_all | solution.py:54
  23.6 3.8 %collective-permute-start = (bf16[2,512,768]{2,1,0:T(8,128)(2,1)}, bf16[2,512,768]{2,1,0:T(8,128)(2,1)}, u32[]{:S(2)}, u32[]{:S(2)}) collective-permute-start(bf16[2,512,768]{2,1,0:T(8,128)(2,1)} %param.4), channel_id=1, source_target_pairs={{0,2},{1,3},{2,4},{3,5},{4,6},{5,7},{6,8},{7,9},{8,10},{9,11},{10,... | collective-permute-start | bytes 4718600 | tf_op jit(solution)/shard_map/ppermute | solution.py:17
  27.4 1.8 fusion.6
  29.2 14.6 %all-to-all-done = bf16[32,24,128]{2,1,0:T(8,128)(2,1)S(1)} async-done(((bf16[32,24,128]{2,1,0:T(8,128)(2,1)}), bf16[32,24,128]{2,1,0:T(8,128)(2,1)S(1)}, u32[]{:S(2)}, u32[]{:S(2)}) %all-to-all-start) | async-done | bytes 196640 | tf_op jit(solution)/shard_map/all_to_all | solution.py:54
  45.6 38.9 %all-to-all-start.1 = ((bf16[16,96,768]{2,1,0:T(8,128)(2,1)}), bf16[16,96,768]{2,1,0:T(8,128)(2,1)S(1)}, u32[]{:S(2)}, u32[]{:S(2)}) async-start(bf16[16,96,768]{2,1,0:T(8,128)(2,1)} %broadcast_in_dim.5), calls=%async_computation.1 | async-start | bytes 4718592 | tf_op jit(solution)/shard_map/all_to_all | solution.py:54
  84.5 4.8 %fusion.16 = (bf16[2,512,768]{2,1,0:T(8,128)(2,1)}, f32[2,512,768]{2,1,0:T(8,128)}) fusion(f32[2,512]{1,0:T(2,128)S(1)} %get-tuple-element.15, bf16[2,512,768]{2,1,0:T(8,128)(2,1)} %param.4), kind=kLoop, calls=%fused_computation.27 | loop fusion | flops 8650752 | bytes 6295552 | tf_op jit(solution)/shard_map/convert_element_type | solution.py:85
  92.9 3.9 %fusion.3 = bf16[2,512,768]{2,1,0:T(8,128)(2,1)} fusion(bf16[2,512,768]{2,1,0:T(8,128)(2,1)} %collective-permute-done.1, f32[2,512]{1,0:T(2,128)S(1)} %add_rsqrt_fusion), kind=kLoop, calls=%fused_computation.14 | loop fusion | flops 8650752 | bytes 3149824 | tf_op jit(solution)/shard_map/convert_element_type | solution.py:87
  96.8 3.8 %fusion.5 = bf16[2,512,768]{2,1,0:T(8,128)(2,1)} fusion(bf16[2,512,768]{2,1,0:T(8,128)(2,1)} %collective-permute-done, f32[2,512]{1,0:T(2,128)S(1)} %add_rsqrt_fusion.1), kind=kLoop, calls=%fused_computation.16 | loop fusion | flops 8650752 | bytes 3149824 | tf_op jit(solution)/shard_map/convert_element_type | solution.py:86
  100.6 13.7 %all-to-all-done.1 = bf16[16,96,768]{2,1,0:T(8,128)(2,1)S(1)} async-done(((bf16[16,96,768]{2,1,0:T(8,128)(2,1)}), bf16[16,96,768]{2,1,0:T(8,128)(2,1)S(1)}, u32[]{:S(2)}, u32[]{:S(2)}) %all-to-all-start.1) | async-done | bytes 2359328 | tf_op jit(solution)/shard_map/all_to_all | solution.py:54
  114.5 1.8 copy-done.11
  122.5 7.8 %all-to-all-start.4 = ((bf16[16,24,768]{2,1,0:T(8,128)(2,1)}), bf16[16,24,768]{2,1,0:T(8,128)(2,1)S(1)}, u32[]{:S(2)}, u32[]{:S(2)}) async-start(bf16[16,24,768]{2,1,0:T(8,128)(2,1)} %bitcast.22), calls=%async_computation.4 | async-start | bytes 1179648 | tf_op jit(solution)/shard_map/all_to_all | solution.py:102
  130.3 3.1 %fusion.41 = bf16[384,768]{1,0:T(8,128)(2,1)} fusion(bf16[1024,384]{0,1:T(8,128)(2,1)S(1)} %fusion.39, bf16[1024,768]{1,0:T(8,128)(2,1)} %bitcast.112), kind=kOutput, calls=%fused_computation.62 | convolution fusion | flops 604569600 | bytes 2949120 | tf_op jit(solution)/shard_map/dot_general | solution.py:44
  133.4 7.5 %all-to-all-done.4 = bf16[16,24,768]{2,1,0:T(8,128)(2,1)S(1)} async-done(((bf16[16,24,768]{2,1,0:T(8,128)(2,1)}), bf16[16,24,768]{2,1,0:T(8,128)(2,1)S(1)}, u32[]{:S(2)}, u32[]{:S(2)}) %all-to-all-start.4) | async-done | bytes 589856 | tf_op jit(solution)/shard_map/all_to_all | solution.py:102
  141.0 5.9 %all-to-all-start.3 = ((bf16[16,24,768]{2,1,0:T(8,128)(2,1)}), bf16[16,24,768]{2,1,0:T(8,128)(2,1)S(1)}, u32[]{:S(2)}, u32[]{:S(2)}) async-start(bf16[16,24,768]{2,1,0:T(8,128)(2,1)} %bitcast.118), calls=%async_computation.3 | async-start | bytes 1179648 | tf_op jit(solution)/shard_map/all_to_all | solution.py:102
  148.3 4.9 %collective-permute-start.3 = (bf16[2,512,384]{1,0,2:T(2,128)(2,1)}, bf16[2,512,384]{1,0,2:T(2,128)(2,1)}, u32[]{:S(2)}, u32[]{:S(2)}) collective-permute-start(bf16[2,512,384]{1,0,2:T(2,128)(2,1)} %reshape.107), channel_id=1, source_target_pairs={{0,2},{1,3},{2,4},{3,5},{4,6},{5,7},{6,8},{7,9},{8,10},{9,11},{10,... | collective-permute-start | bytes 2359304 | tf_op jit(solution)/shard_map/ppermute | solution.py:17
  153.2 3.4 %collective-permute-start.2 = (bf16[2,512,384]{1,0,2:T(2,128)(2,1)}, bf16[2,512,384]{1,0,2:T(2,128)(2,1)}, u32[]{:S(2)}, u32[]{:S(2)}) collective-permute-start(bf16[2,512,384]{1,0,2:T(2,128)(2,1)} %reshape.107), channel_id=1, source_target_pairs={{2,0},{3,1},{4,2},{5,3},{6,4},{7,5},{8,6},{9,7},{10,8},{11,9},{12,... | collective-permute-start | bytes 2359304 | tf_op jit(solution)/shard_map/ppermute | solution.py:17
  158.3 7.0 %all-to-all-start.2 = ((bf16[16,24,768]{2,1,0:T(8,128)(2,1)}), bf16[16,24,768]{2,1,0:T(8,128)(2,1)}, u32[]{:S(2)}, u32[]{:S(2)}) async-start(bf16[16,24,768]{2,1,0:T(8,128)(2,1)} %bitcast.119), calls=%async_computation.2 | async-start | bytes 1179648 | tf_op jit(solution)/shard_map/all_to_all | solution.py:102
  165.2 2.3 fusion.55
  169.9 28.0 %all-to-all-done.2 = bf16[16,24,768]{2,1,0:T(8,128)(2,1)} async-done(((bf16[16,24,768]{2,1,0:T(8,128)(2,1)}), bf16[16,24,768]{2,1,0:T(8,128)(2,1)}, u32[]{:S(2)}, u32[]{:S(2)}) %all-to-all-start.2) | async-done | bytes 589856 | tf_op jit(solution)/shard_map/all_to_all | solution.py:102
  199.9 15.5 %all-to-all-start.5 = ((bf16[32,24,128]{2,1,0:T(8,128)(2,1)}), bf16[32,24,128]{2,1,0:T(8,128)(2,1)S(1)}, u32[]{:S(2)}, u32[]{:S(2)}) async-start(bf16[32,24,128]{2,1,0:T(8,128)(2,1)} %bitcast.24), calls=%async_computation.5 | async-start | bytes 393216 | tf_op jit(solution)/shard_map/all_to_all | solution.py:109
  219.3 2.9 %fusion.30 = (f32[1024]{0:T(1024)S(1)}, f32[1024,768]{1,0:T(8,128)S(1)}) fusion(f32[2,512,768]{2,1,0:T(8,128)S(1)} %copy-done, f32[1024,768]{1,0:T(8,128)S(1)} %fusion.54, f32[1024,768]{1,0:T(8,128)S(1)} %fusion.55, bf16[1024,384]{0,1:T(8,128)(2,1)S(1)} %bitcast.114, bf16[384,768]{1,0:T(8,128)(2,1)S(1)} %bitcast.117), kind=kOutput, calls=%fused_computation.44 | convolution fusion | flops 621280256 | bytes 13963264 | tf_op jit(solution)/shard_map/dot_general | solution.py:36
  222.2 4.3 %fusion.29 = bf16[1024,768]{1,0:T(8,128)(2,1)} fusion(f32[2,512,768]{2,1,0:T(8,128)S(1)} %copy-done, f32[1024]{0:T(1024)S(1)} %broadcast_multiply_fusion, f32[1024]{0:T(1024)S(1)} %bitcast.121, bf16[2,512,768]{2,1,0:T(8,128)(2,1)S(1)} %copy-done.3, f32[1024,768]{1,0:T(8,128)S(1)} %get-tuple-element.17, f32[1024,768]{1,0:T(8,128)S(1)} %fusion.54, ...), kind=kLoop, calls=%fused_computation.43 | loop fusion | flops 20447232 | bytes 15736832 | tf_op jit(solution)/shard_map/convert_element_type | solution.py:126
  226.5 8.4 %all-to-all-done.5 = bf16[32,24,128]{2,1,0:T(8,128)(2,1)S(1)} async-done(((bf16[32,24,128]{2,1,0:T(8,128)(2,1)}), bf16[32,24,128]{2,1,0:T(8,128)(2,1)S(1)}, u32[]{:S(2)}, u32[]{:S(2)}) %all-to-all-start.5) | async-done | bytes 196640 | tf_op jit(solution)/shard_map/all_to_all | solution.py:109
  (68 shorter events, 26.0 us)
Async XLA Ops:
  0.6 88.7 %collective-permute-start.1 = (bf16[2,512,768]{2,1,0:T(8,128)(2,1)}, bf16[2,512,768]{2,1,0:T(8,128)(2,1)}, u32[]{:S(2)}, u32[]{:S(2)}) collective-permute-start(bf16[2,512,768]{2,1,0:T(8,128)(2,1)} %param.4), channel_id=1, source_target_pairs={{2,0},{3,1},{4,2},{5,3},{6,4},{7,5},{8,6},{9,7},{10,8},{11,9},{12,... | collective-permute-start | bytes 4718600 | tf_op jit(solution)/shard_map/ppermute | solution.py:17
  8.0 35.7 %all-to-all-start = ((bf16[32,24,128]{2,1,0:T(8,128)(2,1)}), bf16[32,24,128]{2,1,0:T(8,128)(2,1)S(1)}, u32[]{:S(2)}, u32[]{:S(2)}) async-start(bf16[32,24,128]{2,1,0:T(8,128)(2,1)} %broadcast_in_dim.4), calls=%async_computation | async-start | bytes 393216 | tf_op jit(solution)/shard_map/all_to_all | solution.py:54
  23.6 67.5 %collective-permute-start = (bf16[2,512,768]{2,1,0:T(8,128)(2,1)}, bf16[2,512,768]{2,1,0:T(8,128)(2,1)}, u32[]{:S(2)}, u32[]{:S(2)}) collective-permute-start(bf16[2,512,768]{2,1,0:T(8,128)(2,1)} %param.4), channel_id=1, source_target_pairs={{0,2},{1,3},{2,4},{3,5},{4,6},{5,7},{6,8},{7,9},{8,10},{9,11},{10,... | collective-permute-start | bytes 4718600 | tf_op jit(solution)/shard_map/ppermute | solution.py:17
  45.6 68.7 %all-to-all-start.1 = ((bf16[16,96,768]{2,1,0:T(8,128)(2,1)}), bf16[16,96,768]{2,1,0:T(8,128)(2,1)S(1)}, u32[]{:S(2)}, u32[]{:S(2)}) async-start(bf16[16,96,768]{2,1,0:T(8,128)(2,1)} %broadcast_in_dim.5), calls=%async_computation.1 | async-start | bytes 4718592 | tf_op jit(solution)/shard_map/all_to_all | solution.py:54
  114.3 2.0 copy-start.11
  114.3 2.9 %copy-start.9 = (bf16[2,512,768]{2,1,0:T(8,128)(2,1)S(1)}, bf16[2,512,768]{2,1,0:T(8,128)(2,1)}, u32[]{:S(2)}) copy-start(bf16[2,512,768]{2,1,0:T(8,128)(2,1)} %fusion.5) | copy-start | bytes 4718596
  114.5 3.5 %copy-start.4 = (bf16[1,16,24,768]{3,2,0,1:T(8,128)(2,1)}, bf16[1,16,24,768]{3,2,0,1:T(8,128)(2,1)S(1)}, u32[]{:S(2)}) copy-start(bf16[1,16,24,768]{3,2,0,1:T(8,128)(2,1)S(1)} %get-tuple-element.2) | copy-start | bytes 1769476
  114.5 3.5 %copy-start.13 = (bf16[1,16,24,768]{3,2,0,1:T(8,128)(2,1)}, bf16[1,16,24,768]{3,2,0,1:T(8,128)(2,1)S(1)}, u32[]{:S(2)}) copy-start(bf16[1,16,24,768]{3,2,0,1:T(8,128)(2,1)S(1)} %get-tuple-element.3) | copy-start | bytes 1769476
  114.5 4.3 %copy-start.6 = (bf16[1,16,24,768]{3,2,0,1:T(8,128)(2,1)}, bf16[1,16,24,768]{3,2,0,1:T(8,128)(2,1)S(1)}, u32[]{:S(2)}) copy-start(bf16[1,16,24,768]{3,2,0,1:T(8,128)(2,1)S(1)} %get-tuple-element.4) | copy-start | bytes 1769476
  117.2 1.7 copy-start.12
  120.9 35.7 %copy-start.1 = (bf16[1024,384]{0,1:T(8,128)(2,1)}, bf16[1024,384]{0,1:T(8,128)(2,1)S(1)}, u32[]{:S(2)}) copy-start(bf16[1024,384]{0,1:T(8,128)(2,1)S(1)} %fusion.39) | copy-start | bytes 2359300
  122.5 18.4 %all-to-all-start.4 = ((bf16[16,24,768]{2,1,0:T(8,128)(2,1)}), bf16[16,24,768]{2,1,0:T(8,128)(2,1)S(1)}, u32[]{:S(2)}, u32[]{:S(2)}) async-start(bf16[16,24,768]{2,1,0:T(8,128)(2,1)} %bitcast.22), calls=%async_computation.4 | async-start | bytes 1179648 | tf_op jit(solution)/shard_map/all_to_all | solution.py:102
  130.3 26.3 %copy-start.10 = (bf16[2,512,768]{2,1,0:T(8,128)(2,1)S(1)}, bf16[2,512,768]{2,1,0:T(8,128)(2,1)}, u32[]{:S(2)}) copy-start(bf16[2,512,768]{2,1,0:T(8,128)(2,1)} %fusion.5) | copy-start | bytes 4718596
  141.0 17.3 %copy-start.7 = (bf16[16,24,768]{2,1,0:T(8,128)(2,1)}, bf16[16,24,768]{2,1,0:T(8,128)(2,1)S(1)}, u32[]{:S(2)}) copy-start(bf16[16,24,768]{2,1,0:T(8,128)(2,1)S(1)} %all-to-all-done.4) | copy-start | bytes 1769476
  141.0 17.3 %all-to-all-start.3 = ((bf16[16,24,768]{2,1,0:T(8,128)(2,1)}), bf16[16,24,768]{2,1,0:T(8,128)(2,1)S(1)}, u32[]{:S(2)}, u32[]{:S(2)}) async-start(bf16[16,24,768]{2,1,0:T(8,128)(2,1)} %bitcast.118), calls=%async_computation.3 | async-start | bytes 1179648 | tf_op jit(solution)/shard_map/all_to_all | solution.py:102
  148.3 67.1 %collective-permute-start.3 = (bf16[2,512,384]{1,0,2:T(2,128)(2,1)}, bf16[2,512,384]{1,0,2:T(2,128)(2,1)}, u32[]{:S(2)}, u32[]{:S(2)}) collective-permute-start(bf16[2,512,384]{1,0,2:T(2,128)(2,1)} %reshape.107), channel_id=1, source_target_pairs={{0,2},{1,3},{2,4},{3,5},{4,6},{5,7},{6,8},{7,9},{8,10},{9,11},{10,... | collective-permute-start | bytes 2359304 | tf_op jit(solution)/shard_map/ppermute | solution.py:17
  153.2 63.5 %collective-permute-start.2 = (bf16[2,512,384]{1,0,2:T(2,128)(2,1)}, bf16[2,512,384]{1,0,2:T(2,128)(2,1)}, u32[]{:S(2)}, u32[]{:S(2)}) collective-permute-start(bf16[2,512,384]{1,0,2:T(2,128)(2,1)} %reshape.107), channel_id=1, source_target_pairs={{2,0},{3,1},{4,2},{5,3},{6,4},{7,5},{8,6},{9,7},{10,8},{11,9},{12,... | collective-permute-start | bytes 2359304 | tf_op jit(solution)/shard_map/ppermute | solution.py:17
  158.3 7.0 %copy-start.8 = (bf16[16,24,768]{2,1,0:T(8,128)(2,1)}, bf16[16,24,768]{2,1,0:T(8,128)(2,1)S(1)}, u32[]{:S(2)}) copy-start(bf16[16,24,768]{2,1,0:T(8,128)(2,1)S(1)} %all-to-all-done.3) | copy-start | bytes 1769476
  158.3 39.6 %all-to-all-start.2 = ((bf16[16,24,768]{2,1,0:T(8,128)(2,1)}), bf16[16,24,768]{2,1,0:T(8,128)(2,1)}, u32[]{:S(2)}, u32[]{:S(2)}) async-start(bf16[16,24,768]{2,1,0:T(8,128)(2,1)} %bitcast.119), calls=%async_computation.2 | async-start | bytes 1179648 | tf_op jit(solution)/shard_map/all_to_all | solution.py:102
  199.9 34.9 %all-to-all-start.5 = ((bf16[32,24,128]{2,1,0:T(8,128)(2,1)}), bf16[32,24,128]{2,1,0:T(8,128)(2,1)S(1)}, u32[]{:S(2)}, u32[]{:S(2)}) async-start(bf16[32,24,128]{2,1,0:T(8,128)(2,1)} %bitcast.24), calls=%async_computation.5 | async-start | bytes 393216 | tf_op jit(solution)/shard_map/all_to_all | solution.py:109
  215.4 2.8 %copy-start.5 = (bf16[1,16,24,768]{3,2,0,1:T(8,128)(2,1)S(1)}, bf16[1,16,24,768]{3,2,0,1:T(8,128)(2,1)}, u32[]{:S(2)}) copy-start(bf16[1,16,24,768]{3,2,0,1:T(8,128)(2,1)} %copy-done.4) | copy-start | bytes 1769476
  216.7 2.5 %copy-start = (f32[2,512,768]{2,1,0:T(8,128)S(1)}, f32[2,512,768]{2,1,0:T(8,128)}, u32[]{:S(2)}) copy-start(f32[2,512,768]{2,1,0:T(8,128)} %get-tuple-element.7) | copy-start | bytes 9437188
  216.7 2.5 %copy-start.14 = (bf16[1,16,24,768]{3,2,0,1:T(8,128)(2,1)S(1)}, bf16[1,16,24,768]{3,2,0,1:T(8,128)(2,1)}, u32[]{:S(2)}) copy-start(bf16[1,16,24,768]{3,2,0,1:T(8,128)(2,1)} %copy-done.13) | copy-start | bytes 1769476
  219.2 2.9 %copy-start.3 = (bf16[2,512,768]{2,1,0:T(8,128)(2,1)S(1)}, bf16[2,512,768]{2,1,0:T(8,128)(2,1)}, u32[]{:S(2)}) copy-start(bf16[2,512,768]{2,1,0:T(8,128)(2,1)} %param.7) | copy-start | bytes 4718596
  (1 other events, 1.7 us)

commit v2 on v1

v2 whole, which is shorter than its diff:
```python
import functools

import jax
import jax.numpy as jnp
from jax import lax
from jax.experimental import pallas as pl
from jax.experimental.pallas import tpu as pltpu
from jax.sharding import Mesh
from jax.sharding import PartitionSpec as P

LANES = 128
X_PARTS, Y_PARTS, CORES = 4, 2, 2
GROUPS = 2
VMEM_BYTES = 40 * 1024 * 1024

EPSILON = 1e-06
GELU_SCALE = 0.7978845608028654
GELU_CUBIC = 0.044715


def gelu_tanh(values):
    return (
        0.5
        * values
        * (1.0 + jnp.tanh(GELU_SCALE * (values + GELU_CUBIC * values * values * values)))
    )


def gelu_slope(values):
    tangent = jnp.tanh(GELU_SCALE * (values + GELU_CUBIC * values * values * values))
    return 0.5 * (1.0 + tangent) + 0.5 * values * (1.0 - tangent * tangent) * GELU_SCALE * (
        1.0 + 3.0 * GELU_CUBIC * values * values
    )


def dot(left, right, left_dim, right_dim):
    return lax.dot_general(
        left, right, (((left_dim,), (right_dim,)), ((), ())), preferred_element_type=jnp.float32
    )


def normalize(values):
    floats = values.astype(jnp.float32)
    row_scale = lax.rsqrt(jnp.mean(floats * floats, axis=-1, keepdims=True) + EPSILON)
    return floats * row_scale, row_scale


def params():
    return pltpu.CompilerParams(vmem_limit_bytes=VMEM_BYTES)


def struct(shape, dtype):
    return jax.ShapeDtypeStruct(shape, dtype)


def cost(flops, nbytes):
    return pl.CostEstimate(flops=flops, bytes_accessed=nbytes, transcendentals=0)


def pack_kernel(conv_ref, point_ref, out_ref):
    taps, c_part, f_part = conv_ref.shape
    pieces = [conv_ref[tap].astype(jnp.float32) for tap in range(taps)]
    pieces.append(point_ref[...].astype(jnp.float32).T)
    pieces.append(jnp.zeros((c_part, LANES - (taps + 1) * f_part), jnp.float32))
    packed = jnp.concatenate(pieces, axis=1).astype(out_ref.dtype)
    out_ref[...] = jnp.broadcast_to(packed[None], out_ref.shape)


def pack(conv_weight, point_weight, peers):
    c_part = conv_weight.shape[1]
    return pl.pallas_call(
        pack_kernel,
        out_shape=struct((peers, c_part, LANES), conv_weight.dtype),
        compiler_params=params(),
        cost_estimate=cost(0, 2 * peers * c_part * LANES),
        name="pack",
    )(conv_weight, point_weight)


def by_tap_kernel(f_part, in_ref, *refs):
    out_refs = refs[-GROUPS:]
    taps = out_refs[0].shape[1]
    turned = [in_ref[y].astype(jnp.float32).T for y in range(Y_PARTS)]
    for tap in range(GROUPS * taps):
        rows = jnp.concatenate([t[tap * f_part : (tap + 1) * f_part] for t in turned], axis=0)
        out_ref = out_refs[tap // taps]
        for copy in range(X_PARTS):
            out_ref[copy, tap % taps] = rows.astype(out_ref.dtype)


def by_tap(gathered, f_part, taps, after):
    width = gathered.shape[1]
    return pl.pallas_call(
        functools.partial(by_tap_kernel, f_part),
        in_specs=[pl.BlockSpec(memory_space=pltpu.VMEM)]
        + [pl.BlockSpec(memory_space=pl.ANY)] * len(after),
        out_shape=[struct((X_PARTS, taps // GROUPS, Y_PARTS * f_part, width), gathered.dtype)]
        * GROUPS,
        compiler_params=params(),
        cost_estimate=cost(0, 4 * gathered.size * 2),
        name="by_tap",
    )(gathered, *after)


def by_channel_kernel(f_part, in_ref, out_ref):
    peers, taps, _, width = in_ref.shape
    total = [sum(in_ref[p, tap].astype(jnp.float32) for p in range(peers)) for tap in range(taps)]
    blank = jnp.zeros((LANES - taps * f_part, width), jnp.float32)
    for y in range(Y_PARTS):
        rows = [t[y * f_part : (y + 1) * f_part] for t in total] + [blank]
        out_ref[y] = jnp.concatenate(rows, axis=0).T.astype(out_ref.dtype)


def by_channel(parts, f_part):
    width = parts.shape[3]
    return pl.pallas_call(
        functools.partial(by_channel_kernel, f_part),
        out_shape=struct((Y_PARTS, width, LANES), parts.dtype),
        compiler_params=params(),
        cost_estimate=cost(0, 4 * parts.size),
        name="by_channel",
    )(parts)


def act_kernel(in_ref, out_ref):
    normed, _ = normalize(in_ref[...])
    out_ref[...] = gelu_tanh(normed).astype(out_ref.dtype)


def activate(inputs, block):
    samples, bins, width = inputs.shape
    rows = pl.BlockSpec((None, block, width), lambda s, i: (s, i, 0))
    return pl.pallas_call(
        act_kernel,
        grid=(samples, bins // block),
        in_specs=[rows],
        out_specs=rows,
        out_shape=struct(inputs.shape, inputs.dtype),
        compiler_params=params(),
        cost_estimate=cost(20 * inputs.size, 4 * inputs.size),
        name="activate",
    )(inputs)


def join_weights(own_refs, other_refs, joined, taps):
    each = own_refs[0].shape[1]
    for tap in range(taps):
        for side, refs in enumerate((own_refs, other_refs)):
            rows = refs[tap // each][:, tap % each].reshape(-1, joined.shape[2])
            joined[tap, pl.ds(side * rows.shape[0], rows.shape[0]), :] = rows


def forward_kernel(scale, samples, steps, *refs):
    acts_refs, cot_ref, refs = refs[:3], refs[3], refs[4:]
    own_w, other_w, refs = refs[:GROUPS], refs[GROUPS : 2 * GROUPS], refs[2 * GROUPS :]
    pre_ref, own_out, other_out, weights, acc = refs
    step = pl.program_id(0)

    @pl.when(step == 0)
    def _():
        join_weights(own_w, other_w, weights, 4)
        acc[...] = jnp.zeros_like(acc)

    for sample in range(samples):
        low, mid, high = [r[sample] for r in acts_refs]
        shifted_low = dot(low, weights[0], 1, 1).astype(jnp.bfloat16).astype(jnp.float32)
        shifted_high = dot(high, weights[2], 1, 1).astype(jnp.bfloat16).astype(jnp.float32)
        preact = shifted_low + dot(mid, weights[1], 1, 1) + shifted_high
        grad_inner = dot(cot_ref[sample], weights[3], 1, 1)
        grad_pre = (grad_inner * gelu_slope(preact)).astype(jnp.bfloat16)
        pre_ref[sample] = grad_pre
        for tap, acts in enumerate((low, mid, high)):
            acc[tap] += dot(grad_pre, acts, 0, 0)

    @pl.when(step == steps - 1)
    def _():
        half = acc.shape[1] // CORES
        for tap in range(3):
            own = acc[tap, pl.ds(0, half), :] * scale
            other = acc[tap, pl.ds(half, half), :] * scale
            own_out[:, tap] = own.reshape(own_out.shape[0], -1, own.shape[1])
            other_out[:, tap] = other.astype(jnp.bfloat16).reshape(
                other_out.shape[0], -1, own.shape[1]
            )


def forward(acts, cotangent, own_w, other_w, scale, block):
    samples, bins, width = cotangent.shape
    parts, _, f_rows, _ = own_w[0].shape
    hidden = CORES * parts * f_rows
    steps = bins // block
    rows = pl.BlockSpec((samples, block, width), lambda i: (0, i, 0))
    whole = pl.BlockSpec(own_w[0].shape, lambda i: (0, 0, 0, 0))
    half = (parts, 3, f_rows, width)
    half_spec = pl.BlockSpec(half, lambda i: (0, 0, 0, 0))
    return pl.pallas_call(
        functools.partial(forward_kernel, scale, samples, steps),
        grid=(steps,),
        in_specs=[rows] * 4 + [whole] * (2 * GROUPS),
        out_specs=[
            pl.BlockSpec((samples, block, hidden), lambda i: (0, i, 0)),
            half_spec,
            half_spec,
        ],
        out_shape=[
            struct((samples, bins, hidden), jnp.bfloat16),
            struct(half, jnp.float32),
            struct(half, jnp.bfloat16),
        ],
        scratch_shapes=[
            pltpu.VMEM((4, hidden, width), jnp.bfloat16),
            pltpu.VMEM((3, hidden, width), jnp.float32),
        ],
        compiler_params=params(),
        cost_estimate=cost(14 * samples * bins * width * hidden, 16 * samples * bins * width),
        name="forward",
    )(*acts, cotangent, *own_w, *other_w)


def backward_kernel(in_ref, cot_ref, up_ref, pre_ref, low_ref, *refs):
    own_w, other_w, (out_ref, weights) = refs[:GROUPS], refs[GROUPS:-2], refs[-2:]

    @pl.when(pl.program_id(0) == 0)
    def _():
        join_weights(own_w, other_w, weights, 3)

    for sample in range(in_ref.shape[0]):
        grad_act = (
            dot(up_ref[sample], weights[0], 1, 0)
            + dot(pre_ref[sample], weights[1], 1, 0)
            + dot(low_ref[sample], weights[2], 1, 0)
        )
        normed, row_scale = normalize(in_ref[sample])
        grad_norm = grad_act * gelu_slope(normed)
        center = jnp.mean(grad_norm * normed, axis=-1, keepdims=True)
        grad = cot_ref[sample].astype(jnp.float32) + row_scale * (grad_norm - normed * center)
        out_ref[sample] = grad.astype(out_ref.dtype)


def backward(inputs, cotangent, grad_upper, grad_pre, grad_lower, own_w, other_w, block):
    samples, bins, width = inputs.shape
    hidden = grad_pre.shape[2]
    wide = pl.BlockSpec((samples, block, width), lambda i: (0, i, 0))
    narrow = pl.BlockSpec((samples, block, hidden), lambda i: (0, i, 0))
    whole = pl.BlockSpec(own_w[0].shape, lambda i: (0, 0, 0, 0))
    return pl.pallas_call(
        backward_kernel,
        grid=(bins // block,),
        in_specs=[wide, wide, narrow, narrow, narrow] + [whole] * (2 * GROUPS),
        out_specs=wide,
        out_shape=struct(inputs.shape, inputs.dtype),
        scratch_shapes=[pltpu.VMEM((3, hidden, width), jnp.bfloat16)],
        compiler_params=params(),
        cost_estimate=cost(6 * samples * bins * width * hidden, 16 * samples * bins * width),
        name="backward",
    )(inputs, cotangent, grad_upper, grad_pre, grad_lower, *own_w, *other_w)


def shifted(array, by):
    count = X_PARTS * Y_PARTS
    pairs = [(i, i + by) for i in range(count) if 0 <= i + by < count]
    return lax.ppermute(array, ("x", "yh"), pairs)


def other_core(array):
    return lax.ppermute(array, "core", [(0, 1), (1, 0)])


def body(inputs, conv_weight, point_weight, cotangent):
    samples, bins, width = inputs.shape
    taps, c_part, f_part = conv_weight.shape
    n_dp = lax.axis_size("dp")
    devices = n_dp * X_PARTS * Y_PARTS * CORES
    grad_scale = float(samples * bins * devices) ** (-0.5)

    packed = pack(conv_weight, point_weight, Y_PARTS * n_dp)
    gathered = lax.all_to_all(packed, ("yh", "dp"), 0, 0).reshape(Y_PARTS, width, LANES)

    acted = activate(inputs, 256)
    acts = (shifted(acted, 1), acted, shifted(acted, -1))

    copies = by_tap(gathered, f_part, taps + 1, [acted])
    own_w = [lax.all_to_all(part, "x", 0, 0) for part in copies]
    other_w = [other_core(part) for part in own_w]

    grad_pre, own, other = forward(acts, cotangent, own_w, other_w, grad_scale, 128)

    grad_upper = shifted(grad_pre, -1)
    grad_lower = shifted(grad_pre, 1)

    pair = (own + other_core(other).astype(jnp.float32)).astype(jnp.bfloat16)
    parts = lax.all_to_all(pair, "x", 0, 0)
    sums = by_channel(parts, f_part).reshape(Y_PARTS * n_dp, c_part, LANES)
    pieces = lax.all_to_all(sums, ("yh", "dp"), 0, 0)
    total = jnp.sum(pieces.astype(jnp.float32), axis=0)
    conv_grad = jnp.stack([total[:, t * f_part : (t + 1) * f_part] for t in range(taps)], axis=0)

    input_grad = backward(
        inputs, cotangent, grad_upper, grad_pre, grad_lower, own_w, other_w, 128
    )
    return (input_grad, conv_grad)


def solution(mesh):
    n_dp = mesh.shape["dp"]
    fine = Mesh(
        mesh.devices.reshape(n_dp, X_PARTS, Y_PARTS, CORES), ("dp", "x", "yh", "core")
    )
    seq = ("x", "yh", "core")
    return jax.shard_map(
        body,
        mesh=fine,
        in_specs=(P("dp", seq, None), P(None, "dp", seq), P(seq, "dp"), P("dp", seq, None)),
        out_specs=(P("dp", seq, None), P(None, "dp", seq)),
        check_vma=False,
    )
```

time: 237 us -> 211 us (0.89)
  the two profiles are of different devices: /device:TPU:4 before, /device:TPU:3 now
where the time goes in v2:
time: 211 us; the launch traced here: 210 us
  waiting for transfers between devices  67.7 us (32%)
  starting transfers between devices  63.1 us (30%)
  blocking collectives  42.8 us (20%)
  Pallas kernels  24.2 us (11%)
  local copies, waits for them, and re-layouts  9.72 us (5%)
    ppermute x4, waiting for transfers between devices, shifted(): return lax.ppermute(array, ('x', 'yh'), pairs)  49.1 us
    all_to_all x1, blocking collectives, body(): own_w = [lax.all_to_all(part, 'x', 0, 0) for part in copies]  27.2 us
    all_to_all x1, starting transfers between devices, body(): lax.all_to_all(packed, ('yh', 'dp'), 0, 0).reshape(Y_PARTS, width, LANES)  18.5 us
    all_to_all x1, blocking collectives, body(): parts = lax.all_to_all(pair, 'x', 0, 0)  15.6 us
    ppermute x4, starting transfers between devices, shifted(): return lax.ppermute(array, ('x', 'yh'), pairs)  14.5 us
    all_to_all x1, waiting for transfers between devices, body(): lax.all_to_all(packed, ('yh', 'dp'), 0, 0).reshape(Y_PARTS, width, LANES)  14.3 us
    all_to_all x1, starting transfers between devices, body(): pieces = lax.all_to_all(sums, ('yh', 'dp'), 0, 0)  14.1 us
    pallas_call x1, Pallas kernels, forward(): pl.pallas_call(functools.partial(forward_kernel, scale, samples, steps),...  13.3 us
  transfers between devices with their start and end apart: 10, of which 6 were waited for; matrix products, arithmetic and copies ran while one was open for 0% of the time, Pallas kernels for 4%

profile of v2, /device:TPU:3, one launch (start us, length us, event | category | flops | bytes accessed | tf_op | source)
XLA Modules:
  0.0 210.2 jit_solution(12696791918063573253)
XLA Ops:
  3.0 18.5 %all-to-all-start = ((bf16[64,24,128]{2,1,0:T(8,128)(2,1)}), bf16[64,24,128]{2,1,0:T(8,128)(2,1)S(1)}, u32[]{:S(2)}, u32[]{:S(2)}) async-start(bf16[64,24,128]{2,1,0:T(8,128)(2,1)} %pack.1), calls=%async_computation | async-start | bytes 786432 | tf_op jit(solution)/shard_map/all_to_all | solution.py:277
  21.4 1.4 copy-done
  22.8 1.5 activate.1.refs_0_.refs_1_
  24.4 4.5 %collective-permute-start.1 = (bf16[2,512,768]{2,1,0:T(8,128)(2,1)S(1)}, bf16[2,512,768]{2,1,0:T(8,128)(2,1)}, u32[]{:S(2)}, u32[]{:S(2)}) collective-permute-start(bf16[2,512,768]{2,1,0:T(8,128)(2,1)S(1)} %activate.1.refs_0_.refs_1_), channel_id=1, source_target_pairs={{2,0},{4,2},{6,4},{8,6},{10,8},{12,10},{14,12},{3,1},{5,3},{7,5},{... | collective-permute-start | bytes 4718600 | tf_op jit(solution)/shard_map/ppermute | solution.py:262
  28.9 2.3 %collective-permute-start = (bf16[2,512,768]{2,1,0:T(8,128)(2,1)S(1)}, bf16[2,512,768]{2,1,0:T(8,128)(2,1)}, u32[]{:S(2)}, u32[]{:S(2)}) collective-permute-start(bf16[2,512,768]{2,1,0:T(8,128)(2,1)S(1)} %activate.1.refs_0_.refs_1_), channel_id=1, source_target_pairs={{0,2},{2,4},{4,6},{6,8},{8,10},{10,12},{12,14},{1,3},{3,5},{5,7},{... | collective-permute-start | bytes 4718600 | tf_op jit(solution)/shard_map/ppermute | solution.py:262
  31.2 14.3 %all-to-all-done = bf16[64,24,128]{2,1,0:T(8,128)(2,1)S(1)} async-done(((bf16[64,24,128]{2,1,0:T(8,128)(2,1)}), bf16[64,24,128]{2,1,0:T(8,128)(2,1)S(1)}, u32[]{:S(2)}, u32[]{:S(2)}) %all-to-all-start) | async-done | bytes 393248 | tf_op jit(solution)/shard_map/all_to_all | solution.py:277
  46.5 27.2 %all_to_all.25.refs_5_.refs_1_ = bf16[4,2,48,768]{3,2,1,0:T(8,128)(2,1)S(1)} all-to-all(bf16[4,2,48,768]{3,2,1,0:T(8,128)(2,1)S(1)} %get-tuple-element.8), channel_id=1, replica_groups=mesh['dp'=32,'x'=4,'yh'=2,'core'=2] {'x'}, dimensions={0} | all-to-all | bytes 1179648 | tf_op jit(solution)/shard_map/all_to_all | solution.py:283
  73.7 3.5 %all-to-all-start.1 = ((bf16[4,2,48,768]{3,2,1,0:T(8,128)(2,1)}), bf16[4,2,48,768]{3,2,1,0:T(8,128)(2,1)S(1)}, u32[]{:S(2)}, u32[]{:S(2)}) async-start(bf16[4,2,48,768]{3,2,1,0:T(8,128)(2,1)} %get-tuple-element.7), calls=%async_computation.1 | async-start | bytes 1179648 | tf_op jit(solution)/shard_map/all_to_all | solution.py:283
  77.2 4.1 %collective-permute-start.3 = (bf16[4,2,48,768]{3,2,1,0:T(8,128)(2,1)S(1)}, bf16[4,2,48,768]{3,2,1,0:T(8,128)(2,1)S(1)}, u32[]{:S(2)}, u32[]{:S(2)}) collective-permute-start(bf16[4,2,48,768]{3,2,1,0:T(8,128)(2,1)S(1)} %all_to_all.25.refs_5_.refs_1_), channel_id=1, source_target_pairs={{0,1},{1,0},{2,3},{3,2},{4,5},{5,4},{6,7},{7,6},{8,9},{9,8},{10,11... | collective-permute-start | bytes 1769480 | tf_op jit(solution)/shard_map/ppermute | solution.py:266
  81.3 2.2 %all-to-all-done.1.refs_4_.refs_0_ = bf16[4,2,48,768]{3,2,1,0:T(8,128)(2,1)S(1)} async-done(((bf16[4,2,48,768]{3,2,1,0:T(8,128)(2,1)}), bf16[4,2,48,768]{3,2,1,0:T(8,128)(2,1)S(1)}, u32[]{:S(2)}, u32[]{:S(2)}) %all-to-all-start.1) | async-done | bytes 589856 | tf_op jit(solution)/shard_map/all_to_all | solution.py:283
  83.5 5.1 %collective-permute-start.2 = (bf16[4,2,48,768]{3,2,1,0:T(8,128)(2,1)S(1)}, bf16[4,2,48,768]{3,2,1,0:T(8,128)(2,1)S(1)}, u32[]{:S(2)}, u32[]{:S(2)}) collective-permute-start(bf16[4,2,48,768]{3,2,1,0:T(8,128)(2,1)S(1)} %all-to-all-done.1.refs_4_.refs_0_), channel_id=1, source_target_pairs={{0,1},{1,0},{2,3},{3,2},{4,5},{5,4},{6,7},{7,6},{8,9},{9,8},{10,11... | collective-permute-start | bytes 1769480 | tf_op jit(solution)/shard_map/ppermute | solution.py:266
  88.6 12.1 %collective-permute-done.1.refs_2_ = bf16[2,512,768]{2,1,0:T(8,128)(2,1)} collective-permute-done((bf16[2,512,768]{2,1,0:T(8,128)(2,1)S(1)}, bf16[2,512,768]{2,1,0:T(8,128)(2,1)}, u32[]{:S(2)}, u32[]{:S(2)}) %collective-permute-start.1) | collective-permute-done | bytes 1572896 | tf_op jit(solution)/shard_map/ppermute | solution.py:262
  101.5 1.4 copy-done.2
  104.0 13.3 %forward.1 = (bf16[2,512,384]{2,1,0:T(8,128)(2,1)S(1)}, f32[4,3,48,768]{3,2,1,0:T(8,128)S(1)}, bf16[4,3,48,768]{3,2,1,0:T(8,128)(2,1)S(1)}) custom-call(bf16[2,512,768]{2,1,0:T(8,128)(2,1)} %collective-permute-done.refs_0_, bf16[2,512,768]{2,1,0:T(8,128)(2,1)S(1)} %activate.1.refs_0_.refs_1_, bf16[2,512,768]{2,1,0:T(8,128)(2,1)} %collective-permute-done.1.refs_2_, ...), custom_call_target="tpu_custom_call" | custom-call | flops 4227858432 | bytes 12582912 | tf_op jit(solution)/shard_map/forward/pallas_call | solution.py:196
  117.3 3.4 %collective-permute-start.6 = (bf16[4,3,48,768]{3,2,1,0:T(8,128)(2,1)S(1)}, bf16[4,3,48,768]{3,2,1,0:T(8,128)(2,1)S(1)}, u32[]{:S(2)}, u32[]{:S(2)}) collective-permute-start(bf16[4,3,48,768]{3,2,1,0:T(8,128)(2,1)S(1)} %get-tuple-element.11), channel_id=1, source_target_pairs={{0,1},{1,0},{2,3},{3,2},{4,5},{5,4},{6,7},{7,6},{8,9},{9,8},{10,11... | collective-permute-start | bytes 2654216 | tf_op jit(solution)/shard_map/ppermute | solution.py:266
  120.8 2.0 collective-permute-done.6
  123.0 15.6 %all_to_all.26.in_ref = bf16[4,3,48,768]{3,2,1,0:T(8,128)(2,1)S(1)} all-to-all(bf16[4,3,48,768]{3,2,1,0:T(8,128)(2,1)S(1)} %add_convert_fusion), channel_id=1, replica_groups=mesh['dp'=32,'x'=4,'yh'=2,'core'=2] {'x'}, dimensions={0} | all-to-all | bytes 1769472 | tf_op jit(solution)/shard_map/all_to_all | solution.py:292
  139.5 14.1 %all-to-all-start.4 = ((bf16[64,24,128]{2,1,0:T(8,128)(2,1)}), bf16[64,24,128]{2,1,0:T(8,128)(2,1)}, u32[]{:S(2)}, u32[]{:S(2)}) async-start(bf16[64,24,128]{2,1,0:T(8,128)(2,1)} %bitcast.1), calls=%async_computation.4 | async-start | bytes 786432 | tf_op jit(solution)/shard_map/all_to_all | solution.py:294
  153.6 4.5 %collective-permute-start.5 = (bf16[2,512,384]{2,1,0:T(8,128)(2,1)S(1)}, bf16[2,512,384]{2,1,0:T(8,128)(2,1)S(1)}, u32[]{:S(2)}, u32[]{:S(2)}) collective-permute-start(bf16[2,512,384]{2,1,0:T(8,128)(2,1)S(1)} %get-tuple-element.9.pre_ref), channel_id=1, source_target_pairs={{0,2},{2,4},{4,6},{6,8},{8,10},{10,12},{12,14},{1,3},{3,5},{5,7},{... | collective-permute-start | bytes 2359304 | tf_op jit(solution)/shard_map/ppermute | solution.py:262
  158.1 3.2 %collective-permute-start.4 = (bf16[2,512,384]{2,1,0:T(8,128)(2,1)S(1)}, bf16[2,512,384]{2,1,0:T(8,128)(2,1)S(1)}, u32[]{:S(2)}, u32[]{:S(2)}) collective-permute-start(bf16[2,512,384]{2,1,0:T(8,128)(2,1)S(1)} %get-tuple-element.9.pre_ref), channel_id=1, source_target_pairs={{2,0},{4,2},{6,4},{8,6},{10,8},{12,10},{14,12},{3,1},{5,3},{7,5},{... | collective-permute-start | bytes 2359304 | tf_op jit(solution)/shard_map/ppermute | solution.py:262
  161.3 32.5 %collective-permute-done.5.low_ref = bf16[2,512,384]{2,1,0:T(8,128)(2,1)S(1)} collective-permute-done((bf16[2,512,384]{2,1,0:T(8,128)(2,1)S(1)}, bf16[2,512,384]{2,1,0:T(8,128)(2,1)S(1)}, u32[]{:S(2)}, u32[]{:S(2)}) %collective-permute-start.5) | collective-permute-done | bytes 786464 | tf_op jit(solution)/shard_map/ppermute | solution.py:262
  193.8 4.5 %collective-permute-done.4.up_ref = bf16[2,512,384]{2,1,0:T(8,128)(2,1)S(1)} collective-permute-done((bf16[2,512,384]{2,1,0:T(8,128)(2,1)S(1)}, bf16[2,512,384]{2,1,0:T(8,128)(2,1)S(1)}, u32[]{:S(2)}, u32[]{:S(2)}) %collective-permute-start.4) | collective-permute-done | bytes 786464 | tf_op jit(solution)/shard_map/ppermute | solution.py:262
  198.3 1.4 copy-done.3
  201.9 6.5 %backward.1 = bf16[2,512,768]{2,1,0:T(8,128)(2,1)} custom-call(bf16[2,512,768]{2,1,0:T(8,128)(2,1)S(1)} %copy-done.1, bf16[2,512,768]{2,1,0:T(8,128)(2,1)S(1)} %copy-done.3, bf16[2,512,384]{2,1,0:T(8,128)(2,1)S(1)} %collective-permute-done.4.up_ref, bf16[2,512,384]{2,1,0:T(8,128)(2,1)S(1)} %get-tuple-element.9.pre_ref, ...), custom_call_target="tpu_custom_call" | custom-call | flops 1811939328 | bytes 12582912 | tf_op jit(solution)/shard_map/backward/pallas_call | solution.py:246
  (30 shorter events, 10.2 us)
Async XLA Ops:
  0.6 0.7 copy-start.9
  1.4 0.7 copy-start.10
  3.0 42.5 %all-to-all-start = ((bf16[64,24,128]{2,1,0:T(8,128)(2,1)}), bf16[64,24,128]{2,1,0:T(8,128)(2,1)S(1)}, u32[]{:S(2)}, u32[]{:S(2)}) async-start(bf16[64,24,128]{2,1,0:T(8,128)(2,1)} %pack.1), calls=%async_computation | async-start | bytes 786432 | tf_op jit(solution)/shard_map/all_to_all | solution.py:277
  21.4 1.4 copy-start
  24.4 76.3 %collective-permute-start.1 = (bf16[2,512,768]{2,1,0:T(8,128)(2,1)S(1)}, bf16[2,512,768]{2,1,0:T(8,128)(2,1)}, u32[]{:S(2)}, u32[]{:S(2)}) collective-permute-start(bf16[2,512,768]{2,1,0:T(8,128)(2,1)S(1)} %activate.1.refs_0_.refs_1_), channel_id=1, source_target_pairs={{2,0},{4,2},{6,4},{8,6},{10,8},{12,10},{14,12},{3,1},{5,3},{7,5},{... | collective-permute-start | bytes 4718600 | tf_op jit(solution)/shard_map/ppermute | solution.py:262
  28.9 71.8 %collective-permute-start = (bf16[2,512,768]{2,1,0:T(8,128)(2,1)S(1)}, bf16[2,512,768]{2,1,0:T(8,128)(2,1)}, u32[]{:S(2)}, u32[]{:S(2)}) collective-permute-start(bf16[2,512,768]{2,1,0:T(8,128)(2,1)S(1)} %activate.1.refs_0_.refs_1_), channel_id=1, source_target_pairs={{0,2},{2,4},{4,6},{6,8},{8,10},{10,12},{12,14},{1,3},{3,5},{5,7},{... | collective-permute-start | bytes 4718600 | tf_op jit(solution)/shard_map/ppermute | solution.py:262
  73.7 9.7 %all-to-all-start.1 = ((bf16[4,2,48,768]{3,2,1,0:T(8,128)(2,1)}), bf16[4,2,48,768]{3,2,1,0:T(8,128)(2,1)S(1)}, u32[]{:S(2)}, u32[]{:S(2)}) async-start(bf16[4,2,48,768]{3,2,1,0:T(8,128)(2,1)} %get-tuple-element.7), calls=%async_computation.1 | async-start | bytes 1179648 | tf_op jit(solution)/shard_map/all_to_all | solution.py:283
  77.2 23.5 %collective-permute-start.3 = (bf16[4,2,48,768]{3,2,1,0:T(8,128)(2,1)S(1)}, bf16[4,2,48,768]{3,2,1,0:T(8,128)(2,1)S(1)}, u32[]{:S(2)}, u32[]{:S(2)}) collective-permute-start(bf16[4,2,48,768]{3,2,1,0:T(8,128)(2,1)S(1)} %all_to_all.25.refs_5_.refs_1_), channel_id=1, source_target_pairs={{0,1},{1,0},{2,3},{3,2},{4,5},{5,4},{6,7},{7,6},{8,9},{9,8},{10,11... | collective-permute-start | bytes 1769480 | tf_op jit(solution)/shard_map/ppermute | solution.py:266
  83.5 18.0 %collective-permute-start.2 = (bf16[4,2,48,768]{3,2,1,0:T(8,128)(2,1)S(1)}, bf16[4,2,48,768]{3,2,1,0:T(8,128)(2,1)S(1)}, u32[]{:S(2)}, u32[]{:S(2)}) collective-permute-start(bf16[4,2,48,768]{3,2,1,0:T(8,128)(2,1)S(1)} %all-to-all-done.1.refs_4_.refs_0_), channel_id=1, source_target_pairs={{0,1},{1,0},{2,3},{3,2},{4,5},{5,4},{6,7},{7,6},{8,9},{9,8},{10,11... | collective-permute-start | bytes 1769480 | tf_op jit(solution)/shard_map/ppermute | solution.py:266
  100.7 0.8 copy-start.4
  101.5 1.4 copy-start.2
  102.9 1.1 copy-start.5
  104.0 13.3 %copy-start.7 = (bf16[4,2,48,768]{3,2,1,0:T(8,128)(2,1)}, bf16[4,2,48,768]{3,2,1,0:T(8,128)(2,1)S(1)}, u32[]{:S(2)}) copy-start(bf16[4,2,48,768]{3,2,1,0:T(8,128)(2,1)S(1)} %collective-permute-done.2.refs_6_.refs_2_) | copy-start | bytes 1769476
  117.3 5.5 %collective-permute-start.6 = (bf16[4,3,48,768]{3,2,1,0:T(8,128)(2,1)S(1)}, bf16[4,3,48,768]{3,2,1,0:T(8,128)(2,1)S(1)}, u32[]{:S(2)}, u32[]{:S(2)}) collective-permute-start(bf16[4,3,48,768]{3,2,1,0:T(8,128)(2,1)S(1)} %get-tuple-element.11), channel_id=1, source_target_pairs={{0,1},{1,0},{2,3},{3,2},{4,5},{5,4},{6,7},{7,6},{8,9},{9,8},{10,11... | collective-permute-start | bytes 2654216 | tf_op jit(solution)/shard_map/ppermute | solution.py:266
  123.0 75.3 %copy-start.1 = (bf16[2,512,768]{2,1,0:T(8,128)(2,1)S(1)}, bf16[2,512,768]{2,1,0:T(8,128)(2,1)}, u32[]{:S(2)}) copy-start(bf16[2,512,768]{2,1,0:T(8,128)(2,1)} %in_ref.3) | copy-start | bytes 4718596
  139.5 68.8 %all-to-all-start.4 = ((bf16[64,24,128]{2,1,0:T(8,128)(2,1)}), bf16[64,24,128]{2,1,0:T(8,128)(2,1)}, u32[]{:S(2)}, u32[]{:S(2)}) async-start(bf16[64,24,128]{2,1,0:T(8,128)(2,1)} %bitcast.1), calls=%async_computation.4 | async-start | bytes 786432 | tf_op jit(solution)/shard_map/all_to_all | solution.py:294
  153.6 40.2 %collective-permute-start.5 = (bf16[2,512,384]{2,1,0:T(8,128)(2,1)S(1)}, bf16[2,512,384]{2,1,0:T(8,128)(2,1)S(1)}, u32[]{:S(2)}, u32[]{:S(2)}) collective-permute-start(bf16[2,512,384]{2,1,0:T(8,128)(2,1)S(1)} %get-tuple-element.9.pre_ref), channel_id=1, source_target_pairs={{0,2},{2,4},{4,6},{6,8},{8,10},{10,12},{12,14},{1,3},{3,5},{5,7},{... | collective-permute-start | bytes 2359304 | tf_op jit(solution)/shard_map/ppermute | solution.py:262
  158.1 40.3 %collective-permute-start.4 = (bf16[2,512,384]{2,1,0:T(8,128)(2,1)S(1)}, bf16[2,512,384]{2,1,0:T(8,128)(2,1)S(1)}, u32[]{:S(2)}, u32[]{:S(2)}) collective-permute-start(bf16[2,512,384]{2,1,0:T(8,128)(2,1)S(1)} %get-tuple-element.9.pre_ref), channel_id=1, source_target_pairs={{2,0},{4,2},{6,4},{8,6},{10,8},{12,10},{14,12},{3,1},{5,3},{7,5},{... | collective-permute-start | bytes 2359304 | tf_op jit(solution)/shard_map/ppermute | solution.py:262
  198.3 1.4 copy-start.3
  199.7 1.1 copy-start.6
  200.8 1.1 copy-start.8

commit v3 on v2

v3 whole, which is shorter than its diff:
```python
import functools

import jax
import jax.numpy as jnp
from jax import lax
from jax.experimental import pallas as pl
from jax.experimental.pallas import tpu as pltpu
from jax.sharding import Mesh
from jax.sharding import PartitionSpec as P

LANES = 128
X_PARTS, Y_PARTS, CORES = 4, 2, 2
GROUPS = 2
MIB = 1024 * 1024

EPSILON = 1e-06
GELU_SCALE = 0.7978845608028654
GELU_CUBIC = 0.044715


def gelu_tanh(values):
    return (
        0.5
        * values
        * (1.0 + jnp.tanh(GELU_SCALE * (values + GELU_CUBIC * values * values * values)))
    )


def gelu_slope(values):
    tangent = jnp.tanh(GELU_SCALE * (values + GELU_CUBIC * values * values * values))
    return 0.5 * (1.0 + tangent) + 0.5 * values * (1.0 - tangent * tangent) * GELU_SCALE * (
        1.0 + 3.0 * GELU_CUBIC * values * values
    )


def dot(left, right, left_dim, right_dim):
    return lax.dot_general(
        left, right, (((left_dim,), (right_dim,)), ((), ())), preferred_element_type=jnp.float32
    )


def normalize(values):
    floats = values.astype(jnp.float32)
    row_scale = lax.rsqrt(jnp.mean(floats * floats, axis=-1, keepdims=True) + EPSILON)
    return floats * row_scale, row_scale


def params(mib):
    return pltpu.CompilerParams(vmem_limit_bytes=mib * MIB)


def struct(shape, dtype):
    return jax.ShapeDtypeStruct(shape, dtype)


def cost(flops, nbytes):
    return pl.CostEstimate(flops=flops, bytes_accessed=nbytes, transcendentals=0)


ANYWHERE = pl.BlockSpec(memory_space=pl.ANY)
IN_VMEM = pl.BlockSpec(memory_space=pltpu.VMEM)


def pack_kernel(conv_ref, point_ref, *refs):
    out_ref = refs[-1]
    taps, c_part, f_part = conv_ref.shape
    pieces = [conv_ref[tap].astype(jnp.float32) for tap in range(taps)]
    pieces.append(point_ref[...].astype(jnp.float32).T)
    pieces.append(jnp.zeros((c_part, LANES - (taps + 1) * f_part), jnp.float32))
    packed = jnp.concatenate(pieces, axis=1).astype(out_ref.dtype)
    out_ref[...] = jnp.broadcast_to(packed[None], out_ref.shape)


def pack(conv_weight, point_weight, peers, after):
    c_part = conv_weight.shape[1]
    return pl.pallas_call(
        pack_kernel,
        in_specs=[IN_VMEM, IN_VMEM, ANYWHERE],
        out_shape=struct((peers, c_part, LANES), conv_weight.dtype),
        compiler_params=params(8),
        cost_estimate=cost(0, 2 * peers * c_part * LANES),
        name="pack",
    )(conv_weight, point_weight, after)


def by_tap_kernel(f_part, in_ref, *out_refs):
    taps = out_refs[0].shape[1]
    width = out_refs[0].shape[3]
    turned = []
    for y in range(Y_PARTS):
        rows = jnp.stack([in_ref[y, low].astype(jnp.float32) for low in range(Y_PARTS)], axis=1)
        turned.append(rows.reshape(width, LANES).T)
    for tap in range(GROUPS * taps):
        rows = jnp.concatenate([t[tap * f_part : (tap + 1) * f_part] for t in turned], axis=0)
        out_ref = out_refs[tap // taps]
        for copy in range(X_PARTS):
            out_ref[copy, tap % taps] = rows.astype(out_ref.dtype)


def by_tap(gathered, f_part, taps):
    width = gathered.shape[1] * gathered.shape[2] * gathered.shape[3]
    out = struct((X_PARTS, taps // GROUPS, Y_PARTS * f_part, width), gathered.dtype)
    return pl.pallas_call(
        functools.partial(by_tap_kernel, f_part),
        out_shape=[out] * GROUPS,
        compiler_params=params(16),
        cost_estimate=cost(0, 4 * gathered.size * 2),
        name="by_tap",
    )(gathered)


def by_channel_kernel(f_part, in_ref, out_ref):
    peers, taps, _, width = in_ref.shape
    depth, c_part = out_ref.shape[2:4]
    total = [sum(in_ref[p, tap].astype(jnp.float32) for p in range(peers)) for tap in range(taps)]
    blank = jnp.zeros((LANES - taps * f_part, width), jnp.float32)
    for y in range(Y_PARTS):
        rows = [t[y * f_part : (y + 1) * f_part] for t in total] + [blank]
        turned = jnp.concatenate(rows, axis=0).T.reshape(depth, Y_PARTS, c_part, LANES)
        for low in range(Y_PARTS):
            out_ref[y, low] = turned[:, low].astype(out_ref.dtype)


def by_channel(parts, f_part, depth):
    c_part = parts.shape[3] // (depth * Y_PARTS)
    return pl.pallas_call(
        functools.partial(by_channel_kernel, f_part),
        out_shape=struct((Y_PARTS, Y_PARTS, depth, c_part, LANES), parts.dtype),
        compiler_params=params(16),
        cost_estimate=cost(0, 4 * parts.size),
        name="by_channel",
    )(parts)


def add_kernel(in_ref, *refs):
    out_ref = refs[-1]
    total = sum(in_ref[p].astype(jnp.float32) for p in range(in_ref.shape[0]))
    out_ref[...] = total.astype(out_ref.dtype)


def add_parts(parts, after):
    return pl.pallas_call(
        add_kernel,
        in_specs=[IN_VMEM] + [ANYWHERE] * len(after),
        out_shape=struct(parts.shape[1:], parts.dtype),
        compiler_params=params(8),
        cost_estimate=cost(0, 4 * parts.size),
        name="add_parts",
    )(parts, *after)


def finish_kernel(in_ref, out_ref):
    taps, _, f_part = out_ref.shape
    total = sum(in_ref[p].astype(jnp.float32) for p in range(in_ref.shape[0]))
    for tap in range(taps):
        out_ref[tap] = total[:, tap * f_part : (tap + 1) * f_part]


def finish(pieces, taps, f_part):
    return pl.pallas_call(
        finish_kernel,
        out_shape=struct((taps, pieces.shape[1], f_part), jnp.float32),
        compiler_params=params(8),
        cost_estimate=cost(0, 4 * pieces.size),
        name="finish",
    )(pieces)


def act_kernel(in_ref, out_ref):
    normed, _ = normalize(in_ref[...])
    out_ref[...] = gelu_tanh(normed).astype(out_ref.dtype)


def activate(inputs, block):
    samples, bins, width = inputs.shape
    rows = pl.BlockSpec((None, block, width), lambda s, i: (s, i, 0))
    return pl.pallas_call(
        act_kernel,
        grid=(samples, bins // block),
        in_specs=[rows],
        out_specs=rows,
        out_shape=struct(inputs.shape, inputs.dtype),
        compiler_params=params(8),
        cost_estimate=cost(20 * inputs.size, 4 * inputs.size),
        name="activate",
    )(inputs)


def join_weights(own_refs, other_refs, joined, taps):
    each = own_refs[0].shape[1]
    for tap in range(taps):
        for side, refs in enumerate((own_refs, other_refs)):
            rows = refs[tap // each][:, tap % each].reshape(-1, joined.shape[2])
            joined[tap, pl.ds(side * rows.shape[0], rows.shape[0]), :] = rows


def forward_kernel(scale, *refs):
    acts_refs, cot_ref, refs = refs[:3], refs[3], refs[4:]
    own_w, other_w, refs = refs[:GROUPS], refs[GROUPS : 2 * GROUPS], refs[2 * GROUPS :]
    pre_ref, own_out, other_out, weights, turned = refs
    samples, bins, width = cot_ref.shape
    half = weights.shape[1] // CORES
    join_weights(own_w, other_w, weights, 4)
    for sample in range(samples):
        low, mid, high = [r[sample] for r in acts_refs]
        shifted_low = dot(low, weights[0], 1, 1).astype(jnp.bfloat16).astype(jnp.float32)
        shifted_high = dot(high, weights[2], 1, 1).astype(jnp.bfloat16).astype(jnp.float32)
        preact = shifted_low + dot(mid, weights[1], 1, 1) + shifted_high
        grad_inner = dot(cot_ref[sample], weights[3], 1, 1)
        grad_pre = grad_inner * gelu_slope(preact)
        pre_ref[sample] = grad_pre.astype(jnp.bfloat16)
        turned[:, pl.ds(sample * bins, bins)] = grad_pre.T.astype(jnp.bfloat16)
    for tap, acts_ref in enumerate(acts_refs):
        acts = acts_ref[...].reshape(samples * bins, width)
        term = dot(turned[...], acts, 1, 0) * scale
        own_out[:, tap] = term[:half].reshape(own_out.shape[0], -1, width)
        other = term[half:].astype(jnp.bfloat16)
        other_out[:, tap] = other.reshape(other_out.shape[0], -1, width)


def forward(acts, cotangent, own_w, other_w, scale):
    samples, bins, width = cotangent.shape
    parts, _, f_rows, _ = own_w[0].shape
    hidden = CORES * parts * f_rows
    half = (parts, 3, f_rows, width)
    return pl.pallas_call(
        functools.partial(forward_kernel, scale),
        out_shape=[
            struct((samples, bins, hidden), jnp.bfloat16),
            struct(half, jnp.float32),
            struct(half, jnp.bfloat16),
        ],
        scratch_shapes=[
            pltpu.VMEM((4, hidden, width), jnp.bfloat16),
            pltpu.VMEM((hidden, samples * bins), jnp.bfloat16),
        ],
        compiler_params=params(24),
        cost_estimate=cost(14 * samples * bins * width * hidden, 16 * samples * bins * width),
        name="forward",
    )(*acts, cotangent, *own_w, *other_w)


def backward_kernel(in_ref, cot_ref, up_ref, pre_ref, low_ref, *refs):
    own_w, other_w, (out_ref, weights) = refs[:GROUPS], refs[GROUPS:-2], refs[-2:]

    @pl.when(pl.program_id(0) == 0)
    def _():
        join_weights(own_w, other_w, weights, 3)

    for sample in range(in_ref.shape[0]):
        grad_act = (
            dot(up_ref[sample], weights[0], 1, 0)
            + dot(pre_ref[sample], weights[1], 1, 0)
            + dot(low_ref[sample], weights[2], 1, 0)
        )
        normed, row_scale = normalize(in_ref[sample])
        grad_norm = grad_act * gelu_slope(normed)
        center = jnp.mean(grad_norm * normed, axis=-1, keepdims=True)
        grad = cot_ref[sample].astype(jnp.float32) + row_scale * (grad_norm - normed * center)
        out_ref[sample] = grad.astype(out_ref.dtype)


def backward(inputs, cotangent, grad_upper, grad_pre, grad_lower, own_w, other_w, block):
    samples, bins, width = inputs.shape
    hidden = grad_pre.shape[2]
    wide = pl.BlockSpec((samples, block, width), lambda i: (0, i, 0))
    narrow = pl.BlockSpec((samples, block, hidden), lambda i: (0, i, 0))
    whole = pl.BlockSpec(
        own_w[0].shape, lambda i: (0, 0, 0, 0), pipeline_mode=pl.Buffered(1)
    )
    return pl.pallas_call(
        backward_kernel,
        grid=(bins // block,),
        in_specs=[wide, wide, narrow, narrow, narrow] + [whole] * (2 * GROUPS),
        out_specs=wide,
        out_shape=struct(inputs.shape, inputs.dtype),
        scratch_shapes=[pltpu.VMEM((3, hidden, width), jnp.bfloat16)],
        compiler_params=params(24),
        cost_estimate=cost(6 * samples * bins * width * hidden, 16 * samples * bins * width),
        name="backward",
    )(inputs, cotangent, grad_upper, grad_pre, grad_lower, *own_w, *other_w)


def shifted(array, by):
    count = X_PARTS * Y_PARTS
    pairs = [(i, i + by) for i in range(count) if 0 <= i + by < count]
    return lax.ppermute(array, ("x", "yh"), pairs)


def other_core(array):
    return lax.ppermute(array, "core", [(0, 1), (1, 0)])


def body(inputs, conv_weight, point_weight, cotangent):
    samples, bins, width = inputs.shape
    taps, c_part, f_part = conv_weight.shape
    depth = lax.axis_size("z")
    devices = depth * Y_PARTS * X_PARTS * Y_PARTS * CORES
    grad_scale = float(samples * bins * devices) ** (-0.5)

    acted = activate(inputs, 256)
    acts = (shifted(acted, 1), acted, shifted(acted, -1))

    along_z = lax.all_to_all(pack(conv_weight, point_weight, depth, acted), "z", 0, 0)
    copies = jnp.broadcast_to(along_z[None], (Y_PARTS * Y_PARTS,) + along_z.shape)
    gathered = lax.all_to_all(copies, ("yh", "yl"), 0, 0)
    gathered = gathered.reshape(Y_PARTS, Y_PARTS, depth, c_part, LANES)
    own_w = [lax.all_to_all(part, "x", 0, 0) for part in by_tap(gathered, f_part, taps + 1)]
    other_w = [other_core(part) for part in own_w]

    grad_pre, own, other = forward(acts, cotangent, own_w, other_w, grad_scale)

    grad_upper = shifted(grad_pre, -1)
    grad_lower = shifted(grad_pre, 1)

    pair = (own + other_core(other).astype(jnp.float32)).astype(jnp.bfloat16)
    sums = by_channel(lax.all_to_all(pair, "x", 0, 0), f_part, depth)
    sums = sums.reshape(Y_PARTS * Y_PARTS, depth, c_part, LANES)
    sums = add_parts(lax.all_to_all(sums, ("yh", "yl"), 0, 0), (grad_upper, grad_lower))
    conv_grad = finish(lax.all_to_all(sums, "z", 0, 0), taps, f_part)

    input_grad = backward(
        inputs, cotangent, grad_upper, grad_pre, grad_lower, own_w, other_w, 256
    )
    return (input_grad, conv_grad)


def solution(mesh):
    depth = mesh.shape["dp"] // Y_PARTS
    fine = Mesh(
        mesh.devices.reshape(depth, Y_PARTS, X_PARTS, Y_PARTS, CORES),
        ("z", "yl", "x", "yh", "core"),
    )
    dp, seq = ("z", "yl"), ("x", "yh", "core")
    return jax.shard_map(
        body,
        mesh=fine,
        in_specs=(P(dp, seq, None), P(None, dp, seq), P(seq, dp), P(dp, seq, None)),
        out_specs=(P(dp, seq, None), P(None, dp, seq)),
        check_vma=False,
    )
```

time: 211 us -> 226 us (1.071)
  the two profiles are of different devices: /device:TPU:3 before, /device:TPU:2 now
where the time goes in v3:
time: 226 us; the launch traced here: 225 us
  waiting for transfers between devices  75.8 us (34%)
  starting transfers between devices  74.6 us (33%)
  blocking collectives  42.8 us (19%)
  Pallas kernels  19.2 us (8%)
  local copies, waits for them, and re-layouts  10.1 us (4%)
    ppermute x4, starting transfers between devices, shifted(): return lax.ppermute(array, ('x', 'yh'), pairs)  41.1 us
    ppermute x4, waiting for transfers between devices, shifted(): return lax.ppermute(array, ('x', 'yh'), pairs)  33.2 us
    all_to_all x1, waiting for transfers between devices, body(): gathered = lax.all_to_all(copies, ('yh', 'yl'), 0, 0)  32.1 us
    all_to_all x1, blocking collectives, body(): lax.all_to_all(pack(conv_weight, point_weight, depth, acted), 'z', 0, 0)  28.6 us
    all_to_all x1, blocking collectives, body(): lax.all_to_all(part, 'x', 0, 0)  14.2 us
    all_to_all x1, starting transfers between devices, body(): lax.all_to_all(sums, ('yh', 'yl'), 0, 0)  10 us
    unnamed x30, local copies, waits for them, and re-layouts  9.33 us
    pallas_call x1, Pallas kernels, forward(): pl.pallas_call(functools.partial(forward_kernel, scale), out_shape=[struc...  7.63 us
  transfers between devices with their start and end apart: 12, of which 8 were waited for; matrix products, arithmetic and copies ran while one was open for 0% of the time, Pallas kernels for 4%

profile of v3, /device:TPU:2, one launch (start us, length us, event | category | flops | bytes accessed | tf_op | source)
XLA Modules:
  0.0 224.5 jit_solution(10060426826495842099)
XLA Ops:
  3.8 28.6 %all_to_all.35 = bf16[16,24,128]{2,1,0:T(8,128)(2,1)S(1)} all-to-all(bf16[16,24,128]{2,1,0:T(8,128)(2,1)S(1)} %pack.1), channel_id=1, replica_groups=mesh['z'=16,'yl'=2,'x'=4,'yh'=2,'core'=2] {'z'}, dimensions={0} | all-to-all | bytes 196608 | tf_op jit(solution)/shard_map/all_to_all | solution.py:304
  33.1 4.5 %all-to-all-start.1 = ((bf16[4,16,24,128]{3,2,1,0:T(8,128)(2,1)}), bf16[4,16,24,128]{3,2,1,0:T(8,128)(2,1)S(1)}, u32[]{:S(2)}, u32[]{:S(2)}) async-start(bf16[4,16,24,128]{3,2,1,0:T(8,128)(2,1)} %broadcast_in_dim.2), calls=%async_computation.1 | async-start | bytes 786432 | tf_op jit(solution)/shard_map/all_to_all | solution.py:306
  37.6 5.4 %collective-permute-start.1 = (bf16[2,512,768]{2,1,0:T(8,128)(2,1)S(1)}, bf16[2,512,768]{2,1,0:T(8,128)(2,1)}, u32[]{:S(2)}, u32[]{:S(2)}) collective-permute-start(bf16[2,512,768]{2,1,0:T(8,128)(2,1)S(1)} %activate.1.refs_0_.refs_1_), channel_id=1, source_target_pairs={{2,0},{4,2},{6,4},{8,6},{10,8},{12,10},{14,12},{3,1},{5,3},{7,5},{... | collective-permute-start | bytes 4718600 | tf_op jit(solution)/shard_map/ppermute | solution.py:287
  43.0 1.9 collective-permute-start
  44.9 32.1 %all-to-all-done.1 = bf16[4,16,24,128]{3,2,1,0:T(8,128)(2,1)S(1)} async-done(((bf16[4,16,24,128]{3,2,1,0:T(8,128)(2,1)}), bf16[4,16,24,128]{3,2,1,0:T(8,128)(2,1)S(1)}, u32[]{:S(2)}, u32[]{:S(2)}) %all-to-all-start.1) | async-done | bytes 393248 | tf_op jit(solution)/shard_map/all_to_all | solution.py:306
  78.0 14.2 %all_to_all.36.refs_5_.refs_1_ = bf16[4,2,48,768]{3,2,1,0:T(8,128)(2,1)S(1)} all-to-all(bf16[4,2,48,768]{3,2,1,0:T(8,128)(2,1)S(1)} %get-tuple-element.8), channel_id=1, replica_groups=mesh['z'=16,'yl'=2,'x'=4,'yh'=2,'core'=2] {'x'}, dimensions={0} | all-to-all | bytes 1179648 | tf_op jit(solution)/shard_map/all_to_all | solution.py:308
  92.3 4.9 %all-to-all-start.2 = ((bf16[4,2,48,768]{3,2,1,0:T(8,128)(2,1)}), bf16[4,2,48,768]{3,2,1,0:T(8,128)(2,1)S(1)}, u32[]{:S(2)}, u32[]{:S(2)}) async-start(bf16[4,2,48,768]{3,2,1,0:T(8,128)(2,1)} %get-tuple-element.7), calls=%async_computation.2 | async-start | bytes 1179648 | tf_op jit(solution)/shard_map/all_to_all | solution.py:308
  97.2 1.9 collective-permute-start.3
  99.1 5.1 %all-to-all-done.2.refs_4_.refs_0_ = bf16[4,2,48,768]{3,2,1,0:T(8,128)(2,1)S(1)} async-done(((bf16[4,2,48,768]{3,2,1,0:T(8,128)(2,1)}), bf16[4,2,48,768]{3,2,1,0:T(8,128)(2,1)S(1)}, u32[]{:S(2)}, u32[]{:S(2)}) %all-to-all-start.2) | async-done | bytes 589856 | tf_op jit(solution)/shard_map/all_to_all | solution.py:308
  104.2 1.9 collective-permute-start.2
  106.1 5.1 %collective-permute-done.1.refs_2_ = bf16[2,512,768]{2,1,0:T(8,128)(2,1)} collective-permute-done((bf16[2,512,768]{2,1,0:T(8,128)(2,1)S(1)}, bf16[2,512,768]{2,1,0:T(8,128)(2,1)}, u32[]{:S(2)}, u32[]{:S(2)}) %collective-permute-start.1) | collective-permute-done | bytes 1572896 | tf_op jit(solution)/shard_map/ppermute | solution.py:287
  111.2 1.6 copy-done.6
  112.8 7.6 %forward.1 = (bf16[2,512,384]{2,1,0:T(8,128)(2,1)}, f32[4,3,48,768]{3,2,1,0:T(8,128)S(1)}, bf16[4,3,48,768]{3,2,1,0:T(8,128)(2,1)S(1)}) custom-call(bf16[2,512,768]{2,1,0:T(8,128)(2,1)} %collective-permute-done.refs_0_, bf16[2,512,768]{2,1,0:T(8,128)(2,1)S(1)} %activate.1.refs_0_.refs_1_, bf16[2,512,768]{2,1,0:T(8,128)(2,1)} %collective-permute-done.1.refs_2_, ...), custom_call_target="tpu_custom_call" | custom-call | flops 4227858432 | bytes 12582912 | tf_op jit(solution)/shard_map/forward/pallas_call | solution.py:226
  120.5 1.9 collective-permute-start.6
  122.4 2.4 %collective-permute-done.6 = bf16[4,3,48,768]{3,2,1,0:T(8,128)(2,1)S(1)} collective-permute-done((bf16[4,3,48,768]{3,2,1,0:T(8,128)(2,1)S(1)}, bf16[4,3,48,768]{3,2,1,0:T(8,128)(2,1)S(1)}, u32[]{:S(2)}, u32[]{:S(2)}) %collective-permute-start.6) | collective-permute-done | bytes 884768 | tf_op jit(solution)/shard_map/ppermute | solution.py:291
  125.9 4.8 %all-to-all-start.4 = ((bf16[4,3,48,768]{3,2,1,0:T(8,128)(2,1)}), bf16[4,3,48,768]{3,2,1,0:T(8,128)(2,1)S(1)}, u32[]{:S(2)}, u32[]{:S(2)}) async-start(bf16[4,3,48,768]{3,2,1,0:T(8,128)(2,1)} %add_convert_fusion), calls=%async_computation.4 | async-start | bytes 1769472 | tf_op jit(solution)/shard_map/all_to_all | solution.py:317
  130.8 31.8 %collective-permute-start.5 = (bf16[2,512,384]{2,1,0:T(8,128)(2,1)}, bf16[2,512,384]{2,1,0:T(8,128)(2,1)S(1)}, u32[]{:S(2)}, u32[]{:S(2)}) collective-permute-start(bf16[2,512,384]{2,1,0:T(8,128)(2,1)} %get-tuple-element.9.pre_ref), channel_id=1, source_target_pairs={{0,2},{2,4},{4,6},{6,8},{8,10},{10,12},{12,14},{1,3},{3,5},{5,7},{... | collective-permute-start | bytes 2359304 | tf_op jit(solution)/shard_map/ppermute | solution.py:287
  162.6 1.9 collective-permute-start.4
  165.5 10.0 %all-to-all-start.5 = ((bf16[4,16,24,128]{3,2,1,0:T(8,128)(2,1)}), bf16[4,16,24,128]{3,2,1,0:T(8,128)(2,1)S(1)}, u32[]{:S(2)}, u32[]{:S(2)}) async-start(bf16[4,16,24,128]{3,2,1,0:T(8,128)(2,1)} %bitcast.1), calls=%async_computation.5 | async-start | bytes 786432 | tf_op jit(solution)/shard_map/all_to_all | solution.py:319
  175.5 22.2 %collective-permute-done.5.low_ref.refs_1_ = bf16[2,512,384]{2,1,0:T(8,128)(2,1)S(1)} collective-permute-done((bf16[2,512,384]{2,1,0:T(8,128)(2,1)}, bf16[2,512,384]{2,1,0:T(8,128)(2,1)S(1)}, u32[]{:S(2)}, u32[]{:S(2)}) %collective-permute-start.5) | collective-permute-done | bytes 786464 | tf_op jit(solution)/shard_map/ppermute | solution.py:287
  197.8 5.9 %collective-permute-done.4.up_ref.refs_0_ = bf16[2,512,384]{2,1,0:T(8,128)(2,1)S(1)} collective-permute-done((bf16[2,512,384]{2,1,0:T(8,128)(2,1)}, bf16[2,512,384]{2,1,0:T(8,128)(2,1)S(1)}, u32[]{:S(2)}, u32[]{:S(2)}) %collective-permute-start.4) | collective-permute-done | bytes 786464 | tf_op jit(solution)/shard_map/ppermute | solution.py:287
  203.7 2.7 %all-to-all-done.5.in_ref = bf16[4,16,24,128]{3,2,1,0:T(8,128)(2,1)S(1)} async-done(((bf16[4,16,24,128]{3,2,1,0:T(8,128)(2,1)}), bf16[4,16,24,128]{3,2,1,0:T(8,128)(2,1)S(1)}, u32[]{:S(2)}, u32[]{:S(2)}) %all-to-all-start.5) | async-done | bytes 393248 | tf_op jit(solution)/shard_map/all_to_all | solution.py:319
  207.1 3.5 %all-to-all-start.6 = ((bf16[16,24,128]{2,1,0:T(8,128)(2,1)}), bf16[16,24,128]{2,1,0:T(8,128)(2,1)S(1)}, u32[]{:S(2)}, u32[]{:S(2)}) async-start(bf16[16,24,128]{2,1,0:T(8,128)(2,1)} %copy-done.12), calls=%async_computation.6 | async-start | bytes 196608 | tf_op jit(solution)/shard_map/all_to_all | solution.py:320
  216.3 7.2 %backward.1 = bf16[2,512,768]{2,1,0:T(8,128)(2,1)} custom-call(bf16[2,512,768]{2,1,0:T(8,128)(2,1)S(1)} %copy-done.1, bf16[2,512,768]{2,1,0:T(8,128)(2,1)S(1)} %copy-done.7, bf16[2,512,384]{2,1,0:T(8,128)(2,1)S(1)} %collective-permute-done.4.up_ref.refs_0_, bf16[2,512,384]{2,1,0:T(8,128)(2,1)} %get-tuple-element.9.pre_ref, ...), custom_call_target="tpu_custom_call" | custom-call | flops 1811939328 | bytes 12582912 | tf_op jit(solution)/shard_map/backward/pallas_call | solution.py:271
  (42 shorter events, 14.3 us)
Async XLA Ops:
  0.6 1.4 copy-start
  2.0 1.6 copy-start.13
  2.0 1.6 copy-start.14
  33.1 43.9 %all-to-all-start.1 = ((bf16[4,16,24,128]{3,2,1,0:T(8,128)(2,1)}), bf16[4,16,24,128]{3,2,1,0:T(8,128)(2,1)S(1)}, u32[]{:S(2)}, u32[]{:S(2)}) async-start(bf16[4,16,24,128]{3,2,1,0:T(8,128)(2,1)} %broadcast_in_dim.2), calls=%async_computation.1 | async-start | bytes 786432 | tf_op jit(solution)/shard_map/all_to_all | solution.py:306
  37.6 73.6 %collective-permute-start.1 = (bf16[2,512,768]{2,1,0:T(8,128)(2,1)S(1)}, bf16[2,512,768]{2,1,0:T(8,128)(2,1)}, u32[]{:S(2)}, u32[]{:S(2)}) collective-permute-start(bf16[2,512,768]{2,1,0:T(8,128)(2,1)S(1)} %activate.1.refs_0_.refs_1_), channel_id=1, source_target_pairs={{2,0},{4,2},{6,4},{8,6},{10,8},{12,10},{14,12},{3,1},{5,3},{7,5},{... | collective-permute-start | bytes 4718600 | tf_op jit(solution)/shard_map/ppermute | solution.py:287
  43.0 68.2 %collective-permute-start = (bf16[2,512,768]{2,1,0:T(8,128)(2,1)S(1)}, bf16[2,512,768]{2,1,0:T(8,128)(2,1)}, u32[]{:S(2)}, u32[]{:S(2)}) collective-permute-start(bf16[2,512,768]{2,1,0:T(8,128)(2,1)S(1)} %activate.1.refs_0_.refs_1_), channel_id=1, source_target_pairs={{0,2},{2,4},{4,6},{6,8},{8,10},{10,12},{12,14},{1,3},{3,5},{5,7},{... | collective-permute-start | bytes 4718600 | tf_op jit(solution)/shard_map/ppermute | solution.py:287
  92.3 28.2 %copy-start.2 = (bf16[4,2,48,768]{3,2,1,0:T(8,128)(2,1)}, bf16[4,2,48,768]{3,2,1,0:T(8,128)(2,1)S(1)}, u32[]{:S(2)}) copy-start(bf16[4,2,48,768]{3,2,1,0:T(8,128)(2,1)S(1)} %all_to_all.36.refs_5_.refs_1_) | copy-start | bytes 1769476
  92.3 11.9 %all-to-all-start.2 = ((bf16[4,2,48,768]{3,2,1,0:T(8,128)(2,1)}), bf16[4,2,48,768]{3,2,1,0:T(8,128)(2,1)S(1)}, u32[]{:S(2)}, u32[]{:S(2)}) async-start(bf16[4,2,48,768]{3,2,1,0:T(8,128)(2,1)} %get-tuple-element.7), calls=%async_computation.2 | async-start | bytes 1179648 | tf_op jit(solution)/shard_map/all_to_all | solution.py:308
  97.2 14.0 %collective-permute-start.3 = (bf16[4,2,48,768]{3,2,1,0:T(8,128)(2,1)S(1)}, bf16[4,2,48,768]{3,2,1,0:T(8,128)(2,1)S(1)}, u32[]{:S(2)}, u32[]{:S(2)}) collective-permute-start(bf16[4,2,48,768]{3,2,1,0:T(8,128)(2,1)S(1)} %all_to_all.36.refs_5_.refs_1_), channel_id=1, source_target_pairs={{0,1},{1,0},{2,3},{3,2},{4,5},{5,4},{6,7},{7,6},{8,9},{9,8},{10,11... | collective-permute-start | bytes 1769480 | tf_op jit(solution)/shard_map/ppermute | solution.py:291
  104.1 16.3 %copy-start.4 = (bf16[4,2,48,768]{3,2,1,0:T(8,128)(2,1)}, bf16[4,2,48,768]{3,2,1,0:T(8,128)(2,1)S(1)}, u32[]{:S(2)}) copy-start(bf16[4,2,48,768]{3,2,1,0:T(8,128)(2,1)S(1)} %all-to-all-done.2.refs_4_.refs_0_) | copy-start | bytes 1769476
  104.2 7.0 %collective-permute-start.2 = (bf16[4,2,48,768]{3,2,1,0:T(8,128)(2,1)S(1)}, bf16[4,2,48,768]{3,2,1,0:T(8,128)(2,1)S(1)}, u32[]{:S(2)}, u32[]{:S(2)}) collective-permute-start(bf16[4,2,48,768]{3,2,1,0:T(8,128)(2,1)S(1)} %all-to-all-done.2.refs_4_.refs_0_), channel_id=1, source_target_pairs={{0,1},{1,0},{2,3},{3,2},{4,5},{5,4},{6,7},{7,6},{8,9},{9,8},{10,11... | collective-permute-start | bytes 1769480 | tf_op jit(solution)/shard_map/ppermute | solution.py:291
  111.2 9.3 %copy-start.8 = (bf16[4,2,48,768]{3,2,1,0:T(8,128)(2,1)}, bf16[4,2,48,768]{3,2,1,0:T(8,128)(2,1)S(1)}, u32[]{:S(2)}) copy-start(bf16[4,2,48,768]{3,2,1,0:T(8,128)(2,1)S(1)} %collective-permute-done.3.refs_7_.refs_3_) | copy-start | bytes 1769476
  111.2 1.6 copy-start.6
  112.8 7.7 %copy-start.10 = (bf16[4,2,48,768]{3,2,1,0:T(8,128)(2,1)}, bf16[4,2,48,768]{3,2,1,0:T(8,128)(2,1)S(1)}, u32[]{:S(2)}) copy-start(bf16[4,2,48,768]{3,2,1,0:T(8,128)(2,1)S(1)} %collective-permute-done.2.refs_6_.refs_2_) | copy-start | bytes 1769476
  120.5 4.3 %collective-permute-start.6 = (bf16[4,3,48,768]{3,2,1,0:T(8,128)(2,1)S(1)}, bf16[4,3,48,768]{3,2,1,0:T(8,128)(2,1)S(1)}, u32[]{:S(2)}, u32[]{:S(2)}) collective-permute-start(bf16[4,3,48,768]{3,2,1,0:T(8,128)(2,1)S(1)} %get-tuple-element.11), channel_id=1, source_target_pairs={{0,1},{1,0},{2,3},{3,2},{4,5},{5,4},{6,7},{7,6},{8,9},{9,8},{10,11... | collective-permute-start | bytes 2654216 | tf_op jit(solution)/shard_map/ppermute | solution.py:291
  125.9 38.6 %all-to-all-start.4 = ((bf16[4,3,48,768]{3,2,1,0:T(8,128)(2,1)}), bf16[4,3,48,768]{3,2,1,0:T(8,128)(2,1)S(1)}, u32[]{:S(2)}, u32[]{:S(2)}) async-start(bf16[4,3,48,768]{3,2,1,0:T(8,128)(2,1)} %add_convert_fusion), calls=%async_computation.4 | async-start | bytes 1769472 | tf_op jit(solution)/shard_map/all_to_all | solution.py:317
  130.8 67.0 %collective-permute-start.5 = (bf16[2,512,384]{2,1,0:T(8,128)(2,1)}, bf16[2,512,384]{2,1,0:T(8,128)(2,1)S(1)}, u32[]{:S(2)}, u32[]{:S(2)}) collective-permute-start(bf16[2,512,384]{2,1,0:T(8,128)(2,1)} %get-tuple-element.9.pre_ref), channel_id=1, source_target_pairs={{0,2},{2,4},{4,6},{6,8},{8,10},{10,12},{12,14},{1,3},{3,5},{5,7},{... | collective-permute-start | bytes 2359304 | tf_op jit(solution)/shard_map/ppermute | solution.py:287
  162.6 41.0 %collective-permute-start.4 = (bf16[2,512,384]{2,1,0:T(8,128)(2,1)}, bf16[2,512,384]{2,1,0:T(8,128)(2,1)S(1)}, u32[]{:S(2)}, u32[]{:S(2)}) collective-permute-start(bf16[2,512,384]{2,1,0:T(8,128)(2,1)} %get-tuple-element.9.pre_ref), channel_id=1, source_target_pairs={{2,0},{4,2},{6,4},{8,6},{10,8},{12,10},{14,12},{3,1},{5,3},{7,5},{... | collective-permute-start | bytes 2359304 | tf_op jit(solution)/shard_map/ppermute | solution.py:287
  165.5 45.1 %copy-start.1 = (bf16[2,512,768]{2,1,0:T(8,128)(2,1)S(1)}, bf16[2,512,768]{2,1,0:T(8,128)(2,1)}, u32[]{:S(2)}) copy-start(bf16[2,512,768]{2,1,0:T(8,128)(2,1)} %in_ref.3) | copy-start | bytes 4718596
  165.5 40.9 %all-to-all-start.5 = ((bf16[4,16,24,128]{3,2,1,0:T(8,128)(2,1)}), bf16[4,16,24,128]{3,2,1,0:T(8,128)(2,1)S(1)}, u32[]{:S(2)}, u32[]{:S(2)}) async-start(bf16[4,16,24,128]{3,2,1,0:T(8,128)(2,1)} %bitcast.1), calls=%async_computation.5 | async-start | bytes 786432 | tf_op jit(solution)/shard_map/all_to_all | solution.py:319
  207.1 16.7 %all-to-all-start.6 = ((bf16[16,24,128]{2,1,0:T(8,128)(2,1)}), bf16[16,24,128]{2,1,0:T(8,128)(2,1)S(1)}, u32[]{:S(2)}, u32[]{:S(2)}) async-start(bf16[16,24,128]{2,1,0:T(8,128)(2,1)} %copy-done.12), calls=%async_computation.6 | async-start | bytes 196608 | tf_op jit(solution)/shard_map/all_to_all | solution.py:320
  210.6 1.1 copy-start.3
  211.7 1.1 copy-start.5
  212.7 1.4 copy-start.7
  (3 other events, 2.8 us)

commit v4 on v3

v4 whole, which is shorter than its diff:
```python
import functools

import jax
import jax.numpy as jnp
from jax import lax
from jax.experimental import pallas as pl
from jax.experimental.pallas import tpu as pltpu
from jax.sharding import Mesh
from jax.sharding import PartitionSpec as P

LANES = 128
X_PARTS, Y_PARTS, Z_PARTS, CORES = 4, 2, 4, 2
GROUPS = 1
MIB = 1024 * 1024

EPSILON = 1e-06
GELU_SCALE = 0.7978845608028654
GELU_CUBIC = 0.044715


def gelu_tanh(values):
    return (
        0.5
        * values
        * (1.0 + jnp.tanh(GELU_SCALE * (values + GELU_CUBIC * values * values * values)))
    )


def gelu_slope(values):
    tangent = jnp.tanh(GELU_SCALE * (values + GELU_CUBIC * values * values * values))
    return 0.5 * (1.0 + tangent) + 0.5 * values * (1.0 - tangent * tangent) * GELU_SCALE * (
        1.0 + 3.0 * GELU_CUBIC * values * values
    )


def dot(left, right, left_dim, right_dim):
    return lax.dot_general(
        left, right, (((left_dim,), (right_dim,)), ((), ())), preferred_element_type=jnp.float32
    )


def normalize(values):
    floats = values.astype(jnp.float32)
    row_scale = lax.rsqrt(jnp.mean(floats * floats, axis=-1, keepdims=True) + EPSILON)
    return floats * row_scale, row_scale


def params(mib):
    return pltpu.CompilerParams(vmem_limit_bytes=mib * MIB)


def struct(shape, dtype):
    return jax.ShapeDtypeStruct(shape, dtype)


def cost(flops, nbytes):
    return pl.CostEstimate(flops=flops, bytes_accessed=nbytes, transcendentals=0)


ANYWHERE = pl.BlockSpec(memory_space=pl.ANY)
IN_VMEM = pl.BlockSpec(memory_space=pltpu.VMEM)


def pack_kernel(conv_ref, point_ref, out_ref):
    taps, c_part, f_part = conv_ref.shape
    pieces = [conv_ref[tap].astype(jnp.float32) for tap in range(taps)]
    pieces.append(point_ref[...].astype(jnp.float32).T)
    pieces.append(jnp.zeros((c_part, LANES - (taps + 1) * f_part), jnp.float32))
    packed = jnp.concatenate(pieces, axis=1).astype(out_ref.dtype)
    out_ref[...] = jnp.broadcast_to(packed[None], out_ref.shape)


def pack(conv_weight, point_weight, peers):
    c_part = conv_weight.shape[1]
    return pl.pallas_call(
        pack_kernel,
        out_shape=struct((peers, c_part, LANES), conv_weight.dtype),
        compiler_params=params(8),
        cost_estimate=cost(0, 2 * peers * c_part * LANES),
        name="pack",
    )(conv_weight, point_weight)


def assemble_kernel(f_part, taps, in_ref, _, out_ref):
    blocks = in_ref.shape[0] // Y_PARTS
    for low in range(Y_PARTS):
        pieces = [in_ref[Y_PARTS * block + low].astype(jnp.float32) for block in range(blocks)]
        rows = jnp.concatenate(
            [
                piece[:, tap * f_part : (tap + 1) * f_part]
                for tap in range(taps)
                for piece in pieces
            ],
            axis=1,
        )
        span = rows.shape[0]
        for copy in range(Z_PARTS):
            out_ref[copy, pl.ds(low * span, span), :] = rows.astype(out_ref.dtype)


def assemble(gathered, f_part, taps, after):
    peers, c_part, _ = gathered.shape
    lanes = peers // Y_PARTS * taps * f_part
    return pl.pallas_call(
        functools.partial(assemble_kernel, f_part, taps),
        in_specs=[IN_VMEM, ANYWHERE],
        out_shape=struct((Z_PARTS, Y_PARTS * c_part, lanes), gathered.dtype),
        compiler_params=params(8),
        cost_estimate=cost(0, 4 * gathered.size * 2),
        name="assemble",
    )(gathered, after)


def turn_kernel(f_part, own_ref, other_ref, out_ref):
    taps, rows, width = own_ref.shape
    far, near, span, lanes = out_ref.shape[1], out_ref.shape[0], *out_ref.shape[2:]
    total = [own_ref[tap] + other_ref[tap].astype(jnp.float32) for tap in range(taps)]
    blocks = [
        total[tap][block * f_part : (block + 1) * f_part]
        for block in range(rows // f_part)
        for tap in range(taps)
    ]
    blocks.append(jnp.zeros((lanes - taps * rows, width), jnp.float32))
    turned = jnp.concatenate(blocks, axis=0).T
    for zh in range(far):
        for zl in range(near):
            first = (zh * near + zl) * span
            out_ref[zl, zh] = turned[first : first + span].astype(out_ref.dtype)


def turn(own, other, f_part, depth):
    taps, rows, width = own.shape
    lanes = -(-taps * rows // LANES) * LANES
    out = (Z_PARTS, depth // Z_PARTS, width // depth, lanes)
    return pl.pallas_call(
        functools.partial(turn_kernel, f_part),
        out_shape=struct(out, jnp.bfloat16),
        compiler_params=params(16),
        cost_estimate=cost(0, 8 * own.size),
        name="turn",
    )(own, other)


def split_kernel(lanes, in_ref, *refs):
    out_ref = refs[-1]
    total = sum(in_ref[p].astype(jnp.float32) for p in range(in_ref.shape[0]))
    span = out_ref.shape[1]
    blank = jnp.zeros((span, LANES - lanes), jnp.float32)
    for block in range(out_ref.shape[0] // Y_PARTS):
        for low in range(Y_PARTS):
            part = total[low * span : (low + 1) * span, block * lanes : (block + 1) * lanes]
            part = jnp.concatenate([part, blank], axis=1)
            out_ref[Y_PARTS * block + low] = part.astype(out_ref.dtype)


def split(parts, lanes, blocks, after):
    return pl.pallas_call(
        functools.partial(split_kernel, lanes),
        in_specs=[IN_VMEM] + [ANYWHERE] * len(after),
        out_shape=struct((blocks * Y_PARTS, parts.shape[1] // Y_PARTS, LANES), parts.dtype),
        compiler_params=params(8),
        cost_estimate=cost(0, 4 * parts.size),
        name="split",
    )(parts, *after)


def add_kernel(in_ref, out_ref):
    total = sum(in_ref[p].astype(jnp.float32) for p in range(in_ref.shape[0]))
    out_ref[...] = total.astype(out_ref.dtype)


def add_parts(parts):
    return pl.pallas_call(
        add_kernel,
        out_shape=struct(parts.shape[1:], parts.dtype),
        compiler_params=params(8),
        cost_estimate=cost(0, 4 * parts.size),
        name="add_parts",
    )(parts)


def finish_kernel(in_ref, out_ref):
    taps, _, f_part = out_ref.shape
    total = sum(in_ref[p].astype(jnp.float32) for p in range(in_ref.shape[0]))
    for tap in range(taps):
        out_ref[tap] = total[:, tap * f_part : (tap + 1) * f_part]


def finish(pieces, taps, f_part):
    return pl.pallas_call(
        finish_kernel,
        out_shape=struct((taps, pieces.shape[1], f_part), jnp.float32),
        compiler_params=params(8),
        cost_estimate=cost(0, 4 * pieces.size),
        name="finish",
    )(pieces)


def act_kernel(in_ref, _, out_ref):
    normed, _ = normalize(in_ref[...])
    out_ref[...] = gelu_tanh(normed).astype(out_ref.dtype)


def activate(inputs, block, after):
    samples, bins, width = inputs.shape
    rows = pl.BlockSpec((None, block, width), lambda s, i: (s, i, 0))
    return pl.pallas_call(
        act_kernel,
        grid=(samples, bins // block),
        in_specs=[rows, ANYWHERE],
        out_specs=rows,
        out_shape=struct(inputs.shape, inputs.dtype),
        compiler_params=params(8),
        cost_estimate=cost(20 * inputs.size, 4 * inputs.size),
        name="activate",
    )(inputs, after)


def join_weights(own_refs, other_refs, joined, point):
    near, each, span, lanes = own_refs[0].shape
    half = lanes // 4
    for side, refs in enumerate((own_refs, other_refs)):
        for group, ref in enumerate(refs):
            for zl in range(near):
                for part in range(each):
                    zh = group * each + part
                    rows = pl.ds((zh * near + zl) * span, span)
                    block = ref[zl, part]
                    for tap in range(4):
                        piece = block[:, tap * half : (tap + 1) * half]
                        if tap < 3:
                            joined[tap, rows, side * half : (side + 1) * half] = piece
                        else:
                            point[rows, side * half : (side + 1) * half] = piece


def forward_kernel(scale, *refs):
    acts_refs, cot_ref, refs = refs[:3], refs[3], refs[4:]
    own_w, other_w, refs = refs[:GROUPS], refs[GROUPS : 2 * GROUPS], refs[2 * GROUPS :]
    pre_ref, own_out, other_out, weights, point, turned = refs
    samples, bins, width = cot_ref.shape
    half = weights.shape[2] // CORES
    join_weights(own_w, other_w, weights, point)
    for sample in range(samples):
        low, mid, high = [r[sample] for r in acts_refs]
        shifted_low = dot(low, weights[0], 1, 0).astype(jnp.bfloat16).astype(jnp.float32)
        shifted_high = dot(high, weights[2], 1, 0).astype(jnp.bfloat16).astype(jnp.float32)
        preact = shifted_low + dot(mid, weights[1], 1, 0) + shifted_high
        grad_inner = dot(cot_ref[sample], point[...], 1, 0)
        grad_pre = grad_inner * gelu_slope(preact)
        pre_ref[sample] = grad_pre.astype(jnp.bfloat16)
        turned[:, pl.ds(sample * bins, bins)] = grad_pre.T.astype(jnp.bfloat16)
    for tap, acts_ref in enumerate(acts_refs):
        acts = acts_ref[...].reshape(samples * bins, width)
        term = dot(turned[...], acts, 1, 0) * scale
        own_out[tap] = term[:half]
        other_out[tap] = term[half:].astype(jnp.bfloat16)


def forward(acts, cotangent, own_w, other_w, scale):
    samples, bins, width = cotangent.shape
    hidden = CORES * own_w[0].shape[3] // 4
    half = (3, hidden // CORES, width)
    return pl.pallas_call(
        functools.partial(forward_kernel, scale),
        out_shape=[
            struct((samples, bins, hidden), jnp.bfloat16),
            struct(half, jnp.float32),
            struct(half, jnp.bfloat16),
            struct((3, width, hidden), jnp.bfloat16),
        ],
        scratch_shapes=[
            pltpu.VMEM((width, hidden), jnp.bfloat16),
            pltpu.VMEM((hidden, samples * bins), jnp.bfloat16),
        ],
        compiler_params=params(24),
        cost_estimate=cost(14 * samples * bins * width * hidden, 16 * samples * bins * width),
        name="forward",
    )(*acts, cotangent, *own_w, *other_w)


def backward_kernel(in_ref, cot_ref, up_ref, pre_ref, low_ref, weights, out_ref):
    for sample in range(in_ref.shape[0]):
        grad_act = (
            dot(up_ref[sample], weights[0], 1, 1)
            + dot(pre_ref[sample], weights[1], 1, 1)
            + dot(low_ref[sample], weights[2], 1, 1)
        )
        normed, row_scale = normalize(in_ref[sample])
        grad_norm = grad_act * gelu_slope(normed)
        center = jnp.mean(grad_norm * normed, axis=-1, keepdims=True)
        grad = cot_ref[sample].astype(jnp.float32) + row_scale * (grad_norm - normed * center)
        out_ref[sample] = grad.astype(out_ref.dtype)


def backward(inputs, cotangent, grad_upper, grad_pre, grad_lower, weights, block):
    samples, bins, width = inputs.shape
    hidden = grad_pre.shape[2]
    wide = pl.BlockSpec((samples, block, width), lambda i: (0, i, 0))
    narrow = pl.BlockSpec((samples, block, hidden), lambda i: (0, i, 0))
    whole = pl.BlockSpec(weights.shape, lambda i: (0, 0, 0), pipeline_mode=pl.Buffered(1))
    return pl.pallas_call(
        backward_kernel,
        grid=(bins // block,),
        in_specs=[wide, wide, narrow, narrow, narrow, whole],
        out_specs=wide,
        out_shape=struct(inputs.shape, inputs.dtype),
        compiler_params=params(24),
        cost_estimate=cost(6 * samples * bins * width * hidden, 16 * samples * bins * width),
        name="backward",
    )(inputs, cotangent, grad_upper, grad_pre, grad_lower, weights)


def shifted(array, by):
    count = X_PARTS * Y_PARTS
    pairs = [(i, i + by) for i in range(count) if 0 <= i + by < count]
    return lax.ppermute(array, ("x", "yh"), pairs)


def other_core(array):
    return lax.ppermute(array, "core", [(0, 1), (1, 0)])


def body(inputs, conv_weight, point_weight, cotangent):
    samples, bins, width = inputs.shape
    taps, c_part, f_part = conv_weight.shape
    near, far = lax.axis_size("zl"), lax.axis_size("zh")
    depth = near * far
    blocks = X_PARTS * Y_PARTS
    devices = depth * Y_PARTS * blocks * CORES
    grad_scale = float(samples * bins * devices) ** (-0.5)
    plane = ("x", "yh", "yl")

    packed = pack(conv_weight, point_weight, blocks * Y_PARTS)
    pieces = lax.all_to_all(packed, plane, 0, 0)

    acted = activate(inputs, 256, pieces)
    acts = (shifted(acted, 1), acted, shifted(acted, -1))

    def along_z(spread):
        part = lax.all_to_all(spread, "zh", 0, 0)
        part = lax.all_to_all(jnp.broadcast_to(part[None], (near,) + part.shape), "zl", 0, 0)
        return part, other_core(part)

    def nothing(spread):
        blank = jnp.zeros((near,) + spread.shape, spread.dtype)
        return blank, blank

    spread = assemble(pieces, f_part, taps + 1, acted)[:far]
    own_w, other_w = lax.cond(lax.axis_index("x") < X_PARTS, along_z, nothing, spread)

    grad_pre, own, other, weights = forward(acts, cotangent, [own_w], [other_w], grad_scale)

    grad_upper = shifted(grad_pre, -1)
    grad_lower = shifted(grad_pre, 1)

    sums = lax.all_to_all(turn(own, other_core(other), f_part, depth), "zl", 0, 0)
    sums = lax.all_to_all(add_parts(sums), "zh", 0, 0)
    sums = split(sums, taps * f_part, blocks, (grad_upper, grad_lower))
    conv_grad = finish(lax.all_to_all(sums, plane, 0, 0), taps, f_part)

    input_grad = backward(inputs, cotangent, grad_upper, grad_pre, grad_lower, weights, 256)
    return (input_grad, conv_grad)


def solution(mesh):
    depth = mesh.shape["dp"] // Y_PARTS
    fine = Mesh(
        mesh.devices.reshape(depth // Z_PARTS, Z_PARTS, Y_PARTS, X_PARTS, Y_PARTS, CORES),
        ("zh", "zl", "yl", "x", "yh", "core"),
    )
    dp, seq = ("zh", "zl", "yl"), ("x", "yh", "core")
    return jax.shard_map(
        body,
        mesh=fine,
        in_specs=(P(dp, seq, None), P(None, dp, seq), P(seq, dp), P(dp, seq, None)),
        out_specs=(P(dp, seq, None), P(None, dp, seq)),
        check_vma=False,
    )
```

time: 226 us -> 186 us (0.82)
  waiting for transfers between devices: 75.8 us -> 39 us
  starting transfers between devices: 74.6 us -> 39.4 us
  blocking collectives: 42.8 us -> 77.8 us
  local copies, waits for them, and re-layouts: 10.1 us -> 7.01 us
    all_to_all x2 -> x3, blocking collectives: 42.8 us -> 77.8 us  [the longest x1 33.3 us: along_z(): part = lax.all_to_all(spread, 'zh', 0, 0)]
    ppermute x4, waiting for transfers between devices: 33.2 us -> 5.01 us  [shifted(): return lax.ppermute(array, ('x', 'yh'), pairs)]
    ppermute x4, starting transfers between devices: 41.1 us -> 15.6 us  [shifted(): return lax.ppermute(array, ('x', 'yh'), pairs)]
    all_to_all x5 -> x3, waiting for transfers between devices: 40.2 us -> 28.6 us  [the longest x1 16.6 us: body(): lax.all_to_all(turn(own, other_core(other), f_part, depth), 'zl', 0, 0)]
    all_to_all x5 -> x3, starting transfers between devices: 27.7 us -> 19.9 us  [the longest x1 10.2 us: body(): sums = lax.all_to_all(add_parts(sums), 'zh', 0, 0)]
    ppermute x3 -> x2, waiting for transfers between devices: 2.4 us -> 5.42 us  [other_core(): return lax.ppermute(array, 'core', [(0, 1), (1, 0)])]
    unnamed x30 -> x16, local copies, waits for them, and re-layouts: 9.33 us -> 6.94 us
    ppermute x3 -> x2, starting transfers between devices: 5.74 us -> 3.94 us  [other_core(): return lax.ppermute(array, 'core', [(0, 1), (1, 0)])]
  transfers between devices with their start and end apart: 12 -> 9, of which waited for: 8 -> 6; matrix products, arithmetic and copies ran while one was open for 0% -> 0% of each run, Pallas kernels for 4% -> 4%
where the time goes in v4:
time: 186 us; the launch traced here: 185 us
  blocking collectives  77.8 us (42%)
  starting transfers between devices  39.4 us (21%)
  waiting for transfers between devices  39 us (21%)
  Pallas kernels  20.8 us (11%)
  local copies, waits for them, and re-layouts  7.01 us (4%)
    all_to_all x1, blocking collectives, along_z(): part = lax.all_to_all(spread, 'zh', 0, 0)  33.3 us
    all_to_all x1, blocking collectives, along_z(): lax.all_to_all(jnp.broadcast_to(part[None], (near,) + part.shape), 'zl',...  29.7 us
    all_to_all x1, waiting for transfers between devices, body(): lax.all_to_all(turn(own, other_core(other), f_part, depth), 'zl', 0, 0)  16.6 us
    ppermute x4, starting transfers between devices, shifted(): return lax.ppermute(array, ('x', 'yh'), pairs)  15.6 us
    all_to_all x1, blocking collectives, body(): pieces = lax.all_to_all(packed, plane, 0, 0)  14.7 us
    all_to_all x1, waiting for transfers between devices, body(): sums = lax.all_to_all(add_parts(sums), 'zh', 0, 0)  12 us
    all_to_all x1, starting transfers between devices, body(): sums = lax.all_to_all(add_parts(sums), 'zh', 0, 0)  10.2 us
    pallas_call x1, Pallas kernels, forward(): pl.pallas_call(functools.partial(forward_kernel, scale), out_shape=[struc...  8.33 us
  transfers between devices with their start and end apart: 9, of which 6 were waited for; matrix products, arithmetic and copies ran while one was open for 0% of the time, Pallas kernels for 4%

profile of v4, /device:TPU:2, one launch (start us, length us, event | category | flops | bytes accessed | tf_op | source)
XLA Modules:
  0.0 184.8 jit_solution(1746301783766027151)
XLA Ops:
  2.2 14.7 %all_to_all.30._.in_ref = bf16[16,24,128]{2,1,0:T(8,128)(2,1)S(1)} all-to-all(bf16[16,24,128]{2,1,0:T(8,128)(2,1)S(1)} %pack.1), channel_id=1, replica_groups=mesh['zh'=4,'zl'=4,'yl'=2,'x'=4,'yh'=2,'core'=2] {'x','yh','yl'}, dimensions={0} | all-to-all | bytes 196608 | tf_op jit(solution)/shard_map/all_to_all | solution.py:335
  16.9 1.4 copy-done
  18.3 1.5 activate.1._.refs_1_
  19.9 4.3 %collective-permute-start.2 = (bf16[2,512,768]{2,1,0:T(8,128)(2,1)S(1)}, bf16[2,512,768]{2,1,0:T(8,128)(2,1)}, u32[]{:S(2)}, u32[]{:S(2)}) collective-permute-start(bf16[2,512,768]{2,1,0:T(8,128)(2,1)S(1)} %activate.1._.refs_1_), channel_id=1, source_target_pairs={{2,0},{4,2},{6,4},{8,6},{10,8},{12,10},{14,12},{3,1},{5,3},{7,5},{... | collective-permute-start | bytes 4718600 | tf_op jit(solution)/shard_map/ppermute | solution.py:317
  24.2 3.0 %collective-permute-start.1 = (bf16[2,512,768]{2,1,0:T(8,128)(2,1)S(1)}, bf16[2,512,768]{2,1,0:T(8,128)(2,1)}, u32[]{:S(2)}, u32[]{:S(2)}) collective-permute-start(bf16[2,512,768]{2,1,0:T(8,128)(2,1)S(1)} %activate.1._.refs_1_), channel_id=1, source_target_pairs={{0,2},{2,4},{4,6},{6,8},{8,10},{10,12},{12,14},{1,3},{3,5},{5,7},{... | collective-permute-start | bytes 4718600 | tf_op jit(solution)/shard_map/ppermute | solution.py:317
  27.4 68.2 %conditional.1 = (bf16[4,4,48,768]{3,2,1,0:T(8,128)(2,1)}, bf16[4,4,48,768]{3,2,1,0:T(8,128)(2,1)}) conditional(s32[]{:T(128)} %convert_element_type.3, () %tuple.16, bf16[4,48,768]{2,1,0:T(8,128)(2,1)S(1)} %assemble.1), branch_computations={%region_0.0_spmd, %region_1.0_spmd} | conditional | bytes 9142328 | solution.py:350
  27.4 33.3 %all_to_all.28 = bf16[4,48,768]{2,1,0:T(8,128)(2,1)S(1)} all-to-all(bf16[4,48,768]{2,1,0:T(8,128)(2,1)S(1)} %param.1), channel_id=1, replica_groups=mesh['zh'=4,'zl'=4,'yl'=2,'x'=4,'yh'=2,'core'=2] {'zh'}, dimensions={0} | all-to-all | bytes 589824 | tf_op jit(solution)/shard_map/cond/branch_1_fun/all_to_all | solution.py:341
  60.8 29.7 %all_to_all.29 = bf16[4,4,48,768]{3,2,1,0:T(8,128)(2,1)} all-to-all(bf16[4,4,48,768]{3,2,1,0:T(8,128)(2,1)S(1)} %broadcast_in_dim.0), channel_id=1, replica_groups=mesh['zh'=4,'zl'=4,'yl'=2,'x'=4,'yh'=2,'core'=2] {'zl'}, dimensions={0} | all-to-all | bytes 2359296 | tf_op jit(solution)/shard_map/cond/branch_1_fun/all_to_all | solution.py:342
  90.5 1.9 %collective-permute-start = (bf16[4,4,48,768]{3,2,1,0:T(8,128)(2,1)}, bf16[4,4,48,768]{3,2,1,0:T(8,128)(2,1)}, u32[]{:S(2)}, u32[]{:S(2)}) collective-permute-start(bf16[4,4,48,768]{3,2,1,0:T(8,128)(2,1)} %all_to_all.29), channel_id=1, source_target_pairs={{0,1},{1,0},{2,3},{3,2},{4,5},{5,4},{6,7},{7,6},{8,9},{9,8},{10,11... | collective-permute-start | bytes 3538952 | tf_op jit(solution)/shard_map/cond/branch_1_fun/ppermute | solution.py:321
  92.5 3.2 %collective-permute-done = bf16[4,4,48,768]{3,2,1,0:T(8,128)(2,1)} collective-permute-done((bf16[4,4,48,768]{3,2,1,0:T(8,128)(2,1)}, bf16[4,4,48,768]{3,2,1,0:T(8,128)(2,1)}, u32[]{:S(2)}, u32[]{:S(2)}) %collective-permute-start) | collective-permute-done | bytes 1179680 | tf_op jit(solution)/shard_map/cond/branch_1_fun/ppermute | solution.py:321
  95.6 8.3 %forward.1 = (bf16[2,512,384]{2,1,0:T(8,128)(2,1)}, f32[3,192,768]{2,1,0:T(8,128)S(1)}, bf16[3,192,768]{2,1,0:T(8,128)(2,1)S(1)}, bf16[3,768,384]{2,1,0:T(8,128)(2,1)S(1)}) custom-call(bf16[2,512,768]{2,1,0:T(8,128)(2,1)} %collective-permute-done.1.refs_0_, bf16[2,512,768]{2,1,0:T(8,128)(2,1)S(1)} %activate.1._.refs_1_, ...), custom_call_target="tpu_custom_call" | custom-call | flops 4227858432 | bytes 12582912 | tf_op jit(solution)/shard_map/forward/pallas_call | solution.py:264
  105.2 2.0 %collective-permute-start.5 = (bf16[3,192,768]{2,1,0:T(8,128)(2,1)S(1)}, bf16[3,192,768]{2,1,0:T(8,128)(2,1)S(1)}, u32[]{:S(2)}, u32[]{:S(2)}) collective-permute-start(bf16[3,192,768]{2,1,0:T(8,128)(2,1)S(1)} %get-tuple-element.14), channel_id=1, source_target_pairs={{0,1},{1,0},{2,3},{3,2},{4,5},{5,4},{6,7},{7,6},{8,9},{9,8},{10,11... | collective-permute-start | bytes 2654216 | tf_op jit(solution)/shard_map/ppermute | solution.py:321
  107.3 2.3 %collective-permute-done.5.other_ref = bf16[3,192,768]{2,1,0:T(8,128)(2,1)S(1)} collective-permute-done((bf16[3,192,768]{2,1,0:T(8,128)(2,1)S(1)}, bf16[3,192,768]{2,1,0:T(8,128)(2,1)S(1)}, u32[]{:S(2)}, u32[]{:S(2)}) %collective-permute-start.5) | collective-permute-done | bytes 884768 | tf_op jit(solution)/shard_map/ppermute | solution.py:321
  110.8 3.5 %all-to-all-start.3 = ((bf16[4,4,48,640]{3,2,1,0:T(8,128)(2,1)}), bf16[4,4,48,640]{3,2,1,0:T(8,128)(2,1)S(1)}, u32[]{:S(2)}, u32[]{:S(2)}) async-start(bf16[4,4,48,640]{3,2,1,0:T(8,128)(2,1)} %turn.1), calls=%async_computation.3 | async-start | bytes 1966080 | tf_op jit(solution)/shard_map/all_to_all | solution.py:357
  114.3 4.5 %collective-permute-start.4 = (bf16[2,512,384]{2,1,0:T(8,128)(2,1)}, bf16[2,512,384]{2,1,0:T(8,128)(2,1)S(1)}, u32[]{:S(2)}, u32[]{:S(2)}) collective-permute-start(bf16[2,512,384]{2,1,0:T(8,128)(2,1)} %get-tuple-element.11.pre_ref), channel_id=1, source_target_pairs={{0,2},{2,4},{4,6},{6,8},{8,10},{10,12},{12,14},{1,3},{3,5},{5,7},{... | collective-permute-start | bytes 2359304 | tf_op jit(solution)/shard_map/ppermute | solution.py:317
  118.9 3.7 %collective-permute-start.3 = (bf16[2,512,384]{2,1,0:T(8,128)(2,1)}, bf16[2,512,384]{2,1,0:T(8,128)(2,1)S(1)}, u32[]{:S(2)}, u32[]{:S(2)}) collective-permute-start(bf16[2,512,384]{2,1,0:T(8,128)(2,1)} %get-tuple-element.11.pre_ref), channel_id=1, source_target_pairs={{2,0},{4,2},{6,4},{8,6},{10,8},{12,10},{14,12},{3,1},{5,3},{7,5},{... | collective-permute-start | bytes 2359304 | tf_op jit(solution)/shard_map/ppermute | solution.py:317
  122.6 16.6 %all-to-all-done.3.in_ref = bf16[4,4,48,640]{3,2,1,0:T(8,128)(2,1)S(1)} async-done(((bf16[4,4,48,640]{3,2,1,0:T(8,128)(2,1)}), bf16[4,4,48,640]{3,2,1,0:T(8,128)(2,1)S(1)}, u32[]{:S(2)}, u32[]{:S(2)}) %all-to-all-start.3) | async-done | bytes 983072 | tf_op jit(solution)/shard_map/all_to_all | solution.py:357
  140.0 10.2 %all-to-all-start.4 = ((bf16[4,48,640]{2,1,0:T(8,128)(2,1)}), bf16[4,48,640]{2,1,0:T(8,128)(2,1)S(1)}, u32[]{:S(2)}, u32[]{:S(2)}) async-start(bf16[4,48,640]{2,1,0:T(8,128)(2,1)} %add_parts.1), calls=%async_computation.4 | async-start | bytes 491520 | tf_op jit(solution)/shard_map/all_to_all | solution.py:358
  150.3 2.8 %collective-permute-done.4.low_ref.refs_1_ = bf16[2,512,384]{2,1,0:T(8,128)(2,1)S(1)} collective-permute-done((bf16[2,512,384]{2,1,0:T(8,128)(2,1)}, bf16[2,512,384]{2,1,0:T(8,128)(2,1)S(1)}, u32[]{:S(2)}, u32[]{:S(2)}) %collective-permute-start.4) | collective-permute-done | bytes 786464 | tf_op jit(solution)/shard_map/ppermute | solution.py:317
  153.1 2.2 %collective-permute-done.3.up_ref.refs_0_ = bf16[2,512,384]{2,1,0:T(8,128)(2,1)S(1)} collective-permute-done((bf16[2,512,384]{2,1,0:T(8,128)(2,1)}, bf16[2,512,384]{2,1,0:T(8,128)(2,1)S(1)}, u32[]{:S(2)}, u32[]{:S(2)}) %collective-permute-start.3) | collective-permute-done | bytes 786464 | tf_op jit(solution)/shard_map/ppermute | solution.py:317
  155.3 12.0 %all-to-all-done.4.in_ref = bf16[4,48,640]{2,1,0:T(8,128)(2,1)S(1)} async-done(((bf16[4,48,640]{2,1,0:T(8,128)(2,1)}), bf16[4,48,640]{2,1,0:T(8,128)(2,1)S(1)}, u32[]{:S(2)}, u32[]{:S(2)}) %all-to-all-start.4) | async-done | bytes 245792 | tf_op jit(solution)/shard_map/all_to_all | solution.py:358
  168.0 6.1 %all-to-all-start.5 = ((bf16[16,24,128]{2,1,0:T(8,128)(2,1)}), bf16[16,24,128]{2,1,0:T(8,128)(2,1)S(1)}, u32[]{:S(2)}, u32[]{:S(2)}) async-start(bf16[16,24,128]{2,1,0:T(8,128)(2,1)} %split.1), calls=%async_computation.5 | async-start | bytes 196608 | tf_op jit(solution)/shard_map/all_to_all | solution.py:360
  174.2 1.5 copy-done.3
  177.0 7.1 %backward.1 = bf16[2,512,768]{2,1,0:T(8,128)(2,1)} custom-call(bf16[2,512,768]{2,1,0:T(8,128)(2,1)S(1)} %copy-done.1, bf16[2,512,768]{2,1,0:T(8,128)(2,1)S(1)} %copy-done.5, bf16[2,512,384]{2,1,0:T(8,128)(2,1)S(1)} %collective-permute-done.3.up_ref.refs_0_, bf16[2,512,384]{2,1,0:T(8,128)(2,1)} %get-tuple-element.11.pre_ref, ...), custom_call_target="tpu_custom_call" | custom-call | flops 1811939328 | bytes 12582912 | tf_op jit(solution)/shard_map/backward/pallas_call | solution.py:302
  (24 shorter events, 8.0 us)
Async XLA Ops:
  0.6 0.7 copy-start.6
  1.4 0.7 copy-start.7
  16.9 1.4 copy-start
  19.9 75.8 %collective-permute-start.2 = (bf16[2,512,768]{2,1,0:T(8,128)(2,1)S(1)}, bf16[2,512,768]{2,1,0:T(8,128)(2,1)}, u32[]{:S(2)}, u32[]{:S(2)}) collective-permute-start(bf16[2,512,768]{2,1,0:T(8,128)(2,1)S(1)} %activate.1._.refs_1_), channel_id=1, source_target_pairs={{2,0},{4,2},{6,4},{8,6},{10,8},{12,10},{14,12},{3,1},{5,3},{7,5},{... | collective-permute-start | bytes 4718600 | tf_op jit(solution)/shard_map/ppermute | solution.py:317
  24.2 71.4 %collective-permute-start.1 = (bf16[2,512,768]{2,1,0:T(8,128)(2,1)S(1)}, bf16[2,512,768]{2,1,0:T(8,128)(2,1)}, u32[]{:S(2)}, u32[]{:S(2)}) collective-permute-start(bf16[2,512,768]{2,1,0:T(8,128)(2,1)S(1)} %activate.1._.refs_1_), channel_id=1, source_target_pairs={{0,2},{2,4},{4,6},{6,8},{8,10},{10,12},{12,14},{1,3},{3,5},{5,7},{... | collective-permute-start | bytes 4718600 | tf_op jit(solution)/shard_map/ppermute | solution.py:317
  27.4 68.2 %copy-start.4 = (bf16[2,512,768]{2,1,0:T(8,128)(2,1)S(1)}, bf16[2,512,768]{2,1,0:T(8,128)(2,1)}, u32[]{:S(2)}) copy-start(bf16[2,512,768]{2,1,0:T(8,128)(2,1)} %cot_ref.1) | copy-start | bytes 4718596
  90.5 5.1 %collective-permute-start = (bf16[4,4,48,768]{3,2,1,0:T(8,128)(2,1)}, bf16[4,4,48,768]{3,2,1,0:T(8,128)(2,1)}, u32[]{:S(2)}, u32[]{:S(2)}) collective-permute-start(bf16[4,4,48,768]{3,2,1,0:T(8,128)(2,1)} %all_to_all.29), channel_id=1, source_target_pairs={{0,1},{1,0},{2,3},{3,2},{4,5},{5,4},{6,7},{7,6},{8,9},{9,8},{10,11... | collective-permute-start | bytes 3538952 | tf_op jit(solution)/shard_map/cond/branch_1_fun/ppermute | solution.py:321
  104.0 1.2 copy-start.2
  105.2 4.3 %collective-permute-start.5 = (bf16[3,192,768]{2,1,0:T(8,128)(2,1)S(1)}, bf16[3,192,768]{2,1,0:T(8,128)(2,1)S(1)}, u32[]{:S(2)}, u32[]{:S(2)}) collective-permute-start(bf16[3,192,768]{2,1,0:T(8,128)(2,1)S(1)} %get-tuple-element.14), channel_id=1, source_target_pairs={{0,1},{1,0},{2,3},{3,2},{4,5},{5,4},{6,7},{7,6},{8,9},{9,8},{10,11... | collective-permute-start | bytes 2654216 | tf_op jit(solution)/shard_map/ppermute | solution.py:321
  110.8 28.4 %all-to-all-start.3 = ((bf16[4,4,48,640]{3,2,1,0:T(8,128)(2,1)}), bf16[4,4,48,640]{3,2,1,0:T(8,128)(2,1)S(1)}, u32[]{:S(2)}, u32[]{:S(2)}) async-start(bf16[4,4,48,640]{3,2,1,0:T(8,128)(2,1)} %turn.1), calls=%async_computation.3 | async-start | bytes 1966080 | tf_op jit(solution)/shard_map/all_to_all | solution.py:357
  114.3 38.8 %collective-permute-start.4 = (bf16[2,512,384]{2,1,0:T(8,128)(2,1)}, bf16[2,512,384]{2,1,0:T(8,128)(2,1)S(1)}, u32[]{:S(2)}, u32[]{:S(2)}) collective-permute-start(bf16[2,512,384]{2,1,0:T(8,128)(2,1)} %get-tuple-element.11.pre_ref), channel_id=1, source_target_pairs={{0,2},{2,4},{4,6},{6,8},{8,10},{10,12},{12,14},{1,3},{3,5},{5,7},{... | collective-permute-start | bytes 2359304 | tf_op jit(solution)/shard_map/ppermute | solution.py:317
  118.9 36.4 %collective-permute-start.3 = (bf16[2,512,384]{2,1,0:T(8,128)(2,1)}, bf16[2,512,384]{2,1,0:T(8,128)(2,1)S(1)}, u32[]{:S(2)}, u32[]{:S(2)}) collective-permute-start(bf16[2,512,384]{2,1,0:T(8,128)(2,1)} %get-tuple-element.11.pre_ref), channel_id=1, source_target_pairs={{2,0},{4,2},{6,4},{8,6},{10,8},{12,10},{14,12},{3,1},{5,3},{7,5},{... | collective-permute-start | bytes 2359304 | tf_op jit(solution)/shard_map/ppermute | solution.py:317
  140.0 34.1 %copy-start.1 = (bf16[2,512,768]{2,1,0:T(8,128)(2,1)S(1)}, bf16[2,512,768]{2,1,0:T(8,128)(2,1)}, u32[]{:S(2)}) copy-start(bf16[2,512,768]{2,1,0:T(8,128)(2,1)} %in_ref.3) | copy-start | bytes 4718596
  140.0 27.2 %all-to-all-start.4 = ((bf16[4,48,640]{2,1,0:T(8,128)(2,1)}), bf16[4,48,640]{2,1,0:T(8,128)(2,1)S(1)}, u32[]{:S(2)}, u32[]{:S(2)}) async-start(bf16[4,48,640]{2,1,0:T(8,128)(2,1)} %add_parts.1), calls=%async_computation.4 | async-start | bytes 491520 | tf_op jit(solution)/shard_map/all_to_all | solution.py:358
  168.0 16.1 %all-to-all-start.5 = ((bf16[16,24,128]{2,1,0:T(8,128)(2,1)}), bf16[16,24,128]{2,1,0:T(8,128)(2,1)S(1)}, u32[]{:S(2)}, u32[]{:S(2)}) async-start(bf16[16,24,128]{2,1,0:T(8,128)(2,1)} %split.1), calls=%async_computation.5 | async-start | bytes 196608 | tf_op jit(solution)/shard_map/all_to_all | solution.py:360
  174.2 1.5 copy-start.3
  175.6 1.4 copy-start.5

commit v5 on v4

v5 whole, which is shorter than its diff:
```python
import functools

import jax
import jax.numpy as jnp
from jax import lax
from jax.experimental import pallas as pl
from jax.experimental.pallas import tpu as pltpu
from jax.sharding import Mesh
from jax.sharding import PartitionSpec as P

LANES = 128
X_PARTS, Y_PARTS, Z_PARTS, CORES = 4, 2, 4, 2
MIB = 1024 * 1024

EPSILON = 1e-06
GELU_SCALE = 0.7978845608028654
GELU_CUBIC = 0.044715


def gelu_tanh(values):
    return (
        0.5
        * values
        * (1.0 + jnp.tanh(GELU_SCALE * (values + GELU_CUBIC * values * values * values)))
    )


def gelu_slope(values):
    tangent = jnp.tanh(GELU_SCALE * (values + GELU_CUBIC * values * values * values))
    return 0.5 * (1.0 + tangent) + 0.5 * values * (1.0 - tangent * tangent) * GELU_SCALE * (
        1.0 + 3.0 * GELU_CUBIC * values * values
    )


def dot(left, right, left_dim, right_dim):
    return lax.dot_general(
        left, right, (((left_dim,), (right_dim,)), ((), ())), preferred_element_type=jnp.float32
    )


def normalize(values):
    floats = values.astype(jnp.float32)
    row_scale = lax.rsqrt(jnp.mean(floats * floats, axis=-1, keepdims=True) + EPSILON)
    return floats * row_scale, row_scale


def params(mib):
    return pltpu.CompilerParams(vmem_limit_bytes=mib * MIB)


def struct(shape, dtype):
    return jax.ShapeDtypeStruct(shape, dtype)


def cost(flops, nbytes):
    return pl.CostEstimate(flops=flops, bytes_accessed=nbytes, transcendentals=0)


ANYWHERE = pl.BlockSpec(memory_space=pl.ANY)
IN_VMEM = pl.BlockSpec(memory_space=pltpu.VMEM)
IN_HBM = pl.BlockSpec(memory_space=pltpu.HBM)
IN_SMEM = pl.BlockSpec(memory_space=pltpu.SMEM)


def in_hbm(array):
    return pltpu.with_memory_space_constraint(array, pltpu.HBM)


def once_kernel(in_ref, *refs):
    refs[-1][...] = in_ref[...]


def once(array, *after):
    return pl.pallas_call(
        once_kernel,
        in_specs=[IN_VMEM] + [ANYWHERE] * len(after),
        out_shape=struct(array.shape, array.dtype),
        compiler_params=params(8),
        cost_estimate=cost(0, 4 * array.size),
        name="once",
    )(array, *after)


def held(stage, *args):
    def blank(*args):
        return jnp.zeros(out.shape, out.dtype)

    out = jax.eval_shape(stage, *args)
    return lax.cond(lax.axis_index("x") < X_PARTS, stage, blank, *args)


def pack_kernel(conv_ref, point_ref, out_ref):
    taps, c_part, f_part = conv_ref.shape
    pieces = [conv_ref[tap].astype(jnp.float32) for tap in range(taps)]
    pieces.append(point_ref[...].astype(jnp.float32).T)
    pieces.append(jnp.zeros((c_part, LANES - (taps + 1) * f_part), jnp.float32))
    packed = jnp.concatenate(pieces, axis=1).astype(out_ref.dtype)
    out_ref[...] = jnp.broadcast_to(packed[None], out_ref.shape)


def pack(conv_weight, point_weight, peers):
    c_part = conv_weight.shape[1]
    return pl.pallas_call(
        pack_kernel,
        out_shape=struct((peers, c_part, LANES), conv_weight.dtype),
        compiler_params=params(8),
        cost_estimate=cost(0, 2 * peers * c_part * LANES),
        name="pack",
    )(conv_weight, point_weight)


def assemble_kernel(f_part, taps, in_ref, out_ref):
    blocks = in_ref.shape[0] // Y_PARTS
    for low in range(Y_PARTS):
        pieces = [in_ref[Y_PARTS * block + low].astype(jnp.float32) for block in range(blocks)]
        rows = jnp.concatenate(
            [
                piece[:, tap * f_part : (tap + 1) * f_part]
                for tap in range(taps)
                for piece in pieces
            ],
            axis=1,
        )
        span = rows.shape[0]
        for copy in range(Z_PARTS):
            out_ref[copy, pl.ds(low * span, span), :] = rows.astype(out_ref.dtype)


def assemble(gathered, f_part, taps):
    peers, c_part, _ = gathered.shape
    lanes = peers // Y_PARTS * taps * f_part
    return pl.pallas_call(
        functools.partial(assemble_kernel, f_part, taps),
        out_shape=struct((Z_PARTS, Y_PARTS * c_part, lanes), gathered.dtype),
        compiler_params=params(8),
        cost_estimate=cost(0, 4 * gathered.size * 2),
        name="assemble",
    )(gathered)


def by_channel_kernel(f_part, in_ref, out_ref):
    peers, taps, _, width = in_ref.shape
    depth, c_part = out_ref.shape[0], out_ref.shape[3]
    total = [sum(in_ref[p, tap].astype(jnp.float32) for p in range(peers)) for tap in range(taps)]
    blank = jnp.zeros((LANES - taps * f_part, width), jnp.float32)
    for y in range(Y_PARTS):
        rows = [t[y * f_part : (y + 1) * f_part] for t in total] + [blank]
        turned = jnp.concatenate(rows, axis=0).T.reshape(depth, Y_PARTS, c_part, LANES)
        for low in range(Y_PARTS):
            out_ref[:, y, low] = turned[:, low].astype(out_ref.dtype)


def by_channel(parts, f_part, depth):
    c_part = parts.shape[3] // (depth * Y_PARTS)
    return pl.pallas_call(
        functools.partial(by_channel_kernel, f_part),
        out_shape=struct((depth, Y_PARTS, Y_PARTS, c_part, LANES), parts.dtype),
        compiler_params=params(16),
        cost_estimate=cost(0, 4 * parts.size),
        name="by_channel",
    )(parts)


def add_kernel(in_ref, out_ref):
    total = sum(in_ref[p].astype(jnp.float32) for p in range(in_ref.shape[0]))
    out_ref[...] = total.astype(out_ref.dtype)


def add_parts(parts):
    return pl.pallas_call(
        add_kernel,
        out_shape=struct(parts.shape[1:], parts.dtype),
        compiler_params=params(8),
        cost_estimate=cost(0, 4 * parts.size),
        name="add_parts",
    )(parts)


def finish_kernel(in_ref, _, out_ref):
    taps, _, f_part = out_ref.shape
    total = sum(in_ref[p].astype(jnp.float32) for p in range(in_ref.shape[0]))
    for tap in range(taps):
        out_ref[tap] = total[:, tap * f_part : (tap + 1) * f_part]


def finish(pieces, taps, f_part, after):
    return pl.pallas_call(
        finish_kernel,
        in_specs=[IN_VMEM, ANYWHERE],
        out_shape=struct((taps, pieces.shape[1], f_part), jnp.float32),
        compiler_params=params(8),
        cost_estimate=cost(0, 4 * pieces.size),
        name="finish",
    )(pieces, after)


def act_kernel(in_ref, _, *out_refs):
    for sample, out_ref in enumerate(out_refs):
        normed, _ = normalize(in_ref[sample])
        out_ref[...] = gelu_tanh(normed).astype(out_ref.dtype)


def activate(inputs, block, after):
    samples, bins, width = inputs.shape
    return pl.pallas_call(
        act_kernel,
        grid=(bins // block,),
        in_specs=[pl.BlockSpec((samples, block, width), lambda i: (0, i, 0)), ANYWHERE],
        out_specs=[pl.BlockSpec((block, width), lambda i: (i, 0))] * samples,
        out_shape=[struct((bins, width), inputs.dtype)] * samples,
        compiler_params=params(8),
        cost_estimate=cost(20 * inputs.size, 4 * inputs.size),
        name="activate",
    )(inputs, after)


def roles(yh):
    return (2 * yh, 1, 2 - 2 * yh)


def join_weights(sides, joined, point, yh, zl):
    for side, refs in enumerate(sides):
        for low, ref in enumerate(refs):
            pairs, far, span, lanes = ref.shape
            near, half = 2 * pairs, lanes // 4
            columns = slice(side * half, (side + 1) * half)
            for high in range(pairs):
                for zh in range(far):
                    first = (zh * near + (zl ^ (2 * high + low))) * span
                    rows = pl.ds(pl.multiple_of(first, span), span)
                    block = ref[high, zh]
                    for tap, role in enumerate(roles(yh)):
                        joined[role, rows, columns] = block[:, tap * half : (tap + 1) * half]
                    if point is not None:
                        point[rows, columns] = block[:, 3 * half :]


def forward_kernel(scale, samples, at_ref, *refs):
    count = 3 * samples + 1
    far_refs, refs = refs[: count + 4], refs[count + 4 :]
    pre_ref, own_out, other_out, acts, cot, packed, weights, point, turned, sems = refs
    _, bins, width = cot.shape
    half = weights.shape[2] // CORES
    near_refs = [acts.at[i] for i in range(3 * samples)] + [cot] + [packed.at[i] for i in range(4)]
    copies = [
        pltpu.make_async_copy(far_ref, near_ref, sems.at[i])
        for i, (far_ref, near_ref) in enumerate(zip(far_refs, near_refs))
    ]
    for copy in copies[count:]:
        copy.start()
    for sample in range(samples):
        for role in range(3):
            copies[role * samples + sample].start()
        if sample == 0:
            copies[count - 1].start()
    for copy in copies[count:]:
        copy.wait()
    sides = [[packed.at[2 * side + low] for low in range(2)] for side in range(CORES)]
    join_weights(sides, weights, point, at_ref[0], at_ref[1])
    for sample in range(samples):
        for role in range(3):
            copies[role * samples + sample].wait()
        if sample == 0:
            copies[count - 1].wait()
        handed, mid, partner = [acts[role * samples + sample] for role in range(3)]
        shifted = dot(handed, weights[0], 1, 0).astype(jnp.bfloat16).astype(jnp.float32)
        shifted += dot(partner, weights[2], 1, 0).astype(jnp.bfloat16).astype(jnp.float32)
        preact = shifted + dot(mid, weights[1], 1, 0)
        grad_inner = dot(cot[sample], point[...], 1, 0)
        grad_pre = grad_inner * gelu_slope(preact)
        pre_ref[sample] = grad_pre.astype(jnp.bfloat16)
        turned[sample] = grad_pre.T.astype(jnp.bfloat16)
    for role, tap in enumerate(roles(at_ref[0])):
        term = sum(
            dot(turned[sample], acts[role * samples + sample], 1, 0) for sample in range(samples)
        )
        term = term * scale
        own_out[:, tap] = term[:half].reshape(own_out.shape[0], -1, width)
        other = term[half:].astype(jnp.bfloat16)
        other_out[:, tap] = other.reshape(other_out.shape[0], -1, width)


def forward(at, acts, cotangent, own_w, other_w, scale):
    samples, bins, width = cotangent.shape
    hidden = CORES * own_w[0].shape[3] // 4
    half = (X_PARTS, 3, hidden // CORES // X_PARTS, width)
    count = 3 * samples
    return pl.pallas_call(
        functools.partial(forward_kernel, scale, samples),
        in_specs=[IN_SMEM] + [IN_HBM] * (count + 5),
        out_specs=[IN_VMEM] * 3,
        out_shape=[
            struct((samples, bins, hidden), jnp.bfloat16),
            struct(half, jnp.float32),
            struct(half, jnp.bfloat16),
        ],
        scratch_shapes=[
            pltpu.VMEM((count, bins, width), jnp.bfloat16),
            pltpu.VMEM(cotangent.shape, jnp.bfloat16),
            pltpu.VMEM((4,) + own_w[0].shape, jnp.bfloat16),
            pltpu.VMEM((3, width, hidden), jnp.bfloat16),
            pltpu.VMEM((width, hidden), jnp.bfloat16),
            pltpu.VMEM((samples, hidden, bins), jnp.bfloat16),
            pltpu.SemaphoreType.DMA((count + 5,)),
        ],
        compiler_params=params(30),
        cost_estimate=cost(14 * samples * bins * width * hidden, 16 * samples * bins * width),
        name="forward",
    )(at, *[in_hbm(array) for array in (*acts, cotangent)], *own_w, *other_w)


def backward_kernel(at_ref, in_ref, cot_ref, partner_ref, pre_ref, handed_ref, *refs):
    packed, (out_ref, token_ref, weights) = refs[:4], refs[4:]

    @pl.when(pl.program_id(0) == 0)
    def _():
        join_weights((packed[:2], packed[2:]), weights, None, at_ref[0], at_ref[1])
        token_ref[...] = jnp.zeros_like(token_ref)

    for sample in range(in_ref.shape[0]):
        grad_act = (
            dot(partner_ref[sample], weights[0], 1, 1)
            + dot(pre_ref[sample], weights[1], 1, 1)
            + dot(handed_ref[sample], weights[2], 1, 1)
        )
        normed, row_scale = normalize(in_ref[sample])
        grad_norm = grad_act * gelu_slope(normed)
        center = jnp.mean(grad_norm * normed, axis=-1, keepdims=True)
        grad = cot_ref[sample].astype(jnp.float32) + row_scale * (grad_norm - normed * center)
        out_ref[sample] = grad.astype(out_ref.dtype)


def backward(at, inputs, cotangent, partner, grad_pre, handed, packed, block):
    samples, bins, width = inputs.shape
    hidden = grad_pre.shape[2]
    wide = pl.BlockSpec((samples, block, width), lambda i: (0, i, 0))
    narrow = pl.BlockSpec((samples, block, hidden), lambda i: (0, i, 0))
    whole = pl.BlockSpec(
        packed[0].shape, lambda i: (0, 0, 0, 0), pipeline_mode=pl.Buffered(1)
    )
    return pl.pallas_call(
        backward_kernel,
        grid=(bins // block,),
        in_specs=[IN_SMEM, wide, wide, narrow, narrow, narrow] + [whole] * 4,
        out_specs=[wide, pl.BlockSpec((8, LANES), lambda i: (0, 0))],
        out_shape=[struct(inputs.shape, inputs.dtype), struct((8, LANES), jnp.float32)],
        scratch_shapes=[pltpu.VMEM((3, width, hidden), jnp.bfloat16)],
        compiler_params=params(24),
        cost_estimate=cost(6 * samples * bins * width * hidden, 16 * samples * bins * width),
        name="backward",
    )(
        at,
        in_hbm(inputs),
        in_hbm(cotangent),
        partner,
        grad_pre,
        handed,
        *packed,
    )


def exchanged(array):
    return lax.ppermute(array, "yh", [(0, 1), (1, 0)])


def handed_on(array):
    lower = [(Y_PARTS * i, Y_PARTS * (i + 1)) for i in range(X_PARTS - 1)]
    higher = [(Y_PARTS * (i + 1) + 1, Y_PARTS * i + 1) for i in range(X_PARTS - 1)]
    return lax.ppermute(array, ("x", "yh"), lower + higher)


def z_pair(array, bit):
    near = lax.axis_size("zl")
    return lax.ppermute(array, "zl", [(i, i ^ bit) for i in range(near)])


def other_core(array):
    return lax.ppermute(array, "core", [(0, 1), (1, 0)])


def body(inputs, conv_weight, point_weight, cotangent):
    samples, bins, width = inputs.shape
    taps, c_part, f_part = conv_weight.shape
    near, far = lax.axis_size("zl"), lax.axis_size("zh")
    depth = near * far
    blocks = X_PARTS * Y_PARTS
    devices = depth * Y_PARTS * blocks * CORES
    grad_scale = float(samples * bins * devices) ** (-0.5)
    at = jnp.stack([lax.axis_index("yh"), lax.axis_index("zl")]).astype(jnp.int32)

    packed = pack(conv_weight, point_weight, blocks * Y_PARTS)
    pieces = lax.all_to_all(packed, ("x", "yh", "yl"), 0, 0)

    mids = list(activate(inputs, 256, pieces))
    partners = [exchanged(mid) for mid in mids]

    part = lax.all_to_all(assemble(pieces, f_part, taps + 1)[:far], "zh", 0, 0)
    part = once(part, partners[0])
    handed = [handed_on(partners[0])]
    two = once(jnp.stack([part, z_pair(part, 2)]), handed[0], partners[1])
    handed.append(handed_on(partners[1]))
    other_two = other_core(two)
    last = once(z_pair(two, 1), handed[1])

    packed = (two, last, other_two, other_core(last))

    grad_pre, own, other = forward(
        at, handed + mids + partners, cotangent, packed[:2], packed[2:], grad_scale
    )

    def first_sums(own, other):
        pair = own + other_core(other).astype(jnp.float32)
        return lax.all_to_all(pair.astype(jnp.bfloat16), "x", 0, 0)

    def second_sums(part):
        return lax.all_to_all(part, ("zh", "zl"), 0, 0)

    grad_partner = exchanged(grad_pre)
    parts = held(first_sums, own, other)
    grad_handed = handed_on(once(grad_partner, parts))
    parts = held(second_sums, by_channel(parts, f_part, depth))
    sums = add_parts(parts.reshape(depth, Y_PARTS * Y_PARTS, c_part, LANES))
    pieces = lax.all_to_all(sums, ("yh", "yl"), 0, 0)

    input_grad, token = backward(
        at, inputs, cotangent, grad_partner, grad_pre, grad_handed, packed, 256
    )
    return (input_grad, finish(pieces, taps, f_part, token))


def solution(mesh):
    depth = mesh.shape["dp"] // Y_PARTS
    fine = Mesh(
        mesh.devices.reshape(depth // Z_PARTS, Z_PARTS, Y_PARTS, X_PARTS, Y_PARTS, CORES),
        ("zh", "zl", "yl", "x", "yh", "core"),
    )
    dp, seq = ("zh", "zl", "yl"), ("x", "yh", "core")
    return jax.shard_map(
        body,
        mesh=fine,
        in_specs=(P(dp, seq, None), P(None, dp, seq), P(seq, dp), P(dp, seq, None)),
        out_specs=(P(dp, seq, None), P(None, dp, seq)),
        check_vma=False,
    )
```

time: 186 us -> 189 us (1.016)
  the two profiles are of different devices: /device:TPU:2 before, /device:TPU:8 now
where the time goes in v5:
time: 189 us; the launch traced here: 187 us
  blocking collectives  60.2 us (32%)
  starting transfers between devices  54.2 us (29%)
  waiting for transfers between devices  34.9 us (18%)
  Pallas kernels  25.9 us (14%)
  local copies, waits for them, and re-layouts  9.34 us (5%)
    all_to_all x1, blocking collectives, second_sums(): return lax.all_to_all(part, ('zh', 'zl'), 0, 0)  28.5 us
    ppermute x2, waiting for transfers between devices, z_pair(): return lax.ppermute(array, 'zl', [(i, i ^ bit) for i in range(near)])  20.6 us
    all_to_all x1, blocking collectives, first_sums(): return lax.all_to_all(pair.astype(jnp.bfloat16), 'x', 0, 0)  17.1 us
    all_to_all x1, blocking collectives, body(): pieces = lax.all_to_all(packed, ('x', 'yh', 'yl'), 0, 0)  14.6 us
    all_to_all x1, starting transfers between devices, body(): part = lax.all_to_all(assemble(pieces, f_part, taps + 1)[:far], 'zh', 0, 0)  14 us
    ppermute x3, starting transfers between devices, exchanged(): return lax.ppermute(array, 'yh', [(0, 1), (1, 0)])  11.2 us
    pallas_call x1, Pallas kernels, forward(): pl.pallas_call(functools.partial(forward_kernel, scale, samples), in_spec...  10.7 us
    all_to_all x1, waiting for transfers between devices, body(): part = lax.all_to_all(assemble(pieces, f_part, taps + 1)[:far], 'zh', 0, 0)  9.87 us
  transfers between devices with their start and end apart: 13, of which 5 were waited for; matrix products, arithmetic and copies ran while one was open for 1% of the time, Pallas kernels for 6%

profile of v5, /device:TPU:8, one launch (start us, length us, event | category | flops | bytes accessed | tf_op | source)
XLA Modules:
  0.0 187.4 jit_solution(17347410759637212494)
XLA Ops:
  2.2 14.6 %all_to_all.25._.in_ref = bf16[16,24,128]{2,1,0:T(8,128)(2,1)S(1)} all-to-all(bf16[16,24,128]{2,1,0:T(8,128)(2,1)S(1)} %pack.1), channel_id=1, replica_groups=mesh['zh'=4,'zl'=4,'yl'=2,'x'=4,'yh'=2,'core'=2] {'x','yh','yl'}, dimensions={0} | all-to-all | bytes 196608 | tf_op jit(solution)/shard_map/all_to_all | solution.py:392
  20.7 3.5 %collective-permute-start.1 = (bf16[512,768]{1,0:T(8,128)(2,1)S(1)}, bf16[512,768]{1,0:T(8,128)(2,1)S(1)}, u32[]{:S(2)}, u32[]{:S(2)}) collective-permute-start(bf16[512,768]{1,0:T(8,128)(2,1)S(1)} %get-tuple-element.22.refs_2_), channel_id=1, source_target_pairs={{0,2},{2,0},{1,3},{3,1},{4,6},{6,4},{5,7},{7,5},{8,10},{10,8},{9,1... | collective-permute-start | bytes 2359304 | tf_op jit(solution)/shard_map/ppermute | solution.py:363
  25.1 14.0 %all-to-all-start.3 = ((bf16[4,48,768]{2,1,0:T(8,128)(2,1)}), bf16[4,48,768]{2,1,0:T(8,128)(2,1)S(1)}, u32[]{:S(2)}, u32[]{:S(2)}) async-start(bf16[4,48,768]{2,1,0:T(8,128)(2,1)} %assemble.1), calls=%async_computation.3 | async-start | bytes 589824 | tf_op jit(solution)/shard_map/all_to_all | solution.py:397
  39.1 3.8 %collective-permute-start.3 = (bf16[512,768]{1,0:T(8,128)(2,1)}, bf16[512,768]{1,0:T(8,128)(2,1)S(1)}, u32[]{:S(2)}, u32[]{:S(2)}) collective-permute-start(bf16[512,768]{1,0:T(8,128)(2,1)} %copy-done.14), channel_id=1, source_target_pairs={{0,2},{2,0},{1,3},{3,1},{4,6},{6,4},{5,7},{7,5},{8,10},{10,8},{9,1... | collective-permute-start | bytes 2359304 | tf_op jit(solution)/shard_map/ppermute | solution.py:363
  42.9 2.5 %collective-permute-start.2 = (bf16[512,768]{1,0:T(8,128)(2,1)S(1)}, bf16[512,768]{1,0:T(8,128)(2,1)S(1)}, u32[]{:S(2)}, u32[]{:S(2)}) collective-permute-start(bf16[512,768]{1,0:T(8,128)(2,1)S(1)} %collective-permute-done.1.refs_0_.refs_4_), channel_id=1, source_target_pairs={{0,4},{4,8},{8,12},{6,2},{10,6},{14,10},{1,5},{5,9},{9,13},{7,3},{... | collective-permute-start | bytes 2359304 | tf_op jit(solution)/shard_map/ppermute | solution.py:369
  45.4 9.9 %all-to-all-done.3.in_ref = bf16[4,48,768]{2,1,0:T(8,128)(2,1)S(1)} async-done(((bf16[4,48,768]{2,1,0:T(8,128)(2,1)}), bf16[4,48,768]{2,1,0:T(8,128)(2,1)S(1)}, u32[]{:S(2)}, u32[]{:S(2)}) %all-to-all-start.3) | async-done | bytes 294944 | tf_op jit(solution)/shard_map/all_to_all | solution.py:397
  55.3 7.5 %collective-permute-start.5 = (bf16[4,48,768]{2,1,0:T(8,128)(2,1)S(1)}, bf16[4,48,768]{2,1,0:T(8,128)(2,1)S(1)}, u32[]{:S(2)}, u32[]{:S(2)}) collective-permute-start(bf16[4,48,768]{2,1,0:T(8,128)(2,1)S(1)} %once.4), channel_id=1, source_target_pairs={{0,64},{32,96},{64,0},{96,32},{1,65},{33,97},{65,1},{97,33},{2,66}... | collective-permute-start | bytes 884744 | tf_op jit(solution)/shard_map/ppermute | solution.py:374
  62.8 2.5 %collective-permute-start.4 = (bf16[512,768]{1,0:T(8,128)(2,1)S(1)}, bf16[512,768]{1,0:T(8,128)(2,1)S(1)}, u32[]{:S(2)}, u32[]{:S(2)}) collective-permute-start(bf16[512,768]{1,0:T(8,128)(2,1)S(1)} %collective-permute-done.3.refs_1_.refs_5_), channel_id=1, source_target_pairs={{0,4},{4,8},{8,12},{6,2},{10,6},{14,10},{1,5},{5,9},{9,13},{7,3},{... | collective-permute-start | bytes 2359304 | tf_op jit(solution)/shard_map/ppermute | solution.py:369
  65.3 9.0 %collective-permute-done.5 = bf16[4,48,768]{2,1,0:T(8,128)(2,1)S(1)} collective-permute-done((bf16[4,48,768]{2,1,0:T(8,128)(2,1)S(1)}, bf16[4,48,768]{2,1,0:T(8,128)(2,1)S(1)}, u32[]{:S(2)}, u32[]{:S(2)}) %collective-permute-start.5) | collective-permute-done | bytes 294944 | tf_op jit(solution)/shard_map/ppermute | solution.py:374
  76.4 1.9 %collective-permute-start.6 = (bf16[2,4,48,768]{3,2,1,0:T(8,128)(2,1)S(1)}, bf16[2,4,48,768]{3,2,1,0:T(8,128)(2,1)S(1)}, u32[]{:S(2)}, u32[]{:S(2)}) collective-permute-start(bf16[2,4,48,768]{3,2,1,0:T(8,128)(2,1)S(1)} %once.5.refs_7_.refs_0_), channel_id=1, source_target_pairs={{0,32},{32,0},{64,96},{96,64},{1,33},{33,1},{65,97},{97,65},{2,34}... | collective-permute-start | bytes 1769480 | tf_op jit(solution)/shard_map/ppermute | solution.py:374
  78.4 1.9 %collective-permute-start.7 = (bf16[2,4,48,768]{3,2,1,0:T(8,128)(2,1)S(1)}, bf16[2,4,48,768]{3,2,1,0:T(8,128)(2,1)S(1)}, u32[]{:S(2)}, u32[]{:S(2)}) collective-permute-start(bf16[2,4,48,768]{3,2,1,0:T(8,128)(2,1)S(1)} %once.5.refs_7_.refs_0_), channel_id=1, source_target_pairs={{0,1},{1,0},{2,3},{3,2},{4,5},{5,4},{6,7},{7,6},{8,9},{9,8},{10,11... | collective-permute-start | bytes 1769480 | tf_op jit(solution)/shard_map/ppermute | solution.py:378
  80.3 11.6 %collective-permute-done.6.in_ref = bf16[2,4,48,768]{3,2,1,0:T(8,128)(2,1)S(1)} collective-permute-done((bf16[2,4,48,768]{3,2,1,0:T(8,128)(2,1)S(1)}, bf16[2,4,48,768]{3,2,1,0:T(8,128)(2,1)S(1)}, u32[]{:S(2)}, u32[]{:S(2)}) %collective-permute-start.6) | collective-permute-done | bytes 589856 | tf_op jit(solution)/shard_map/ppermute | solution.py:374
  92.8 1.9 %collective-permute-start.8 = (bf16[2,4,48,768]{3,2,1,0:T(8,128)(2,1)S(1)}, bf16[2,4,48,768]{3,2,1,0:T(8,128)(2,1)S(1)}, u32[]{:S(2)}, u32[]{:S(2)}) collective-permute-start(bf16[2,4,48,768]{3,2,1,0:T(8,128)(2,1)S(1)} %once.6.refs_8_.refs_1_), channel_id=1, source_target_pairs={{0,1},{1,0},{2,3},{3,2},{4,5},{5,4},{6,7},{7,6},{8,9},{9,8},{10,11... | collective-permute-start | bytes 1769480 | tf_op jit(solution)/shard_map/ppermute | solution.py:378
  96.7 10.7 %forward.1 = (bf16[2,512,384]{2,1,0:T(8,128)(2,1)S(1)}, f32[4,3,48,768]{3,2,1,0:T(8,128)}, bf16[4,3,48,768]{3,2,1,0:T(8,128)(2,1)}) custom-call(s32[2]{0:T(128)S(1)} %pad_add_fusion.at_ref, bf16[512,768]{1,0:T(8,128)(2,1)} %copy-done.3, bf16[512,768]{1,0:T(8,128)(2,1)} %copy-done.5, bf16[512,768]{1,0:T(8,128)(2,1)} %copy-done.13, ...), custom_call_target="tpu_custom_call" | custom-call | flops 4227858432 | bytes 12582912 | tf_op jit(solution)/shard_map/forward/pallas_call | solution.py:288
  107.4 3.9 %collective-permute-start.9 = (bf16[2,512,384]{2,1,0:T(8,128)(2,1)S(1)}, bf16[2,512,384]{2,1,0:T(8,128)(2,1)S(1)}, u32[]{:S(2)}, u32[]{:S(2)}) collective-permute-start(bf16[2,512,384]{2,1,0:T(8,128)(2,1)S(1)} %get-tuple-element.24.pre_ref), channel_id=1, source_target_pairs={{0,2},{2,0},{1,3},{3,1},{4,6},{6,4},{5,7},{7,5},{8,10},{10,8},{9,1... | collective-permute-start | bytes 2359304 | tf_op jit(solution)/shard_map/ppermute | solution.py:363
  111.3 23.3 %conditional.2 = (bf16[4,3,48,768]{3,2,1,0:T(8,128)(2,1)}) conditional(s32[]{:T(128)} %convert_element_type.10, () %tuple.20, (bf16[4,3,48,768]{3,2,1,0:T(8,128)(2,1)}, f32[4,3,48,768]{3,2,1,0:T(8,128)}) %tuple.21), branch_computations={%region_0.0_spmd, %region_1.0_spmd} | conditional | flops 1327104 | bytes 8847408 | solution.py:89
  111.3 1.9 %collective-permute-start = (bf16[4,3,48,768]{3,2,1,0:T(8,128)(2,1)}, bf16[4,3,48,768]{3,2,1,0:T(8,128)(2,1)S(1)}, u32[]{:S(2)}, u32[]{:S(2)}) collective-permute-start(bf16[4,3,48,768]{3,2,1,0:T(8,128)(2,1)} %get-tuple-element.12), channel_id=1, source_target_pairs={{0,1},{1,0},{2,3},{3,2},{4,5},{5,4},{6,7},{7,6},{8,9},{9,8},{10,11... | collective-permute-start | bytes 2654216 | tf_op jit(solution)/shard_map/cond/branch_1_fun/ppermute | solution.py:378
  113.2 2.6 %collective-permute-done = bf16[4,3,48,768]{3,2,1,0:T(8,128)(2,1)S(1)} collective-permute-done((bf16[4,3,48,768]{3,2,1,0:T(8,128)(2,1)}, bf16[4,3,48,768]{3,2,1,0:T(8,128)(2,1)S(1)}, u32[]{:S(2)}, u32[]{:S(2)}) %collective-permute-start) | collective-permute-done | bytes 884768 | tf_op jit(solution)/shard_map/cond/branch_1_fun/ppermute | solution.py:378
  117.5 17.1 %all_to_all.23 = bf16[4,3,48,768]{3,2,1,0:T(8,128)(2,1)} all-to-all(bf16[4,3,48,768]{3,2,1,0:T(8,128)(2,1)S(1)} %add_convert_fusion), channel_id=1, replica_groups=mesh['zh'=4,'zl'=4,'yl'=2,'x'=4,'yh'=2,'core'=2] {'x'}, dimensions={0} | all-to-all | bytes 1769472 | tf_op jit(solution)/shard_map/cond/branch_1_fun/all_to_all | solution.py:413
  134.7 3.5 %collective-permute-start.10 = (bf16[2,512,384]{2,1,0:T(8,128)(2,1)S(1)}, bf16[2,512,384]{2,1,0:T(8,128)(2,1)}, u32[]{:S(2)}, u32[]{:S(2)}) collective-permute-start(bf16[2,512,384]{2,1,0:T(8,128)(2,1)S(1)} %once.7), channel_id=1, source_target_pairs={{0,4},{4,8},{8,12},{6,2},{10,6},{14,10},{1,5},{5,9},{9,13},{7,3},{... | collective-permute-start | bytes 2359304 | tf_op jit(solution)/shard_map/ppermute | solution.py:369
  139.1 28.5 %conditional.3 = (bf16[16,2,2,24,128]{4,3,2,1,0:T(8,128)(2,1)}) conditional(s32[]{:T(128)} %convert_element_type.10, () %tuple.22, bf16[16,2,2,24,128]{4,3,2,1,0:T(8,128)(2,1)} %by_channel.1), branch_computations={%region_2.0_spmd, %region_3.0_spmd} | conditional | bytes 786440 | solution.py:89
  139.1 28.5 %all_to_all.24 = bf16[16,2,2,24,128]{4,3,2,1,0:T(8,128)(2,1)} all-to-all(bf16[16,2,2,24,128]{4,3,2,1,0:T(8,128)(2,1)} %param.3), channel_id=1, replica_groups=mesh['zh'=4,'zl'=4,'yl'=2,'x'=4,'yh'=2,'core'=2] {'zh','zl'}, dimensions={0} | all-to-all | bytes 786432 | tf_op jit(solution)/shard_map/cond/branch_1_fun/all_to_all | solution.py:416
  169.3 5.5 %all-to-all-start.4 = ((bf16[4,24,128]{2,1,0:T(8,128)(2,1)}), bf16[4,24,128]{2,1,0:T(8,128)(2,1)}, u32[]{:S(2)}, u32[]{:S(2)}) async-start(bf16[4,24,128]{2,1,0:T(8,128)(2,1)} %copy-done.10), calls=%async_computation.4 | async-start | bytes 49152 | tf_op jit(solution)/shard_map/all_to_all | solution.py:423
  177.0 9.0 %backward.1 = (bf16[2,512,768]{2,1,0:T(8,128)(2,1)}, f32[8,128]{1,0:T(8,128)S(1)}) custom-call(s32[2]{0:T(128)S(1)} %pad_add_fusion.at_ref, bf16[2,512,768]{2,1,0:T(8,128)(2,1)} %in_ref.3, bf16[2,512,768]{2,1,0:T(8,128)(2,1)} %cot_ref.1, bf16[2,512,384]{2,1,0:T(8,128)(2,1)S(1)} %collective-permute-done.9.in_ref.partner_ref, ...), custom_call_target="tpu_custom_call" | custom-call | flops 1811939328 | bytes 12582912 | tf_op jit(solution)/shard_map/backward/pallas_call | solution.py:341
  (54 shorter events, 19.3 us)
Async XLA Ops:
  16.8 1.4 copy-start
  20.7 22.2 %copy-start.13 = (bf16[512,768]{1,0:T(8,128)(2,1)}, bf16[512,768]{1,0:T(8,128)(2,1)S(1)}, u32[]{:S(2)}) copy-start(bf16[512,768]{1,0:T(8,128)(2,1)S(1)} %get-tuple-element.22.refs_2_) | copy-start | bytes 2359300
  20.7 22.2 %collective-permute-start.1 = (bf16[512,768]{1,0:T(8,128)(2,1)S(1)}, bf16[512,768]{1,0:T(8,128)(2,1)S(1)}, u32[]{:S(2)}, u32[]{:S(2)}) collective-permute-start(bf16[512,768]{1,0:T(8,128)(2,1)S(1)} %get-tuple-element.22.refs_2_), channel_id=1, source_target_pairs={{0,2},{2,0},{1,3},{3,1},{4,6},{6,4},{5,7},{7,5},{8,10},{10,8},{9,1... | collective-permute-start | bytes 2359304 | tf_op jit(solution)/shard_map/ppermute | solution.py:363
  25.1 30.2 %all-to-all-start.3 = ((bf16[4,48,768]{2,1,0:T(8,128)(2,1)}), bf16[4,48,768]{2,1,0:T(8,128)(2,1)S(1)}, u32[]{:S(2)}, u32[]{:S(2)}) async-start(bf16[4,48,768]{2,1,0:T(8,128)(2,1)} %assemble.1), calls=%async_computation.3 | async-start | bytes 589824 | tf_op jit(solution)/shard_map/all_to_all | solution.py:397
  39.1 23.7 %collective-permute-start.3 = (bf16[512,768]{1,0:T(8,128)(2,1)}, bf16[512,768]{1,0:T(8,128)(2,1)S(1)}, u32[]{:S(2)}, u32[]{:S(2)}) collective-permute-start(bf16[512,768]{1,0:T(8,128)(2,1)} %copy-done.14), channel_id=1, source_target_pairs={{0,2},{2,0},{1,3},{3,1},{4,6},{6,4},{5,7},{7,5},{8,10},{10,8},{9,1... | collective-permute-start | bytes 2359304 | tf_op jit(solution)/shard_map/ppermute | solution.py:363
  42.9 33.5 %copy-start.1 = (bf16[512,768]{1,0:T(8,128)(2,1)}, bf16[512,768]{1,0:T(8,128)(2,1)S(1)}, u32[]{:S(2)}) copy-start(bf16[512,768]{1,0:T(8,128)(2,1)S(1)} %collective-permute-done.1.refs_0_.refs_4_) | copy-start | bytes 2359300
  42.9 31.4 %collective-permute-start.2 = (bf16[512,768]{1,0:T(8,128)(2,1)S(1)}, bf16[512,768]{1,0:T(8,128)(2,1)S(1)}, u32[]{:S(2)}, u32[]{:S(2)}) collective-permute-start(bf16[512,768]{1,0:T(8,128)(2,1)S(1)} %collective-permute-done.1.refs_0_.refs_4_), channel_id=1, source_target_pairs={{0,4},{4,8},{8,12},{6,2},{10,6},{14,10},{1,5},{5,9},{9,13},{7,3},{... | collective-permute-start | bytes 2359304 | tf_op jit(solution)/shard_map/ppermute | solution.py:369
  55.3 19.0 %collective-permute-start.5 = (bf16[4,48,768]{2,1,0:T(8,128)(2,1)S(1)}, bf16[4,48,768]{2,1,0:T(8,128)(2,1)S(1)}, u32[]{:S(2)}, u32[]{:S(2)}) collective-permute-start(bf16[4,48,768]{2,1,0:T(8,128)(2,1)S(1)} %once.4), channel_id=1, source_target_pairs={{0,64},{32,96},{64,0},{96,32},{1,65},{33,97},{65,1},{97,33},{2,66}... | collective-permute-start | bytes 884744 | tf_op jit(solution)/shard_map/ppermute | solution.py:374
  62.8 13.6 %copy-start.2 = (bf16[512,768]{1,0:T(8,128)(2,1)}, bf16[512,768]{1,0:T(8,128)(2,1)S(1)}, u32[]{:S(2)}) copy-start(bf16[512,768]{1,0:T(8,128)(2,1)S(1)} %collective-permute-done.3.refs_1_.refs_5_) | copy-start | bytes 2359300
  62.8 17.5 %collective-permute-start.4 = (bf16[512,768]{1,0:T(8,128)(2,1)S(1)}, bf16[512,768]{1,0:T(8,128)(2,1)S(1)}, u32[]{:S(2)}, u32[]{:S(2)}) collective-permute-start(bf16[512,768]{1,0:T(8,128)(2,1)S(1)} %collective-permute-done.3.refs_1_.refs_5_), channel_id=1, source_target_pairs={{0,4},{4,8},{8,12},{6,2},{10,6},{14,10},{1,5},{5,9},{9,13},{7,3},{... | collective-permute-start | bytes 2359304 | tf_op jit(solution)/shard_map/ppermute | solution.py:369
  74.3 0.9 copy-start.3
  75.2 1.1 copy-start.4
  76.4 15.4 %collective-permute-start.6 = (bf16[2,4,48,768]{3,2,1,0:T(8,128)(2,1)S(1)}, bf16[2,4,48,768]{3,2,1,0:T(8,128)(2,1)S(1)}, u32[]{:S(2)}, u32[]{:S(2)}) collective-permute-start(bf16[2,4,48,768]{3,2,1,0:T(8,128)(2,1)S(1)} %once.5.refs_7_.refs_0_), channel_id=1, source_target_pairs={{0,32},{32,0},{64,96},{96,64},{1,33},{33,1},{65,97},{97,65},{2,34}... | collective-permute-start | bytes 1769480 | tf_op jit(solution)/shard_map/ppermute | solution.py:374
  78.4 16.4 %collective-permute-start.7 = (bf16[2,4,48,768]{3,2,1,0:T(8,128)(2,1)S(1)}, bf16[2,4,48,768]{3,2,1,0:T(8,128)(2,1)S(1)}, u32[]{:S(2)}, u32[]{:S(2)}) collective-permute-start(bf16[2,4,48,768]{3,2,1,0:T(8,128)(2,1)S(1)} %once.5.refs_7_.refs_0_), channel_id=1, source_target_pairs={{0,1},{1,0},{2,3},{3,2},{4,5},{5,4},{6,7},{7,6},{8,9},{9,8},{10,11... | collective-permute-start | bytes 1769480 | tf_op jit(solution)/shard_map/ppermute | solution.py:378
  92.8 3.9 %collective-permute-start.8 = (bf16[2,4,48,768]{3,2,1,0:T(8,128)(2,1)S(1)}, bf16[2,4,48,768]{3,2,1,0:T(8,128)(2,1)S(1)}, u32[]{:S(2)}, u32[]{:S(2)}) collective-permute-start(bf16[2,4,48,768]{3,2,1,0:T(8,128)(2,1)S(1)} %once.6.refs_8_.refs_1_), channel_id=1, source_target_pairs={{0,1},{1,0},{2,3},{3,2},{4,5},{5,4},{6,7},{7,6},{8,9},{9,8},{10,11... | collective-permute-start | bytes 1769480 | tf_op jit(solution)/shard_map/ppermute | solution.py:378
  94.8 12.6 %copy-start.6 = (bf16[2,4,48,768]{3,2,1,0:T(8,128)(2,1)}, bf16[2,4,48,768]{3,2,1,0:T(8,128)(2,1)S(1)}, u32[]{:S(2)}) copy-start(bf16[2,4,48,768]{3,2,1,0:T(8,128)(2,1)S(1)} %collective-permute-done.7.refs_9_.refs_2_) | copy-start | bytes 1769476
  96.7 10.7 %copy-start.8 = (bf16[2,4,48,768]{3,2,1,0:T(8,128)(2,1)}, bf16[2,4,48,768]{3,2,1,0:T(8,128)(2,1)S(1)}, u32[]{:S(2)}) copy-start(bf16[2,4,48,768]{3,2,1,0:T(8,128)(2,1)S(1)} %collective-permute-done.8.refs_10_.refs_3_) | copy-start | bytes 1769476
  107.4 27.2 %collective-permute-start.9 = (bf16[2,512,384]{2,1,0:T(8,128)(2,1)S(1)}, bf16[2,512,384]{2,1,0:T(8,128)(2,1)S(1)}, u32[]{:S(2)}, u32[]{:S(2)}) collective-permute-start(bf16[2,512,384]{2,1,0:T(8,128)(2,1)S(1)} %get-tuple-element.24.pre_ref), channel_id=1, source_target_pairs={{0,2},{2,0},{1,3},{3,1},{4,6},{6,4},{5,7},{7,5},{8,10},{10,8},{9,1... | collective-permute-start | bytes 2359304 | tf_op jit(solution)/shard_map/ppermute | solution.py:363
  111.3 4.5 %collective-permute-start = (bf16[4,3,48,768]{3,2,1,0:T(8,128)(2,1)}, bf16[4,3,48,768]{3,2,1,0:T(8,128)(2,1)S(1)}, u32[]{:S(2)}, u32[]{:S(2)}) collective-permute-start(bf16[4,3,48,768]{3,2,1,0:T(8,128)(2,1)} %get-tuple-element.12), channel_id=1, source_target_pairs={{0,1},{1,0},{2,3},{3,2},{4,5},{5,4},{6,7},{7,6},{8,9},{9,8},{10,11... | collective-permute-start | bytes 2654216 | tf_op jit(solution)/shard_map/cond/branch_1_fun/ppermute | solution.py:378
  134.6 3.6 %copy-start.15 = (bf16[4,3,48,768]{3,2,1,0:T(8,128)(2,1)S(1)}, bf16[4,3,48,768]{3,2,1,0:T(8,128)(2,1)}, u32[]{:S(2)}) copy-start(bf16[4,3,48,768]{3,2,1,0:T(8,128)(2,1)} %get-tuple-element.29.refs_0_.in_ref) | copy-start | bytes 2654212
  134.7 40.2 %collective-permute-start.10 = (bf16[2,512,384]{2,1,0:T(8,128)(2,1)S(1)}, bf16[2,512,384]{2,1,0:T(8,128)(2,1)}, u32[]{:S(2)}, u32[]{:S(2)}) collective-permute-start(bf16[2,512,384]{2,1,0:T(8,128)(2,1)S(1)} %once.7), channel_id=1, source_target_pairs={{0,4},{4,8},{8,12},{6,2},{10,6},{14,10},{1,5},{5,9},{9,13},{7,3},{... | collective-permute-start | bytes 2359304 | tf_op jit(solution)/shard_map/ppermute | solution.py:369
  169.3 16.7 %all-to-all-start.4 = ((bf16[4,24,128]{2,1,0:T(8,128)(2,1)}), bf16[4,24,128]{2,1,0:T(8,128)(2,1)}, u32[]{:S(2)}, u32[]{:S(2)}) async-start(bf16[4,24,128]{2,1,0:T(8,128)(2,1)} %copy-done.10), calls=%async_computation.4 | async-start | bytes 49152 | tf_op jit(solution)/shard_map/all_to_all | solution.py:423
  174.9 1.1 copy-start.7
  175.9 1.1 copy-start.9
  (5 other events, 3.8 us)

commit v6 on v5

--- a/solution.py
+++ b/solution.py
@@ -138,60 +138,66 @@
     )(gathered)
 
 
-def by_channel_kernel(f_part, in_ref, out_ref):
-    peers, taps, _, width = in_ref.shape
-    depth, c_part = out_ref.shape[0], out_ref.shape[3]
+def by_channel_kernel(in_ref, out_ref):
+    peers, taps, rows, width = in_ref.shape
+    depth, _, c_part, _ = out_ref.shape
     total = [sum(in_ref[p, tap].astype(jnp.float32) for p in range(peers)) for tap in range(taps)]
-    blank = jnp.zeros((LANES - taps * f_part, width), jnp.float32)
-    for y in range(Y_PARTS):
-        rows = [t[y * f_part : (y + 1) * f_part] for t in total] + [blank]
-        turned = jnp.concatenate(rows, axis=0).T.reshape(depth, Y_PARTS, c_part, LANES)
-        for low in range(Y_PARTS):
-            out_ref[:, y, low] = turned[:, low].astype(out_ref.dtype)
-
-
-def by_channel(parts, f_part, depth):
-    c_part = parts.shape[3] // (depth * Y_PARTS)
-    return pl.pallas_call(
-        functools.partial(by_channel_kernel, f_part),
-        out_shape=struct((depth, Y_PARTS, Y_PARTS, c_part, LANES), parts.dtype),
+    turned = jnp.concatenate(total, axis=0).T.reshape(depth, Y_PARTS, c_part, taps * rows)
+    blank = jnp.zeros((depth, c_part, LANES - Y_PARTS * rows), jnp.float32)
+    for tap in range(taps):
+        lanes = slice(tap * rows, (tap + 1) * rows)
+        parts = [turned[:, low, :, lanes] for low in range(Y_PARTS)] + [blank]
+        out_ref[:, tap] = jnp.concatenate(parts, axis=2).astype(out_ref.dtype)
+
+
+def by_channel(parts, depth):
+    taps, c_part = parts.shape[1], parts.shape[3] // (depth * Y_PARTS)
+    return pl.pallas_call(
+        by_channel_kernel,
+        out_shape=struct((depth, taps, c_part, LANES), parts.dtype),
         compiler_params=params(16),
         cost_estimate=cost(0, 4 * parts.size),
         name="by_channel",
     )(parts)
 
 
-def add_kernel(in_ref, out_ref):
-    total = sum(in_ref[p].astype(jnp.float32) for p in range(in_ref.shape[0]))
-    out_ref[...] = total.astype(out_ref.dtype)
-
-
-def add_parts(parts):
-    return pl.pallas_call(
-        add_kernel,
-        out_shape=struct(parts.shape[1:], parts.dtype),
+def add_kernel(f_part, in_ref, _, out_ref):
+    peers, taps, c_part, _ = in_ref.shape
+    total = [sum(in_ref[p, tap].astype(jnp.float32) for p in range(peers)) for tap in range(taps)]
+    blank = jnp.zeros((c_part, LANES - taps * f_part), jnp.float32)
+    for low in range(Y_PARTS):
+        for high in range(Y_PARTS):
+            first = (low * Y_PARTS + high) * f_part
+            parts = [t[:, first : first + f_part] for t in total] + [blank]
+            out_ref[high * Y_PARTS + low] = jnp.concatenate(parts, axis=1).astype(out_ref.dtype)
+
+
+def add_parts(parts, f_part, after):
+    return pl.pallas_call(
+        functools.partial(add_kernel, f_part),
+        in_specs=[IN_VMEM, ANYWHERE],
+        out_shape=struct((Y_PARTS * Y_PARTS,) + parts.shape[2:], parts.dtype),
         compiler_params=params(8),
         cost_estimate=cost(0, 4 * parts.size),
         name="add_parts",
-    )(parts)
-
-
-def finish_kernel(in_ref, _, out_ref):
+    )(parts, after)
+
+
+def finish_kernel(in_ref, out_ref):
     taps, _, f_part = out_ref.shape
     total = sum(in_ref[p].astype(jnp.float32) for p in range(in_ref.shape[0]))
     for tap in range(taps):
         out_ref[tap] = total[:, tap * f_part : (tap + 1) * f_part]
 
 
-def finish(pieces, taps, f_part, after):
+def finish(pieces, taps, f_part):
     return pl.pallas_call(
         finish_kernel,
-        in_specs=[IN_VMEM, ANYWHERE],
         out_shape=struct((taps, pieces.shape[1], f_part), jnp.float32),
         compiler_params=params(8),
         cost_estimate=cost(0, 4 * pieces.size),
         name="finish",
-    )(pieces, after)
+    )(pieces)
 
 
 def act_kernel(in_ref, _, *out_refs):
@@ -412,20 +418,16 @@
         pair = own + other_core(other).astype(jnp.float32)
         return lax.all_to_all(pair.astype(jnp.bfloat16), "x", 0, 0)
 
-    def second_sums(part):
-        return lax.all_to_all(part, ("zh", "zl"), 0, 0)
-
     grad_partner = exchanged(grad_pre)
     parts = held(first_sums, own, other)
     grad_handed = handed_on(once(grad_partner, parts))
-    parts = held(second_sums, by_channel(parts, f_part, depth))
-    sums = add_parts(parts.reshape(depth, Y_PARTS * Y_PARTS, c_part, LANES))
-    pieces = lax.all_to_all(sums, ("yh", "yl"), 0, 0)
-
+    parts = lax.all_to_all(by_channel(parts, depth), ("zh", "zl"), 0, 0)
     input_grad, token = backward(
         at, inputs, cotangent, grad_partner, grad_pre, grad_handed, packed, 256
     )
-    return (input_grad, finish(pieces, taps, f_part, token))
+    sums = add_parts(parts, f_part, token)
+    conv_grad = finish(lax.all_to_all(sums, ("yh", "yl"), 0, 0), taps, f_part)
+    return (input_grad, conv_grad)
 
 
 def solution(mesh):

time: 189 us -> 184 us (0.974)
  the two profiles are of different devices: /device:TPU:8 before, /device:TPU:32 now
where the time goes in v6:
time: 184 us; the launch traced here: 183 us
  starting transfers between devices  53.9 us (29%)
  waiting for transfers between devices  51.8 us (28%)
  blocking collectives  41 us (22%)
  Pallas kernels  25.4 us (14%)
  local copies, waits for them, and re-layouts  7.61 us (4%)
  other arithmetic  1.85 us (1%)
    ppermute x2, waiting for transfers between devices, z_pair(): return lax.ppermute(array, 'zl', [(i, i ^ bit) for i in range(near)])  18 us
    all_to_all x1, blocking collectives, first_sums(): return lax.all_to_all(pair.astype(jnp.bfloat16), 'x', 0, 0)  17 us
    ppermute x3, waiting for transfers between devices, handed_on(): return lax.ppermute(array, ('x', 'yh'), lower + higher)  15.5 us
    all_to_all x1, blocking collectives, body(): pieces = lax.all_to_all(packed, ('x', 'yh', 'yl'), 0, 0)  14.6 us
    all_to_all x1, starting transfers between devices, body(): part = lax.all_to_all(assemble(pieces, f_part, taps + 1)[:far], 'zh', 0, 0)  14.2 us
    all_to_all x1, waiting for transfers between devices, body(): part = lax.all_to_all(assemble(pieces, f_part, taps + 1)[:far], 'zh', 0, 0)  13.9 us
    ppermute x3, starting transfers between devices, exchanged(): return lax.ppermute(array, 'yh', [(0, 1), (1, 0)])  11.5 us
    pallas_call x1, Pallas kernels, forward(): pl.pallas_call(functools.partial(forward_kernel, scale, samples), in_spec...  10.7 us
  transfers between devices with their start and end apart: 13, of which 6 were waited for; matrix products, arithmetic and copies ran while one was open for 1% of the time, Pallas kernels for 7%

profile of v6, /device:TPU:32, one launch (start us, length us, event | category | flops | bytes accessed | tf_op | source)
XLA Modules:
  0.0 182.6 jit_solution(1937518786203386905)
XLA Ops:
  2.2 14.6 %all_to_all.25._.in_ref = bf16[16,24,128]{2,1,0:T(8,128)(2,1)S(1)} all-to-all(bf16[16,24,128]{2,1,0:T(8,128)(2,1)S(1)} %pack.1), channel_id=1, replica_groups=mesh['zh'=4,'zl'=4,'yl'=2,'x'=4,'yh'=2,'core'=2] {'x','yh','yl'}, dimensions={0} | all-to-all | bytes 196608 | tf_op jit(solution)/shard_map/all_to_all | solution.py:398
  19.8 3.4 %collective-permute-start.1 = (bf16[512,768]{1,0:T(8,128)(2,1)S(1)}, bf16[512,768]{1,0:T(8,128)(2,1)S(1)}, u32[]{:S(2)}, u32[]{:S(2)}) collective-permute-start(bf16[512,768]{1,0:T(8,128)(2,1)S(1)} %get-tuple-element.18.refs_2_), channel_id=1, source_target_pairs={{0,2},{2,0},{1,3},{3,1},{4,6},{6,4},{5,7},{7,5},{8,10},{10,8},{9,1... | collective-permute-start | bytes 2359304 | tf_op jit(solution)/shard_map/ppermute | solution.py:369
  24.0 14.2 %all-to-all-start.2 = ((bf16[4,48,768]{2,1,0:T(8,128)(2,1)}), bf16[4,48,768]{2,1,0:T(8,128)(2,1)S(1)}, u32[]{:S(2)}, u32[]{:S(2)}) async-start(bf16[4,48,768]{2,1,0:T(8,128)(2,1)} %assemble.1), calls=%async_computation.2 | async-start | bytes 589824 | tf_op jit(solution)/shard_map/all_to_all | solution.py:403
  38.2 4.0 %collective-permute-start.3 = (bf16[512,768]{1,0:T(8,128)(2,1)S(1)}, bf16[512,768]{1,0:T(8,128)(2,1)S(1)}, u32[]{:S(2)}, u32[]{:S(2)}) collective-permute-start(bf16[512,768]{1,0:T(8,128)(2,1)S(1)} %get-tuple-element.19.refs_3_), channel_id=1, source_target_pairs={{0,2},{2,0},{1,3},{3,1},{4,6},{6,4},{5,7},{7,5},{8,10},{10,8},{9,1... | collective-permute-start | bytes 2359304 | tf_op jit(solution)/shard_map/ppermute | solution.py:369
  42.2 2.5 %collective-permute-start.2 = (bf16[512,768]{1,0:T(8,128)(2,1)S(1)}, bf16[512,768]{1,0:T(8,128)(2,1)S(1)}, u32[]{:S(2)}, u32[]{:S(2)}) collective-permute-start(bf16[512,768]{1,0:T(8,128)(2,1)S(1)} %collective-permute-done.1.refs_0_.refs_4_), channel_id=1, source_target_pairs={{0,4},{4,8},{8,12},{6,2},{10,6},{14,10},{1,5},{5,9},{9,13},{7,3},{... | collective-permute-start | bytes 2359304 | tf_op jit(solution)/shard_map/ppermute | solution.py:375
  44.7 13.9 %all-to-all-done.2.in_ref = bf16[4,48,768]{2,1,0:T(8,128)(2,1)S(1)} async-done(((bf16[4,48,768]{2,1,0:T(8,128)(2,1)}), bf16[4,48,768]{2,1,0:T(8,128)(2,1)S(1)}, u32[]{:S(2)}, u32[]{:S(2)}) %all-to-all-start.2) | async-done | bytes 294944 | tf_op jit(solution)/shard_map/all_to_all | solution.py:403
  58.6 1.9 %collective-permute-start.5 = (bf16[4,48,768]{2,1,0:T(8,128)(2,1)S(1)}, bf16[4,48,768]{2,1,0:T(8,128)(2,1)S(1)}, u32[]{:S(2)}, u32[]{:S(2)}) collective-permute-start(bf16[4,48,768]{2,1,0:T(8,128)(2,1)S(1)} %once.4), channel_id=1, source_target_pairs={{0,64},{32,96},{64,0},{96,32},{1,65},{33,97},{65,1},{97,33},{2,66}... | collective-permute-start | bytes 884744 | tf_op jit(solution)/shard_map/ppermute | solution.py:380
  60.5 2.9 %collective-permute-start.4 = (bf16[512,768]{1,0:T(8,128)(2,1)S(1)}, bf16[512,768]{1,0:T(8,128)(2,1)S(1)}, u32[]{:S(2)}, u32[]{:S(2)}) collective-permute-start(bf16[512,768]{1,0:T(8,128)(2,1)S(1)} %collective-permute-done.3.refs_1_.refs_5_), channel_id=1, source_target_pairs={{0,4},{4,8},{8,12},{6,2},{10,6},{14,10},{1,5},{5,9},{9,13},{7,3},{... | collective-permute-start | bytes 2359304 | tf_op jit(solution)/shard_map/ppermute | solution.py:375
  63.4 8.2 %collective-permute-done.5 = bf16[4,48,768]{2,1,0:T(8,128)(2,1)S(1)} collective-permute-done((bf16[4,48,768]{2,1,0:T(8,128)(2,1)S(1)}, bf16[4,48,768]{2,1,0:T(8,128)(2,1)S(1)}, u32[]{:S(2)}, u32[]{:S(2)}) %collective-permute-start.5) | collective-permute-done | bytes 294944 | tf_op jit(solution)/shard_map/ppermute | solution.py:380
  73.8 4.8 %collective-permute-start.6 = (bf16[2,4,48,768]{3,2,1,0:T(8,128)(2,1)S(1)}, bf16[2,4,48,768]{3,2,1,0:T(8,128)(2,1)S(1)}, u32[]{:S(2)}, u32[]{:S(2)}) collective-permute-start(bf16[2,4,48,768]{3,2,1,0:T(8,128)(2,1)S(1)} %once.5.refs_7_.refs_0_), channel_id=1, source_target_pairs={{0,32},{32,0},{64,96},{96,64},{1,33},{33,1},{65,97},{97,65},{2,34}... | collective-permute-start | bytes 1769480 | tf_op jit(solution)/shard_map/ppermute | solution.py:380
  78.6 1.9 %collective-permute-start.7 = (bf16[2,4,48,768]{3,2,1,0:T(8,128)(2,1)S(1)}, bf16[2,4,48,768]{3,2,1,0:T(8,128)(2,1)S(1)}, u32[]{:S(2)}, u32[]{:S(2)}) collective-permute-start(bf16[2,4,48,768]{3,2,1,0:T(8,128)(2,1)S(1)} %once.5.refs_7_.refs_0_), channel_id=1, source_target_pairs={{0,1},{1,0},{2,3},{3,2},{4,5},{5,4},{6,7},{7,6},{8,9},{9,8},{10,11... | collective-permute-start | bytes 1769480 | tf_op jit(solution)/shard_map/ppermute | solution.py:384
  80.5 9.8 %collective-permute-done.6.in_ref = bf16[2,4,48,768]{3,2,1,0:T(8,128)(2,1)S(1)} collective-permute-done((bf16[2,4,48,768]{3,2,1,0:T(8,128)(2,1)S(1)}, bf16[2,4,48,768]{3,2,1,0:T(8,128)(2,1)S(1)}, u32[]{:S(2)}, u32[]{:S(2)}) %collective-permute-start.6) | collective-permute-done | bytes 589856 | tf_op jit(solution)/shard_map/ppermute | solution.py:380
  97.0 10.7 %forward.1 = (bf16[2,512,384]{2,1,0:T(8,128)(2,1)S(1)}, f32[4,3,48,768]{3,2,1,0:T(8,128)}, bf16[4,3,48,768]{3,2,1,0:T(8,128)(2,1)}) custom-call(s32[2]{0:T(128)S(1)} %pad_add_fusion.at_ref, bf16[512,768]{1,0:T(8,128)(2,1)} %copy-done.3, bf16[512,768]{1,0:T(8,128)(2,1)} %copy-done.5, bf16[512,768]{1,0:T(8,128)(2,1)} %copy-done.13, ...), custom_call_target="tpu_custom_call" | custom-call | flops 4227858432 | bytes 12582912 | tf_op jit(solution)/shard_map/forward/pallas_call | solution.py:294
  107.7 4.1 %collective-permute-start.9 = (bf16[2,512,384]{2,1,0:T(8,128)(2,1)S(1)}, bf16[2,512,384]{2,1,0:T(8,128)(2,1)S(1)}, u32[]{:S(2)}, u32[]{:S(2)}) collective-permute-start(bf16[2,512,384]{2,1,0:T(8,128)(2,1)S(1)} %get-tuple-element.20.pre_ref), channel_id=1, source_target_pairs={{0,2},{2,0},{1,3},{3,1},{4,6},{6,4},{5,7},{7,5},{8,10},{10,8},{9,1... | collective-permute-start | bytes 2359304 | tf_op jit(solution)/shard_map/ppermute | solution.py:369
  111.9 23.3 %conditional.1 = (bf16[4,3,48,768]{3,2,1,0:T(8,128)(2,1)}) conditional(s32[]{:T(128)} %convert_element_type.9, () %tuple.14, (bf16[4,3,48,768]{3,2,1,0:T(8,128)(2,1)}, f32[4,3,48,768]{3,2,1,0:T(8,128)}) %tuple.15), branch_computations={%region_0.0_spmd, %region_1.0_spmd} | conditional | flops 1327104 | bytes 8847408 | solution.py:89
  111.9 1.9 %collective-permute-start = (bf16[4,3,48,768]{3,2,1,0:T(8,128)(2,1)}, bf16[4,3,48,768]{3,2,1,0:T(8,128)(2,1)S(1)}, u32[]{:S(2)}, u32[]{:S(2)}) collective-permute-start(bf16[4,3,48,768]{3,2,1,0:T(8,128)(2,1)} %get-tuple-element.8), channel_id=1, source_target_pairs={{0,1},{1,0},{2,3},{3,2},{4,5},{5,4},{6,7},{7,6},{8,9},{9,8},{10,11... | collective-permute-start | bytes 2654216 | tf_op jit(solution)/shard_map/cond/branch_1_fun/ppermute | solution.py:384
  113.8 2.6 %collective-permute-done = bf16[4,3,48,768]{3,2,1,0:T(8,128)(2,1)S(1)} collective-permute-done((bf16[4,3,48,768]{3,2,1,0:T(8,128)(2,1)}, bf16[4,3,48,768]{3,2,1,0:T(8,128)(2,1)S(1)}, u32[]{:S(2)}, u32[]{:S(2)}) %collective-permute-start) | collective-permute-done | bytes 884768 | tf_op jit(solution)/shard_map/cond/branch_1_fun/ppermute | solution.py:384
  118.1 17.0 %all_to_all.24 = bf16[4,3,48,768]{3,2,1,0:T(8,128)(2,1)} all-to-all(bf16[4,3,48,768]{3,2,1,0:T(8,128)(2,1)S(1)} %add_convert_fusion), channel_id=1, replica_groups=mesh['zh'=4,'zl'=4,'yl'=2,'x'=4,'yh'=2,'core'=2] {'x'}, dimensions={0} | all-to-all | bytes 1769472 | tf_op jit(solution)/shard_map/cond/branch_1_fun/all_to_all | solution.py:419
  135.2 2.2 %by_channel.1 = bf16[16,3,24,128]{3,2,1,0:T(8,128)(2,1)} custom-call(bf16[4,3,48,768]{3,2,1,0:T(8,128)(2,1)} %get-tuple-element.25.refs_0_.in_ref), custom_call_target="tpu_custom_call" | custom-call | bytes 1769472 | tf_op jit(solution)/shard_map/by_channel/pallas_call | solution.py:155
  137.4 7.6 %all-to-all-start.3 = ((bf16[16,3,24,128]{3,2,1,0:T(8,128)(2,1)}), bf16[16,3,24,128]{3,2,1,0:T(8,128)(2,1)S(1)}, u32[]{:S(2)}, u32[]{:S(2)}) async-start(bf16[16,3,24,128]{3,2,1,0:T(8,128)(2,1)} %by_channel.1), calls=%async_computation.3 | async-start | bytes 589824 | tf_op jit(solution)/shard_map/all_to_all | solution.py:424
  145.2 2.8 %collective-permute-start.10 = (bf16[2,512,384]{2,1,0:T(8,128)(2,1)S(1)}, bf16[2,512,384]{2,1,0:T(8,128)(2,1)S(1)}, u32[]{:S(2)}, u32[]{:S(2)}) collective-permute-start(bf16[2,512,384]{2,1,0:T(8,128)(2,1)S(1)} %once.7), channel_id=1, source_target_pairs={{0,4},{4,8},{8,12},{6,2},{10,6},{14,10},{1,5},{5,9},{9,13},{7,3},{... | collective-permute-start | bytes 2359304 | tf_op jit(solution)/shard_map/ppermute | solution.py:375
  148.0 15.5 %collective-permute-done.10.handed_ref = bf16[2,512,384]{2,1,0:T(8,128)(2,1)S(1)} collective-permute-done((bf16[2,512,384]{2,1,0:T(8,128)(2,1)S(1)}, bf16[2,512,384]{2,1,0:T(8,128)(2,1)S(1)}, u32[]{:S(2)}, u32[]{:S(2)}) %collective-permute-start.10) | collective-permute-done | bytes 786464 | tf_op jit(solution)/shard_map/ppermute | solution.py:375
  163.5 8.9 %backward.1 = (bf16[2,512,768]{2,1,0:T(8,128)(2,1)}, f32[8,128]{1,0:T(8,128)S(1)}) custom-call(s32[2]{0:T(128)S(1)} %pad_add_fusion.at_ref, bf16[2,512,768]{2,1,0:T(8,128)(2,1)} %in_ref.3, bf16[2,512,768]{2,1,0:T(8,128)(2,1)} %cot_ref.1, bf16[2,512,384]{2,1,0:T(8,128)(2,1)S(1)} %collective-permute-done.9.in_ref.partner_ref, ...), custom_call_target="tpu_custom_call" | custom-call | flops 1811939328 | bytes 12582912 | tf_op jit(solution)/shard_map/backward/pallas_call | solution.py:347
  172.5 9.3 %all_to_all.26.in_ref = bf16[4,24,128]{2,1,0:T(8,128)(2,1)S(1)} all-to-all(bf16[4,24,128]{2,1,0:T(8,128)(2,1)S(1)} %add_parts.1), channel_id=1, replica_groups=mesh['zh'=4,'zl'=4,'yl'=2,'x'=4,'yh'=2,'core'=2] {'yh','yl'}, dimensions={0} | all-to-all | bytes 49152 | tf_op jit(solution)/shard_map/all_to_all | solution.py:429
  (51 shorter events, 16.8 us)
Async XLA Ops:
  16.8 1.4 copy-start
  19.8 22.4 %copy-start.13 = (bf16[512,768]{1,0:T(8,128)(2,1)}, bf16[512,768]{1,0:T(8,128)(2,1)S(1)}, u32[]{:S(2)}) copy-start(bf16[512,768]{1,0:T(8,128)(2,1)S(1)} %get-tuple-element.18.refs_2_) | copy-start | bytes 2359300
  19.8 51.9 %copy-start.14 = (bf16[512,768]{1,0:T(8,128)(2,1)}, bf16[512,768]{1,0:T(8,128)(2,1)S(1)}, u32[]{:S(2)}) copy-start(bf16[512,768]{1,0:T(8,128)(2,1)S(1)} %get-tuple-element.19.refs_3_) | copy-start | bytes 2359300
  19.8 22.4 %collective-permute-start.1 = (bf16[512,768]{1,0:T(8,128)(2,1)S(1)}, bf16[512,768]{1,0:T(8,128)(2,1)S(1)}, u32[]{:S(2)}, u32[]{:S(2)}) collective-permute-start(bf16[512,768]{1,0:T(8,128)(2,1)S(1)} %get-tuple-element.18.refs_2_), channel_id=1, source_target_pairs={{0,2},{2,0},{1,3},{3,1},{4,6},{6,4},{5,7},{7,5},{8,10},{10,8},{9,1... | collective-permute-start | bytes 2359304 | tf_op jit(solution)/shard_map/ppermute | solution.py:369
  24.0 34.5 %all-to-all-start.2 = ((bf16[4,48,768]{2,1,0:T(8,128)(2,1)}), bf16[4,48,768]{2,1,0:T(8,128)(2,1)S(1)}, u32[]{:S(2)}, u32[]{:S(2)}) async-start(bf16[4,48,768]{2,1,0:T(8,128)(2,1)} %assemble.1), calls=%async_computation.2 | async-start | bytes 589824 | tf_op jit(solution)/shard_map/all_to_all | solution.py:403
  38.2 22.3 %collective-permute-start.3 = (bf16[512,768]{1,0:T(8,128)(2,1)S(1)}, bf16[512,768]{1,0:T(8,128)(2,1)S(1)}, u32[]{:S(2)}, u32[]{:S(2)}) collective-permute-start(bf16[512,768]{1,0:T(8,128)(2,1)S(1)} %get-tuple-element.19.refs_3_), channel_id=1, source_target_pairs={{0,2},{2,0},{1,3},{3,1},{4,6},{6,4},{5,7},{7,5},{8,10},{10,8},{9,1... | collective-permute-start | bytes 2359304 | tf_op jit(solution)/shard_map/ppermute | solution.py:369
  42.2 31.5 %copy-start.1 = (bf16[512,768]{1,0:T(8,128)(2,1)}, bf16[512,768]{1,0:T(8,128)(2,1)S(1)}, u32[]{:S(2)}) copy-start(bf16[512,768]{1,0:T(8,128)(2,1)S(1)} %collective-permute-done.1.refs_0_.refs_4_) | copy-start | bytes 2359300
  42.2 29.4 %collective-permute-start.2 = (bf16[512,768]{1,0:T(8,128)(2,1)S(1)}, bf16[512,768]{1,0:T(8,128)(2,1)S(1)}, u32[]{:S(2)}, u32[]{:S(2)}) collective-permute-start(bf16[512,768]{1,0:T(8,128)(2,1)S(1)} %collective-permute-done.1.refs_0_.refs_4_), channel_id=1, source_target_pairs={{0,4},{4,8},{8,12},{6,2},{10,6},{14,10},{1,5},{5,9},{9,13},{7,3},{... | collective-permute-start | bytes 2359304 | tf_op jit(solution)/shard_map/ppermute | solution.py:375
  58.6 13.0 %collective-permute-start.5 = (bf16[4,48,768]{2,1,0:T(8,128)(2,1)S(1)}, bf16[4,48,768]{2,1,0:T(8,128)(2,1)S(1)}, u32[]{:S(2)}, u32[]{:S(2)}) collective-permute-start(bf16[4,48,768]{2,1,0:T(8,128)(2,1)S(1)} %once.4), channel_id=1, source_target_pairs={{0,64},{32,96},{64,0},{96,32},{1,65},{33,97},{65,1},{97,33},{2,66}... | collective-permute-start | bytes 884744 | tf_op jit(solution)/shard_map/ppermute | solution.py:380
  60.5 13.3 %copy-start.2 = (bf16[512,768]{1,0:T(8,128)(2,1)}, bf16[512,768]{1,0:T(8,128)(2,1)S(1)}, u32[]{:S(2)}) copy-start(bf16[512,768]{1,0:T(8,128)(2,1)S(1)} %collective-permute-done.3.refs_1_.refs_5_) | copy-start | bytes 2359300
  60.5 20.0 %collective-permute-start.4 = (bf16[512,768]{1,0:T(8,128)(2,1)S(1)}, bf16[512,768]{1,0:T(8,128)(2,1)S(1)}, u32[]{:S(2)}, u32[]{:S(2)}) collective-permute-start(bf16[512,768]{1,0:T(8,128)(2,1)S(1)} %collective-permute-done.3.refs_1_.refs_5_), channel_id=1, source_target_pairs={{0,4},{4,8},{8,12},{6,2},{10,6},{14,10},{1,5},{5,9},{9,13},{7,3},{... | collective-permute-start | bytes 2359304 | tf_op jit(solution)/shard_map/ppermute | solution.py:375
  71.7 0.9 copy-start.3
  72.6 1.1 copy-start.4
  73.8 16.5 %collective-permute-start.6 = (bf16[2,4,48,768]{3,2,1,0:T(8,128)(2,1)S(1)}, bf16[2,4,48,768]{3,2,1,0:T(8,128)(2,1)S(1)}, u32[]{:S(2)}, u32[]{:S(2)}) collective-permute-start(bf16[2,4,48,768]{3,2,1,0:T(8,128)(2,1)S(1)} %once.5.refs_7_.refs_0_), channel_id=1, source_target_pairs={{0,32},{32,0},{64,96},{96,64},{1,33},{33,1},{65,97},{97,65},{2,34}... | collective-permute-start | bytes 1769480 | tf_op jit(solution)/shard_map/ppermute | solution.py:380
  78.6 14.7 %collective-permute-start.7 = (bf16[2,4,48,768]{3,2,1,0:T(8,128)(2,1)S(1)}, bf16[2,4,48,768]{3,2,1,0:T(8,128)(2,1)S(1)}, u32[]{:S(2)}, u32[]{:S(2)}) collective-permute-start(bf16[2,4,48,768]{3,2,1,0:T(8,128)(2,1)S(1)} %once.5.refs_7_.refs_0_), channel_id=1, source_target_pairs={{0,1},{1,0},{2,3},{3,2},{4,5},{5,4},{6,7},{7,6},{8,9},{9,8},{10,11... | collective-permute-start | bytes 1769480 | tf_op jit(solution)/shard_map/ppermute | solution.py:384
  91.3 3.9 %collective-permute-start.8 = (bf16[2,4,48,768]{3,2,1,0:T(8,128)(2,1)S(1)}, bf16[2,4,48,768]{3,2,1,0:T(8,128)(2,1)S(1)}, u32[]{:S(2)}, u32[]{:S(2)}) collective-permute-start(bf16[2,4,48,768]{3,2,1,0:T(8,128)(2,1)S(1)} %once.6.refs_8_.refs_1_), channel_id=1, source_target_pairs={{0,1},{1,0},{2,3},{3,2},{4,5},{5,4},{6,7},{7,6},{8,9},{9,8},{10,11... | collective-permute-start | bytes 1769480 | tf_op jit(solution)/shard_map/ppermute | solution.py:384
  93.3 14.5 %copy-start.6 = (bf16[2,4,48,768]{3,2,1,0:T(8,128)(2,1)}, bf16[2,4,48,768]{3,2,1,0:T(8,128)(2,1)S(1)}, u32[]{:S(2)}) copy-start(bf16[2,4,48,768]{3,2,1,0:T(8,128)(2,1)S(1)} %collective-permute-done.7.refs_9_.refs_2_) | copy-start | bytes 1769476
  95.9 1.1 copy-start.9
  107.7 37.3 %collective-permute-start.9 = (bf16[2,512,384]{2,1,0:T(8,128)(2,1)S(1)}, bf16[2,512,384]{2,1,0:T(8,128)(2,1)S(1)}, u32[]{:S(2)}, u32[]{:S(2)}) collective-permute-start(bf16[2,512,384]{2,1,0:T(8,128)(2,1)S(1)} %get-tuple-element.20.pre_ref), channel_id=1, source_target_pairs={{0,2},{2,0},{1,3},{3,1},{4,6},{6,4},{5,7},{7,5},{8,10},{10,8},{9,1... | collective-permute-start | bytes 2359304 | tf_op jit(solution)/shard_map/ppermute | solution.py:369
  111.9 4.5 %collective-permute-start = (bf16[4,3,48,768]{3,2,1,0:T(8,128)(2,1)}, bf16[4,3,48,768]{3,2,1,0:T(8,128)(2,1)S(1)}, u32[]{:S(2)}, u32[]{:S(2)}) collective-permute-start(bf16[4,3,48,768]{3,2,1,0:T(8,128)(2,1)} %get-tuple-element.8), channel_id=1, source_target_pairs={{0,1},{1,0},{2,3},{3,2},{4,5},{5,4},{6,7},{7,6},{8,9},{9,8},{10,11... | collective-permute-start | bytes 2654216 | tf_op jit(solution)/shard_map/cond/branch_1_fun/ppermute | solution.py:384
  137.4 35.0 %all-to-all-start.3 = ((bf16[16,3,24,128]{3,2,1,0:T(8,128)(2,1)}), bf16[16,3,24,128]{3,2,1,0:T(8,128)(2,1)S(1)}, u32[]{:S(2)}, u32[]{:S(2)}) async-start(bf16[16,3,24,128]{3,2,1,0:T(8,128)(2,1)} %by_channel.1), calls=%async_computation.3 | async-start | bytes 589824 | tf_op jit(solution)/shard_map/all_to_all | solution.py:424
  145.1 18.4 %copy-start.7 = (bf16[2,4,48,768]{3,2,1,0:T(8,128)(2,1)S(1)}, bf16[2,4,48,768]{3,2,1,0:T(8,128)(2,1)}, u32[]{:S(2)}) copy-start(bf16[2,4,48,768]{3,2,1,0:T(8,128)(2,1)} %copy-done.6) | copy-start | bytes 1769476
  145.1 18.4 %copy-start.10 = (bf16[2,4,48,768]{3,2,1,0:T(8,128)(2,1)S(1)}, bf16[2,4,48,768]{3,2,1,0:T(8,128)(2,1)}, u32[]{:S(2)}) copy-start(bf16[2,4,48,768]{3,2,1,0:T(8,128)(2,1)} %copy-done.8) | copy-start | bytes 1769476
  145.2 18.3 %collective-permute-start.10 = (bf16[2,512,384]{2,1,0:T(8,128)(2,1)S(1)}, bf16[2,512,384]{2,1,0:T(8,128)(2,1)S(1)}, u32[]{:S(2)}, u32[]{:S(2)}) collective-permute-start(bf16[2,512,384]{2,1,0:T(8,128)(2,1)S(1)} %once.7), channel_id=1, source_target_pairs={{0,4},{4,8},{8,12},{6,2},{10,6},{14,10},{1,5},{5,9},{9,13},{7,3},{... | collective-permute-start | bytes 2359304 | tf_op jit(solution)/shard_map/ppermute | solution.py:375
  (4 other events, 3.1 us)

commit v7 on v6

--- a/solution.py
+++ b/solution.py
@@ -161,7 +161,7 @@
     )(parts)
 
 
-def add_kernel(f_part, in_ref, _, out_ref):
+def add_kernel(f_part, in_ref, out_ref):
     peers, taps, c_part, _ = in_ref.shape
     total = [sum(in_ref[p, tap].astype(jnp.float32) for p in range(peers)) for tap in range(taps)]
     blank = jnp.zeros((c_part, LANES - taps * f_part), jnp.float32)
@@ -172,32 +172,32 @@
             out_ref[high * Y_PARTS + low] = jnp.concatenate(parts, axis=1).astype(out_ref.dtype)
 
 
-def add_parts(parts, f_part, after):
+def add_parts(parts, f_part):
     return pl.pallas_call(
         functools.partial(add_kernel, f_part),
-        in_specs=[IN_VMEM, ANYWHERE],
         out_shape=struct((Y_PARTS * Y_PARTS,) + parts.shape[2:], parts.dtype),
         compiler_params=params(8),
         cost_estimate=cost(0, 4 * parts.size),
         name="add_parts",
-    )(parts, after)
-
-
-def finish_kernel(in_ref, out_ref):
+    )(parts)
+
+
+def finish_kernel(in_ref, _, out_ref):
     taps, _, f_part = out_ref.shape
     total = sum(in_ref[p].astype(jnp.float32) for p in range(in_ref.shape[0]))
     for tap in range(taps):
         out_ref[tap] = total[:, tap * f_part : (tap + 1) * f_part]
 
 
-def finish(pieces, taps, f_part):
+def finish(pieces, taps, f_part, after):
     return pl.pallas_call(
         finish_kernel,
+        in_specs=[IN_VMEM, ANYWHERE],
         out_shape=struct((taps, pieces.shape[1], f_part), jnp.float32),
         compiler_params=params(8),
         cost_estimate=cost(0, 4 * pieces.size),
         name="finish",
-    )(pieces)
+    )(pieces, after)
 
 
 def act_kernel(in_ref, _, *out_refs):
@@ -243,26 +243,21 @@
 
 def forward_kernel(scale, samples, at_ref, *refs):
     count = 3 * samples + 1
-    far_refs, refs = refs[: count + 4], refs[count + 4 :]
-    pre_ref, own_out, other_out, acts, cot, packed, weights, point, turned, sems = refs
+    far_refs, packed, refs = refs[:count], refs[count : count + 4], refs[count + 4 :]
+    pre_ref, own_out, other_out, acts, cot, weights, point, turned, sems = refs
     _, bins, width = cot.shape
     half = weights.shape[2] // CORES
-    near_refs = [acts.at[i] for i in range(3 * samples)] + [cot] + [packed.at[i] for i in range(4)]
+    near_refs = [acts.at[i] for i in range(3 * samples)] + [cot]
     copies = [
         pltpu.make_async_copy(far_ref, near_ref, sems.at[i])
         for i, (far_ref, near_ref) in enumerate(zip(far_refs, near_refs))
     ]
-    for copy in copies[count:]:
-        copy.start()
     for sample in range(samples):
         for role in range(3):
             copies[role * samples + sample].start()
         if sample == 0:
             copies[count - 1].start()
-    for copy in copies[count:]:
-        copy.wait()
-    sides = [[packed.at[2 * side + low] for low in range(2)] for side in range(CORES)]
-    join_weights(sides, weights, point, at_ref[0], at_ref[1])
+    join_weights((packed[:2], packed[2:]), weights, point, at_ref[0], at_ref[1])
     for sample in range(samples):
         for role in range(3):
             copies[role * samples + sample].wait()
@@ -293,7 +288,7 @@
     count = 3 * samples
     return pl.pallas_call(
         functools.partial(forward_kernel, scale, samples),
-        in_specs=[IN_SMEM] + [IN_HBM] * (count + 5),
+        in_specs=[IN_SMEM] + [IN_HBM] * (count + 1) + [IN_VMEM] * 4,
         out_specs=[IN_VMEM] * 3,
         out_shape=[
             struct((samples, bins, hidden), jnp.bfloat16),
@@ -303,11 +298,10 @@
         scratch_shapes=[
             pltpu.VMEM((count, bins, width), jnp.bfloat16),
             pltpu.VMEM(cotangent.shape, jnp.bfloat16),
-            pltpu.VMEM((4,) + own_w[0].shape, jnp.bfloat16),
             pltpu.VMEM((3, width, hidden), jnp.bfloat16),
             pltpu.VMEM((width, hidden), jnp.bfloat16),
             pltpu.VMEM((samples, hidden, bins), jnp.bfloat16),
-            pltpu.SemaphoreType.DMA((count + 5,)),
+            pltpu.SemaphoreType.DMA((count + 1,)),
         ],
         compiler_params=params(30),
         cost_estimate=cost(14 * samples * bins * width * hidden, 16 * samples * bins * width),
@@ -361,7 +355,7 @@
         partner,
         grad_pre,
         handed,
-        *packed,
+        *[in_hbm(part) for part in packed],
     )
 
 
@@ -394,10 +388,10 @@
     grad_scale = float(samples * bins * devices) ** (-0.5)
     at = jnp.stack([lax.axis_index("yh"), lax.axis_index("zl")]).astype(jnp.int32)
 
-    packed = pack(conv_weight, point_weight, blocks * Y_PARTS)
+    packed = pack(in_hbm(conv_weight), in_hbm(point_weight), blocks * Y_PARTS)
     pieces = lax.all_to_all(packed, ("x", "yh", "yl"), 0, 0)
 
-    mids = list(activate(inputs, 256, pieces))
+    mids = list(activate(in_hbm(inputs), 128, pieces))
     partners = [exchanged(mid) for mid in mids]
 
     part = lax.all_to_all(assemble(pieces, f_part, taps + 1)[:far], "zh", 0, 0)
@@ -415,18 +409,20 @@
     )
 
     def first_sums(own, other):
-        pair = own + other_core(other).astype(jnp.float32)
+        pair = own + other.astype(jnp.float32)
         return lax.all_to_all(pair.astype(jnp.bfloat16), "x", 0, 0)
 
+    other = other_core(other)
     grad_partner = exchanged(grad_pre)
     parts = held(first_sums, own, other)
     grad_handed = handed_on(once(grad_partner, parts))
+
     parts = lax.all_to_all(by_channel(parts, depth), ("zh", "zl"), 0, 0)
     input_grad, token = backward(
         at, inputs, cotangent, grad_partner, grad_pre, grad_handed, packed, 256
     )
-    sums = add_parts(parts, f_part, token)
-    conv_grad = finish(lax.all_to_all(sums, ("yh", "yl"), 0, 0), taps, f_part)
+    sums = add_parts(parts, f_part)
+    conv_grad = finish(lax.all_to_all(sums, ("yh", "yl"), 0, 0), taps, f_part, token)
     return (input_grad, conv_grad)
 
 

time: 184 us -> 174 us (0.946)
  the two profiles are of different devices: /device:TPU:32 before, /device:TPU:8 now
where the time goes in v7:
time: 174 us; the launch traced here: 173 us
  starting transfers between devices  58.9 us (34%)
  waiting for transfers between devices  48.5 us (28%)
  blocking collectives  30.9 us (18%)
  Pallas kernels  28.9 us (17%)
  local copies, waits for them, and re-layouts  2.93 us (2%)
  other arithmetic  1.8 us (1%)
    ppermute x2, waiting for transfers between devices, z_pair(): return lax.ppermute(array, 'zl', [(i, i ^ bit) for i in range(near)])  20.6 us
    all_to_all x1, blocking collectives, first_sums(): return lax.all_to_all(pair.astype(jnp.bfloat16), 'x', 0, 0)  16.3 us
    all_to_all x1, waiting for transfers between devices, body(): parts = lax.all_to_all(by_channel(parts, depth), ('zh', 'zl'), 0, 0)  16.1 us
    all_to_all x1, blocking collectives, body(): pieces = lax.all_to_all(packed, ('x', 'yh', 'yl'), 0, 0)  14.6 us
    all_to_all x1, starting transfers between devices, body(): part = lax.all_to_all(assemble(pieces, f_part, taps + 1)[:far], 'zh', 0, 0)  14 us
    pallas_call x1, Pallas kernels, forward(): pl.pallas_call(functools.partial(forward_kernel, scale, samples), in_spec...  11.6 us
    ppermute x3, starting transfers between devices, exchanged(): return lax.ppermute(array, 'yh', [(0, 1), (1, 0)])  11.2 us
    all_to_all x1, waiting for transfers between devices, body(): part = lax.all_to_all(assemble(pieces, f_part, taps + 1)[:far], 'zh', 0, 0)  9.87 us
  transfers between devices with their start and end apart: 14, of which 5 were waited for; matrix products, arithmetic and copies ran while one was open for 1% of the time, Pallas kernels for 7%

profile of v7, /device:TPU:8, one launch (start us, length us, event | category | flops | bytes accessed | tf_op | source)
XLA Modules:
  0.0 172.8 jit_solution(6417969885553366226)
XLA Ops:
  1.5 14.6 %all_to_all.25._.in_ref = bf16[16,24,128]{2,1,0:T(8,128)(2,1)S(1)} all-to-all(bf16[16,24,128]{2,1,0:T(8,128)(2,1)S(1)} %pack.1), channel_id=1, replica_groups=mesh['zh'=4,'zl'=4,'yl'=2,'x'=4,'yh'=2,'core'=2] {'x','yh','yl'}, dimensions={0} | all-to-all | bytes 196608 | tf_op jit(solution)/shard_map/all_to_all | solution.py:392
  16.1 3.2 %activate.1 = (bf16[512,768]{1,0:T(8,128)(2,1)S(1)}, bf16[512,768]{1,0:T(8,128)(2,1)S(1)}) custom-call(bf16[2,512,768]{2,1,0:T(8,128)(2,1)} %in_ref.3, bf16[16,24,128]{2,1,0:T(8,128)(2,1)S(1)} %all_to_all.25._.in_ref), custom_call_target="tpu_custom_call" | custom-call | flops 15728640 | bytes 3145728 | tf_op jit(solution)/shard_map/activate/pallas_call | solution.py:211
  19.4 3.5 %collective-permute-start = (bf16[512,768]{1,0:T(8,128)(2,1)S(1)}, bf16[512,768]{1,0:T(8,128)(2,1)S(1)}, u32[]{:S(2)}, u32[]{:S(2)}) collective-permute-start(bf16[512,768]{1,0:T(8,128)(2,1)S(1)} %get-tuple-element.18.refs_2_), channel_id=1, source_target_pairs={{0,2},{2,0},{1,3},{3,1},{4,6},{6,4},{5,7},{7,5},{8,10},{10,8},{9,1... | collective-permute-start | bytes 2359304 | tf_op jit(solution)/shard_map/ppermute | solution.py:363
  23.7 14.0 %all-to-all-start.2 = ((bf16[4,48,768]{2,1,0:T(8,128)(2,1)}), bf16[4,48,768]{2,1,0:T(8,128)(2,1)S(1)}, u32[]{:S(2)}, u32[]{:S(2)}) async-start(bf16[4,48,768]{2,1,0:T(8,128)(2,1)} %assemble.1), calls=%async_computation.2 | async-start | bytes 589824 | tf_op jit(solution)/shard_map/all_to_all | solution.py:397
  37.7 3.8 %collective-permute-start.2 = (bf16[512,768]{1,0:T(8,128)(2,1)S(1)}, bf16[512,768]{1,0:T(8,128)(2,1)S(1)}, u32[]{:S(2)}, u32[]{:S(2)}) collective-permute-start(bf16[512,768]{1,0:T(8,128)(2,1)S(1)} %get-tuple-element.19.refs_3_), channel_id=1, source_target_pairs={{0,2},{2,0},{1,3},{3,1},{4,6},{6,4},{5,7},{7,5},{8,10},{10,8},{9,1... | collective-permute-start | bytes 2359304 | tf_op jit(solution)/shard_map/ppermute | solution.py:363
  41.6 2.5 %collective-permute-start.1 = (bf16[512,768]{1,0:T(8,128)(2,1)S(1)}, bf16[512,768]{1,0:T(8,128)(2,1)S(1)}, u32[]{:S(2)}, u32[]{:S(2)}) collective-permute-start(bf16[512,768]{1,0:T(8,128)(2,1)S(1)} %collective-permute-done.refs_0_.refs_4_), channel_id=1, source_target_pairs={{0,4},{4,8},{8,12},{6,2},{10,6},{14,10},{1,5},{5,9},{9,13},{7,3},{... | collective-permute-start | bytes 2359304 | tf_op jit(solution)/shard_map/ppermute | solution.py:369
  44.1 9.9 %all-to-all-done.2.in_ref = bf16[4,48,768]{2,1,0:T(8,128)(2,1)S(1)} async-done(((bf16[4,48,768]{2,1,0:T(8,128)(2,1)}), bf16[4,48,768]{2,1,0:T(8,128)(2,1)S(1)}, u32[]{:S(2)}, u32[]{:S(2)}) %all-to-all-start.2) | async-done | bytes 294944 | tf_op jit(solution)/shard_map/all_to_all | solution.py:397
  54.0 7.5 %collective-permute-start.4 = (bf16[4,48,768]{2,1,0:T(8,128)(2,1)S(1)}, bf16[4,48,768]{2,1,0:T(8,128)(2,1)S(1)}, u32[]{:S(2)}, u32[]{:S(2)}) collective-permute-start(bf16[4,48,768]{2,1,0:T(8,128)(2,1)S(1)} %once.4), channel_id=1, source_target_pairs={{0,64},{32,96},{64,0},{96,32},{1,65},{33,97},{65,1},{97,33},{2,66}... | collective-permute-start | bytes 884744 | tf_op jit(solution)/shard_map/ppermute | solution.py:374
  61.5 2.5 %collective-permute-start.3 = (bf16[512,768]{1,0:T(8,128)(2,1)S(1)}, bf16[512,768]{1,0:T(8,128)(2,1)S(1)}, u32[]{:S(2)}, u32[]{:S(2)}) collective-permute-start(bf16[512,768]{1,0:T(8,128)(2,1)S(1)} %collective-permute-done.2.refs_1_.refs_5_), channel_id=1, source_target_pairs={{0,4},{4,8},{8,12},{6,2},{10,6},{14,10},{1,5},{5,9},{9,13},{7,3},{... | collective-permute-start | bytes 2359304 | tf_op jit(solution)/shard_map/ppermute | solution.py:369
  64.0 9.0 %collective-permute-done.4 = bf16[4,48,768]{2,1,0:T(8,128)(2,1)S(1)} collective-permute-done((bf16[4,48,768]{2,1,0:T(8,128)(2,1)S(1)}, bf16[4,48,768]{2,1,0:T(8,128)(2,1)S(1)}, u32[]{:S(2)}, u32[]{:S(2)}) %collective-permute-start.4) | collective-permute-done | bytes 294944 | tf_op jit(solution)/shard_map/ppermute | solution.py:374
  75.1 1.9 %collective-permute-start.5 = (bf16[2,4,48,768]{3,2,1,0:T(8,128)(2,1)S(1)}, bf16[2,4,48,768]{3,2,1,0:T(8,128)(2,1)S(1)}, u32[]{:S(2)}, u32[]{:S(2)}) collective-permute-start(bf16[2,4,48,768]{3,2,1,0:T(8,128)(2,1)S(1)} %once.5.refs_7_.refs_0_), channel_id=1, source_target_pairs={{0,32},{32,0},{64,96},{96,64},{1,33},{33,1},{65,97},{97,65},{2,34}... | collective-permute-start | bytes 1769480 | tf_op jit(solution)/shard_map/ppermute | solution.py:374
  77.0 1.9 %collective-permute-start.6 = (bf16[2,4,48,768]{3,2,1,0:T(8,128)(2,1)S(1)}, bf16[2,4,48,768]{3,2,1,0:T(8,128)(2,1)S(1)}, u32[]{:S(2)}, u32[]{:S(2)}) collective-permute-start(bf16[2,4,48,768]{3,2,1,0:T(8,128)(2,1)S(1)} %once.5.refs_7_.refs_0_), channel_id=1, source_target_pairs={{0,1},{1,0},{2,3},{3,2},{4,5},{5,4},{6,7},{7,6},{8,9},{9,8},{10,11... | collective-permute-start | bytes 1769480 | tf_op jit(solution)/shard_map/ppermute | solution.py:378
  79.0 11.6 %collective-permute-done.5.in_ref = bf16[2,4,48,768]{3,2,1,0:T(8,128)(2,1)S(1)} collective-permute-done((bf16[2,4,48,768]{3,2,1,0:T(8,128)(2,1)S(1)}, bf16[2,4,48,768]{3,2,1,0:T(8,128)(2,1)S(1)}, u32[]{:S(2)}, u32[]{:S(2)}) %collective-permute-start.5) | collective-permute-done | bytes 589856 | tf_op jit(solution)/shard_map/ppermute | solution.py:374
  91.5 1.9 %collective-permute-start.7 = (bf16[2,4,48,768]{3,2,1,0:T(8,128)(2,1)S(1)}, bf16[2,4,48,768]{3,2,1,0:T(8,128)(2,1)S(1)}, u32[]{:S(2)}, u32[]{:S(2)}) collective-permute-start(bf16[2,4,48,768]{3,2,1,0:T(8,128)(2,1)S(1)} %once.6.refs_8_.refs_1_), channel_id=1, source_target_pairs={{0,1},{1,0},{2,3},{3,2},{4,5},{5,4},{6,7},{7,6},{8,9},{9,8},{10,11... | collective-permute-start | bytes 1769480 | tf_op jit(solution)/shard_map/ppermute | solution.py:378
  95.4 11.6 %forward.1 = (bf16[2,512,384]{2,1,0:T(8,128)(2,1)S(1)}, f32[4,3,48,768]{3,2,1,0:T(8,128)}, bf16[4,3,48,768]{3,2,1,0:T(8,128)(2,1)}) custom-call(s32[2]{0:T(128)S(1)} %pad_add_fusion.at_ref, bf16[512,768]{1,0:T(8,128)(2,1)} %copy-done.4, bf16[512,768]{1,0:T(8,128)(2,1)} %copy-done.6, bf16[512,768]{1,0:T(8,128)(2,1)} %copy-done.9, ...), custom_call_target="tpu_custom_call" | custom-call | flops 4227858432 | bytes 12582912 | tf_op jit(solution)/shard_map/forward/pallas_call | solution.py:289
  107.0 2.0 %collective-permute-start.9 = (bf16[4,3,48,768]{3,2,1,0:T(8,128)(2,1)}, bf16[4,3,48,768]{3,2,1,0:T(8,128)(2,1)S(1)}, u32[]{:S(2)}, u32[]{:S(2)}) collective-permute-start(bf16[4,3,48,768]{3,2,1,0:T(8,128)(2,1)} %get-tuple-element.21), channel_id=1, source_target_pairs={{0,1},{1,0},{2,3},{3,2},{4,5},{5,4},{6,7},{7,6},{8,9},{9,8},{10,11... | collective-permute-start | bytes 2654216 | tf_op jit(solution)/shard_map/ppermute | solution.py:378
  109.1 3.9 %collective-permute-start.8 = (bf16[2,512,384]{2,1,0:T(8,128)(2,1)S(1)}, bf16[2,512,384]{2,1,0:T(8,128)(2,1)S(1)}, u32[]{:S(2)}, u32[]{:S(2)}) collective-permute-start(bf16[2,512,384]{2,1,0:T(8,128)(2,1)S(1)} %get-tuple-element.20.pre_ref), channel_id=1, source_target_pairs={{0,2},{2,0},{1,3},{3,1},{4,6},{6,4},{5,7},{7,5},{8,10},{10,8},{9,1... | collective-permute-start | bytes 2359304 | tf_op jit(solution)/shard_map/ppermute | solution.py:363
  113.0 17.9 %conditional.1 = (bf16[4,3,48,768]{3,2,1,0:T(8,128)(2,1)S(1)}) conditional(s32[]{:T(128)} %convert_element_type.9, () %tuple.14, (bf16[4,3,48,768]{3,2,1,0:T(8,128)(2,1)S(1)}, f32[4,3,48,768]{3,2,1,0:T(8,128)}) %tuple.15), branch_computations={%region_0.0_spmd, %region_1.0_spmd} | conditional | flops 1327104 | bytes 5308424 | solution.py:89
  114.7 16.3 %all_to_all.24 = bf16[4,3,48,768]{3,2,1,0:T(8,128)(2,1)S(1)} all-to-all(bf16[4,3,48,768]{3,2,1,0:T(8,128)(2,1)S(1)} %add_convert_fusion), channel_id=1, replica_groups=mesh['zh'=4,'zl'=4,'yl'=2,'x'=4,'yh'=2,'core'=2] {'x'}, dimensions={0} | all-to-all | bytes 1769472 | tf_op jit(solution)/shard_map/cond/branch_1_fun/all_to_all | solution.py:413
  132.0 6.0 %all-to-all-start.3 = ((bf16[16,3,24,128]{3,2,1,0:T(8,128)(2,1)}), bf16[16,3,24,128]{3,2,1,0:T(8,128)(2,1)S(1)}, u32[]{:S(2)}, u32[]{:S(2)}) async-start(bf16[16,3,24,128]{3,2,1,0:T(8,128)(2,1)} %by_channel.1), calls=%async_computation.3 | async-start | bytes 589824 | tf_op jit(solution)/shard_map/all_to_all | solution.py:420
  138.1 2.5 %collective-permute-start.10 = (bf16[2,512,384]{2,1,0:T(8,128)(2,1)S(1)}, bf16[2,512,384]{2,1,0:T(8,128)(2,1)S(1)}, u32[]{:S(2)}, u32[]{:S(2)}) collective-permute-start(bf16[2,512,384]{2,1,0:T(8,128)(2,1)S(1)} %once.7), channel_id=1, source_target_pairs={{0,4},{4,8},{8,12},{6,2},{10,6},{14,10},{1,5},{5,9},{9,13},{7,3},{... | collective-permute-start | bytes 2359304 | tf_op jit(solution)/shard_map/ppermute | solution.py:369
  140.6 16.1 %all-to-all-done.3.in_ref = bf16[16,3,24,128]{3,2,1,0:T(8,128)(2,1)S(1)} async-done(((bf16[16,3,24,128]{3,2,1,0:T(8,128)(2,1)}), bf16[16,3,24,128]{3,2,1,0:T(8,128)(2,1)S(1)}, u32[]{:S(2)}, u32[]{:S(2)}) %all-to-all-start.3) | async-done | bytes 294944 | tf_op jit(solution)/shard_map/all_to_all | solution.py:420
  157.5 5.0 %all-to-all-start.4 = ((bf16[4,24,128]{2,1,0:T(8,128)(2,1)}), bf16[4,24,128]{2,1,0:T(8,128)(2,1)S(1)}, u32[]{:S(2)}, u32[]{:S(2)}) async-start(bf16[4,24,128]{2,1,0:T(8,128)(2,1)} %add_parts.1), calls=%async_computation.4 | async-start | bytes 49152 | tf_op jit(solution)/shard_map/all_to_all | solution.py:425
  162.5 9.7 %backward.1 = (bf16[2,512,768]{2,1,0:T(8,128)(2,1)}, f32[8,128]{1,0:T(8,128)S(1)}) custom-call(s32[2]{0:T(128)S(1)} %pad_add_fusion.at_ref, bf16[2,512,768]{2,1,0:T(8,128)(2,1)} %in_ref.3, bf16[2,512,768]{2,1,0:T(8,128)(2,1)} %cot_ref.1, bf16[2,512,384]{2,1,0:T(8,128)(2,1)S(1)} %collective-permute-done.8.in_ref.partner_ref, ...), custom_call_target="tpu_custom_call" | custom-call | flops 1811939328 | bytes 12582912 | tf_op jit(solution)/shard_map/backward/pallas_call | solution.py:341
  (46 shorter events, 11.1 us)
Async XLA Ops:
  19.3 22.2 %copy-start.9 = (bf16[512,768]{1,0:T(8,128)(2,1)}, bf16[512,768]{1,0:T(8,128)(2,1)S(1)}, u32[]{:S(2)}) copy-start(bf16[512,768]{1,0:T(8,128)(2,1)S(1)} %get-tuple-element.18.refs_2_) | copy-start | bytes 2359300
  19.4 53.6 %copy-start.10 = (bf16[512,768]{1,0:T(8,128)(2,1)}, bf16[512,768]{1,0:T(8,128)(2,1)S(1)}, u32[]{:S(2)}) copy-start(bf16[512,768]{1,0:T(8,128)(2,1)S(1)} %get-tuple-element.19.refs_3_) | copy-start | bytes 2359300
  19.4 22.2 %collective-permute-start = (bf16[512,768]{1,0:T(8,128)(2,1)S(1)}, bf16[512,768]{1,0:T(8,128)(2,1)S(1)}, u32[]{:S(2)}, u32[]{:S(2)}) collective-permute-start(bf16[512,768]{1,0:T(8,128)(2,1)S(1)} %get-tuple-element.18.refs_2_), channel_id=1, source_target_pairs={{0,2},{2,0},{1,3},{3,1},{4,6},{6,4},{5,7},{7,5},{8,10},{10,8},{9,1... | collective-permute-start | bytes 2359304 | tf_op jit(solution)/shard_map/ppermute | solution.py:363
  23.7 30.2 %all-to-all-start.2 = ((bf16[4,48,768]{2,1,0:T(8,128)(2,1)}), bf16[4,48,768]{2,1,0:T(8,128)(2,1)S(1)}, u32[]{:S(2)}, u32[]{:S(2)}) async-start(bf16[4,48,768]{2,1,0:T(8,128)(2,1)} %assemble.1), calls=%async_computation.2 | async-start | bytes 589824 | tf_op jit(solution)/shard_map/all_to_all | solution.py:397
  37.7 23.7 %collective-permute-start.2 = (bf16[512,768]{1,0:T(8,128)(2,1)S(1)}, bf16[512,768]{1,0:T(8,128)(2,1)S(1)}, u32[]{:S(2)}, u32[]{:S(2)}) collective-permute-start(bf16[512,768]{1,0:T(8,128)(2,1)S(1)} %get-tuple-element.19.refs_3_), channel_id=1, source_target_pairs={{0,2},{2,0},{1,3},{3,1},{4,6},{6,4},{5,7},{7,5},{8,10},{10,8},{9,1... | collective-permute-start | bytes 2359304 | tf_op jit(solution)/shard_map/ppermute | solution.py:363
  41.6 33.5 %copy-start.2 = (bf16[512,768]{1,0:T(8,128)(2,1)}, bf16[512,768]{1,0:T(8,128)(2,1)S(1)}, u32[]{:S(2)}) copy-start(bf16[512,768]{1,0:T(8,128)(2,1)S(1)} %collective-permute-done.refs_0_.refs_4_) | copy-start | bytes 2359300
  41.6 31.4 %collective-permute-start.1 = (bf16[512,768]{1,0:T(8,128)(2,1)S(1)}, bf16[512,768]{1,0:T(8,128)(2,1)S(1)}, u32[]{:S(2)}, u32[]{:S(2)}) collective-permute-start(bf16[512,768]{1,0:T(8,128)(2,1)S(1)} %collective-permute-done.refs_0_.refs_4_), channel_id=1, source_target_pairs={{0,4},{4,8},{8,12},{6,2},{10,6},{14,10},{1,5},{5,9},{9,13},{7,3},{... | collective-permute-start | bytes 2359304 | tf_op jit(solution)/shard_map/ppermute | solution.py:369
  54.0 19.0 %collective-permute-start.4 = (bf16[4,48,768]{2,1,0:T(8,128)(2,1)S(1)}, bf16[4,48,768]{2,1,0:T(8,128)(2,1)S(1)}, u32[]{:S(2)}, u32[]{:S(2)}) collective-permute-start(bf16[4,48,768]{2,1,0:T(8,128)(2,1)S(1)} %once.4), channel_id=1, source_target_pairs={{0,64},{32,96},{64,0},{96,32},{1,65},{33,97},{65,1},{97,33},{2,66}... | collective-permute-start | bytes 884744 | tf_op jit(solution)/shard_map/ppermute | solution.py:374
  61.5 13.6 %copy-start.3 = (bf16[512,768]{1,0:T(8,128)(2,1)}, bf16[512,768]{1,0:T(8,128)(2,1)S(1)}, u32[]{:S(2)}) copy-start(bf16[512,768]{1,0:T(8,128)(2,1)S(1)} %collective-permute-done.2.refs_1_.refs_5_) | copy-start | bytes 2359300
  61.5 17.5 %collective-permute-start.3 = (bf16[512,768]{1,0:T(8,128)(2,1)S(1)}, bf16[512,768]{1,0:T(8,128)(2,1)S(1)}, u32[]{:S(2)}, u32[]{:S(2)}) collective-permute-start(bf16[512,768]{1,0:T(8,128)(2,1)S(1)} %collective-permute-done.2.refs_1_.refs_5_), channel_id=1, source_target_pairs={{0,4},{4,8},{8,12},{6,2},{10,6},{14,10},{1,5},{5,9},{9,13},{7,3},{... | collective-permute-start | bytes 2359304 | tf_op jit(solution)/shard_map/ppermute | solution.py:369
  73.9 1.1 copy-start.5
  75.1 31.9 %copy-start = (bf16[2,4,48,768]{3,2,1,0:T(8,128)(2,1)}, bf16[2,4,48,768]{3,2,1,0:T(8,128)(2,1)S(1)}, u32[]{:S(2)}) copy-start(bf16[2,4,48,768]{3,2,1,0:T(8,128)(2,1)S(1)} %once.5.refs_7_.refs_0_) | copy-start | bytes 1769476
  75.1 15.4 %collective-permute-start.5 = (bf16[2,4,48,768]{3,2,1,0:T(8,128)(2,1)S(1)}, bf16[2,4,48,768]{3,2,1,0:T(8,128)(2,1)S(1)}, u32[]{:S(2)}, u32[]{:S(2)}) collective-permute-start(bf16[2,4,48,768]{3,2,1,0:T(8,128)(2,1)S(1)} %once.5.refs_7_.refs_0_), channel_id=1, source_target_pairs={{0,32},{32,0},{64,96},{96,64},{1,33},{33,1},{65,97},{97,65},{2,34}... | collective-permute-start | bytes 1769480 | tf_op jit(solution)/shard_map/ppermute | solution.py:374
  77.0 16.4 %collective-permute-start.6 = (bf16[2,4,48,768]{3,2,1,0:T(8,128)(2,1)S(1)}, bf16[2,4,48,768]{3,2,1,0:T(8,128)(2,1)S(1)}, u32[]{:S(2)}, u32[]{:S(2)}) collective-permute-start(bf16[2,4,48,768]{3,2,1,0:T(8,128)(2,1)S(1)} %once.5.refs_7_.refs_0_), channel_id=1, source_target_pairs={{0,1},{1,0},{2,3},{3,2},{4,5},{5,4},{6,7},{7,6},{8,9},{9,8},{10,11... | collective-permute-start | bytes 1769480 | tf_op jit(solution)/shard_map/ppermute | solution.py:378
  91.5 15.5 %copy-start.1 = (bf16[2,4,48,768]{3,2,1,0:T(8,128)(2,1)}, bf16[2,4,48,768]{3,2,1,0:T(8,128)(2,1)S(1)}, u32[]{:S(2)}) copy-start(bf16[2,4,48,768]{3,2,1,0:T(8,128)(2,1)S(1)} %once.6.refs_8_.refs_1_) | copy-start | bytes 1769476
  91.5 3.9 %collective-permute-start.7 = (bf16[2,4,48,768]{3,2,1,0:T(8,128)(2,1)S(1)}, bf16[2,4,48,768]{3,2,1,0:T(8,128)(2,1)S(1)}, u32[]{:S(2)}, u32[]{:S(2)}) collective-permute-start(bf16[2,4,48,768]{3,2,1,0:T(8,128)(2,1)S(1)} %once.6.refs_8_.refs_1_), channel_id=1, source_target_pairs={{0,1},{1,0},{2,3},{3,2},{4,5},{5,4},{6,7},{7,6},{8,9},{9,8},{10,11... | collective-permute-start | bytes 1769480 | tf_op jit(solution)/shard_map/ppermute | solution.py:378
  93.5 13.5 %copy-start.7 = (bf16[2,4,48,768]{3,2,1,0:T(8,128)(2,1)}, bf16[2,4,48,768]{3,2,1,0:T(8,128)(2,1)S(1)}, u32[]{:S(2)}) copy-start(bf16[2,4,48,768]{3,2,1,0:T(8,128)(2,1)S(1)} %collective-permute-done.6.refs_9_.refs_2_) | copy-start | bytes 1769476
  95.4 11.7 %copy-start.8 = (bf16[2,4,48,768]{3,2,1,0:T(8,128)(2,1)}, bf16[2,4,48,768]{3,2,1,0:T(8,128)(2,1)S(1)}, u32[]{:S(2)}) copy-start(bf16[2,4,48,768]{3,2,1,0:T(8,128)(2,1)S(1)} %collective-permute-done.7.refs_10_.refs_3_) | copy-start | bytes 1769476
  107.0 5.9 %collective-permute-start.9 = (bf16[4,3,48,768]{3,2,1,0:T(8,128)(2,1)}, bf16[4,3,48,768]{3,2,1,0:T(8,128)(2,1)S(1)}, u32[]{:S(2)}, u32[]{:S(2)}) collective-permute-start(bf16[4,3,48,768]{3,2,1,0:T(8,128)(2,1)} %get-tuple-element.21), channel_id=1, source_target_pairs={{0,1},{1,0},{2,3},{3,2},{4,5},{5,4},{6,7},{7,6},{8,9},{9,8},{10,11... | collective-permute-start | bytes 2654216 | tf_op jit(solution)/shard_map/ppermute | solution.py:378
  109.1 28.9 %collective-permute-start.8 = (bf16[2,512,384]{2,1,0:T(8,128)(2,1)S(1)}, bf16[2,512,384]{2,1,0:T(8,128)(2,1)S(1)}, u32[]{:S(2)}, u32[]{:S(2)}) collective-permute-start(bf16[2,512,384]{2,1,0:T(8,128)(2,1)S(1)} %get-tuple-element.20.pre_ref), channel_id=1, source_target_pairs={{0,2},{2,0},{1,3},{3,1},{4,6},{6,4},{5,7},{7,5},{8,10},{10,8},{9,1... | collective-permute-start | bytes 2359304 | tf_op jit(solution)/shard_map/ppermute | solution.py:363
  130.9 1.1 copy-start.11
  132.0 24.7 %all-to-all-start.3 = ((bf16[16,3,24,128]{3,2,1,0:T(8,128)(2,1)}), bf16[16,3,24,128]{3,2,1,0:T(8,128)(2,1)S(1)}, u32[]{:S(2)}, u32[]{:S(2)}) async-start(bf16[16,3,24,128]{3,2,1,0:T(8,128)(2,1)} %by_channel.1), calls=%async_computation.3 | async-start | bytes 589824 | tf_op jit(solution)/shard_map/all_to_all | solution.py:420
  138.1 24.4 %collective-permute-start.10 = (bf16[2,512,384]{2,1,0:T(8,128)(2,1)S(1)}, bf16[2,512,384]{2,1,0:T(8,128)(2,1)S(1)}, u32[]{:S(2)}, u32[]{:S(2)}) collective-permute-start(bf16[2,512,384]{2,1,0:T(8,128)(2,1)S(1)} %once.7), channel_id=1, source_target_pairs={{0,4},{4,8},{8,12},{6,2},{10,6},{14,10},{1,5},{5,9},{9,13},{7,3},{... | collective-permute-start | bytes 2359304 | tf_op jit(solution)/shard_map/ppermute | solution.py:369
  157.5 14.7 %all-to-all-start.4 = ((bf16[4,24,128]{2,1,0:T(8,128)(2,1)}), bf16[4,24,128]{2,1,0:T(8,128)(2,1)S(1)}, u32[]{:S(2)}, u32[]{:S(2)}) async-start(bf16[4,24,128]{2,1,0:T(8,128)(2,1)} %add_parts.1), calls=%async_computation.4 | async-start | bytes 49152 | tf_op jit(solution)/shard_map/all_to_all | solution.py:425
  (2 other events, 1.8 us)

commit v8 on v7

--- a/solution.py
+++ b/solution.py
@@ -9,6 +9,7 @@
 from jax.sharding import PartitionSpec as P
 
 LANES = 128
+SUBLANES = 8
 X_PARTS, Y_PARTS, Z_PARTS, CORES = 4, 2, 4, 2
 MIB = 1024 * 1024
 
@@ -79,6 +80,10 @@
         cost_estimate=cost(0, 4 * array.size),
         name="once",
     )(array, *after)
+
+
+def corner(array):
+    return array[: 2 * SUBLANES, :LANES]
 
 
 def held(stage, *args):
@@ -237,14 +242,13 @@
                     block = ref[high, zh]
                     for tap, role in enumerate(roles(yh)):
                         joined[role, rows, columns] = block[:, tap * half : (tap + 1) * half]
-                    if point is not None:
-                        point[rows, columns] = block[:, 3 * half :]
+                    point[rows, columns] = block[:, 3 * half :]
 
 
 def forward_kernel(scale, samples, at_ref, *refs):
     count = 3 * samples + 1
     far_refs, packed, refs = refs[:count], refs[count : count + 4], refs[count + 4 :]
-    pre_ref, own_out, other_out, acts, cot, weights, point, turned, sems = refs
+    pre_ref, own_out, other_out, weights_out, acts, cot, weights, point, turned, sems = refs
     _, bins, width = cot.shape
     half = weights.shape[2] // CORES
     near_refs = [acts.at[i] for i in range(3 * samples)] + [cot]
@@ -258,6 +262,8 @@
         if sample == 0:
             copies[count - 1].start()
     join_weights((packed[:2], packed[2:]), weights, point, at_ref[0], at_ref[1])
+    keep = pltpu.make_async_copy(weights, weights_out, sems.at[count])
+    keep.start()
     for sample in range(samples):
         for role in range(3):
             copies[role * samples + sample].wait()
@@ -270,15 +276,14 @@
         grad_inner = dot(cot[sample], point[...], 1, 0)
         grad_pre = grad_inner * gelu_slope(preact)
         pre_ref[sample] = grad_pre.astype(jnp.bfloat16)
-        turned[sample] = grad_pre.T.astype(jnp.bfloat16)
+        turned[:, pl.ds(sample * bins, bins)] = grad_pre.T.astype(jnp.bfloat16)
     for role, tap in enumerate(roles(at_ref[0])):
-        term = sum(
-            dot(turned[sample], acts[role * samples + sample], 1, 0) for sample in range(samples)
-        )
-        term = term * scale
+        block = acts[pl.ds(role * samples, samples)].reshape(samples * bins, width)
+        term = dot(turned[...], block, 1, 0) * scale
         own_out[:, tap] = term[:half].reshape(own_out.shape[0], -1, width)
         other = term[half:].astype(jnp.bfloat16)
         other_out[:, tap] = other.reshape(other_out.shape[0], -1, width)
+    keep.wait()
 
 
 def forward(at, acts, cotangent, own_w, other_w, scale):
@@ -289,19 +294,20 @@
     return pl.pallas_call(
         functools.partial(forward_kernel, scale, samples),
         in_specs=[IN_SMEM] + [IN_HBM] * (count + 1) + [IN_VMEM] * 4,
-        out_specs=[IN_VMEM] * 3,
+        out_specs=[IN_VMEM] * 3 + [IN_HBM],
         out_shape=[
             struct((samples, bins, hidden), jnp.bfloat16),
             struct(half, jnp.float32),
             struct(half, jnp.bfloat16),
+            struct((3, width, hidden), jnp.bfloat16),
         ],
         scratch_shapes=[
             pltpu.VMEM((count, bins, width), jnp.bfloat16),
             pltpu.VMEM(cotangent.shape, jnp.bfloat16),
             pltpu.VMEM((3, width, hidden), jnp.bfloat16),
             pltpu.VMEM((width, hidden), jnp.bfloat16),
-            pltpu.VMEM((samples, hidden, bins), jnp.bfloat16),
-            pltpu.SemaphoreType.DMA((count + 1,)),
+            pltpu.VMEM((hidden, samples * bins), jnp.bfloat16),
+            pltpu.SemaphoreType.DMA((count + 2,)),
         ],
         compiler_params=params(30),
         cost_estimate=cost(14 * samples * bins * width * hidden, 16 * samples * bins * width),
@@ -309,14 +315,8 @@
     )(at, *[in_hbm(array) for array in (*acts, cotangent)], *own_w, *other_w)
 
 
-def backward_kernel(at_ref, in_ref, cot_ref, partner_ref, pre_ref, handed_ref, *refs):
-    packed, (out_ref, token_ref, weights) = refs[:4], refs[4:]
-
-    @pl.when(pl.program_id(0) == 0)
-    def _():
-        join_weights((packed[:2], packed[2:]), weights, None, at_ref[0], at_ref[1])
-        token_ref[...] = jnp.zeros_like(token_ref)
-
+def backward_kernel(in_ref, cot_ref, partner_ref, pre_ref, handed_ref, weights, out_ref, token_ref):
+    token_ref[...] = jnp.zeros_like(token_ref)
     for sample in range(in_ref.shape[0]):
         grad_act = (
             dot(partner_ref[sample], weights[0], 1, 1)
@@ -330,33 +330,22 @@
         out_ref[sample] = grad.astype(out_ref.dtype)
 
 
-def backward(at, inputs, cotangent, partner, grad_pre, handed, packed, block):
+def backward(inputs, cotangent, partner, grad_pre, handed, weights, block):
     samples, bins, width = inputs.shape
     hidden = grad_pre.shape[2]
     wide = pl.BlockSpec((samples, block, width), lambda i: (0, i, 0))
     narrow = pl.BlockSpec((samples, block, hidden), lambda i: (0, i, 0))
-    whole = pl.BlockSpec(
-        packed[0].shape, lambda i: (0, 0, 0, 0), pipeline_mode=pl.Buffered(1)
-    )
+    whole = pl.BlockSpec(weights.shape, lambda i: (0, 0, 0), pipeline_mode=pl.Buffered(1))
     return pl.pallas_call(
         backward_kernel,
         grid=(bins // block,),
-        in_specs=[IN_SMEM, wide, wide, narrow, narrow, narrow] + [whole] * 4,
+        in_specs=[wide, wide, narrow, narrow, narrow, whole],
         out_specs=[wide, pl.BlockSpec((8, LANES), lambda i: (0, 0))],
         out_shape=[struct(inputs.shape, inputs.dtype), struct((8, LANES), jnp.float32)],
-        scratch_shapes=[pltpu.VMEM((3, width, hidden), jnp.bfloat16)],
         compiler_params=params(24),
         cost_estimate=cost(6 * samples * bins * width * hidden, 16 * samples * bins * width),
         name="backward",
-    )(
-        at,
-        in_hbm(inputs),
-        in_hbm(cotangent),
-        partner,
-        grad_pre,
-        handed,
-        *[in_hbm(part) for part in packed],
-    )
+    )(in_hbm(inputs), in_hbm(cotangent), partner, grad_pre, handed, in_hbm(weights))
 
 
 def exchanged(array):
@@ -391,20 +380,20 @@
     packed = pack(in_hbm(conv_weight), in_hbm(point_weight), blocks * Y_PARTS)
     pieces = lax.all_to_all(packed, ("x", "yh", "yl"), 0, 0)
 
-    mids = list(activate(in_hbm(inputs), 128, pieces))
+    mids = list(activate(in_hbm(inputs), 256, pieces))
     partners = [exchanged(mid) for mid in mids]
 
     part = lax.all_to_all(assemble(pieces, f_part, taps + 1)[:far], "zh", 0, 0)
     part = once(part, partners[0])
     handed = [handed_on(partners[0])]
-    two = once(jnp.stack([part, z_pair(part, 2)]), handed[0], partners[1])
+    two = once(jnp.stack([part, z_pair(part, 2)]), corner(handed[0]), partners[1])
     handed.append(handed_on(partners[1]))
     other_two = other_core(two)
-    last = once(z_pair(two, 1), handed[1])
-
-    packed = (two, last, other_two, other_core(last))
-
-    grad_pre, own, other = forward(
+    last = once(z_pair(two, 1), corner(handed[1]))
+
+    packed = (two, last, other_two, in_hbm(other_core(last)))
+
+    grad_pre, own, other, weights = forward(
         at, handed + mids + partners, cotangent, packed[:2], packed[2:], grad_scale
     )
 
@@ -419,7 +408,7 @@
 
     parts = lax.all_to_all(by_channel(parts, depth), ("zh", "zl"), 0, 0)
     input_grad, token = backward(
-        at, inputs, cotangent, grad_partner, grad_pre, grad_handed, packed, 256
+        inputs, cotangent, grad_partner, grad_pre, grad_handed, weights, 256
     )
     sums = add_parts(parts, f_part)
     conv_grad = finish(lax.all_to_all(sums, ("yh", "yl"), 0, 0), taps, f_part, token)

time: 174 us -> 172 us (0.989)
  Pallas kernels: 28.9 us -> 27.1 us
  transfers between devices with their start and end apart: 14 -> 14, of which waited for: 5 -> 6; matrix products, arithmetic and copies ran while one was open for 1% -> 1% of each run, Pallas kernels for 7% -> 6%
where the time goes in v8:
time: 172 us; the launch traced here: 171 us
  starting transfers between devices  59.9 us (35%)
  waiting for transfers between devices  47.6 us (28%)
  blocking collectives  30.9 us (18%)
  Pallas kernels  27.1 us (16%)
  local copies, waits for them, and re-layouts  2.71 us (2%)
  other arithmetic  1.8 us (1%)
    ppermute x2, waiting for transfers between devices, z_pair(): return lax.ppermute(array, 'zl', [(i, i ^ bit) for i in range(near)])  19.5 us
    all_to_all x1, blocking collectives, first_sums(): return lax.all_to_all(pair.astype(jnp.bfloat16), 'x', 0, 0)  16.3 us
    all_to_all x1, waiting for transfers between devices, body(): parts = lax.all_to_all(by_channel(parts, depth), ('zh', 'zl'), 0, 0)  16.1 us
    all_to_all x1, blocking collectives, body(): pieces = lax.all_to_all(packed, ('x', 'yh', 'yl'), 0, 0)  14.6 us
    all_to_all x1, starting transfers between devices, body(): part = lax.all_to_all(assemble(pieces, f_part, taps + 1)[:far], 'zh', 0, 0)  14 us
    pallas_call x1, Pallas kernels, forward(): pl.pallas_call(functools.partial(forward_kernel, scale, samples), in_spec...  12.1 us
    ppermute x3, starting transfers between devices, exchanged(): return lax.ppermute(array, 'yh', [(0, 1), (1, 0)])  11.2 us
    ppermute x2, starting transfers between devices, z_pair(): return lax.ppermute(array, 'zl', [(i, i ^ bit) for i in range(near)])  9.39 us
  transfers between devices with their start and end apart: 14, of which 6 were waited for; matrix products, arithmetic and copies ran while one was open for 1% of the time, Pallas kernels for 6%

profile of v8, /device:TPU:8, one launch (start us, length us, event | category | flops | bytes accessed | tf_op | source)
XLA Modules:
  0.0 171.0 jit_solution(8627196099883858205)
XLA Ops:
  1.5 14.6 %all_to_all.25._.in_ref = bf16[16,24,128]{2,1,0:T(8,128)(2,1)S(1)} all-to-all(bf16[16,24,128]{2,1,0:T(8,128)(2,1)S(1)} %pack.1), channel_id=1, replica_groups=mesh['zh'=4,'zl'=4,'yl'=2,'x'=4,'yh'=2,'core'=2] {'x','yh','yl'}, dimensions={0} | all-to-all | bytes 196608 | tf_op jit(solution)/shard_map/all_to_all | solution.py:381
  16.1 2.6 %activate.1 = (bf16[512,768]{1,0:T(8,128)(2,1)S(1)}, bf16[512,768]{1,0:T(8,128)(2,1)S(1)}) custom-call(bf16[2,512,768]{2,1,0:T(8,128)(2,1)} %in_ref.3, bf16[16,24,128]{2,1,0:T(8,128)(2,1)S(1)} %all_to_all.25._.in_ref), custom_call_target="tpu_custom_call" | custom-call | flops 15728640 | bytes 3145728 | tf_op jit(solution)/shard_map/activate/pallas_call | solution.py:216
  18.8 3.5 %collective-permute-start = (bf16[512,768]{1,0:T(8,128)(2,1)S(1)}, bf16[512,768]{1,0:T(8,128)(2,1)S(1)}, u32[]{:S(2)}, u32[]{:S(2)}) collective-permute-start(bf16[512,768]{1,0:T(8,128)(2,1)S(1)} %get-tuple-element.19.refs_2_), channel_id=1, source_target_pairs={{0,2},{2,0},{1,3},{3,1},{4,6},{6,4},{5,7},{7,5},{8,10},{10,8},{9,1... | collective-permute-start | bytes 2359304 | tf_op jit(solution)/shard_map/ppermute | solution.py:352
  23.1 14.0 %all-to-all-start.2 = ((bf16[4,48,768]{2,1,0:T(8,128)(2,1)}), bf16[4,48,768]{2,1,0:T(8,128)(2,1)S(1)}, u32[]{:S(2)}, u32[]{:S(2)}) async-start(bf16[4,48,768]{2,1,0:T(8,128)(2,1)} %assemble.1), calls=%async_computation.2 | async-start | bytes 589824 | tf_op jit(solution)/shard_map/all_to_all | solution.py:386
  37.1 3.8 %collective-permute-start.2 = (bf16[512,768]{1,0:T(8,128)(2,1)S(1)}, bf16[512,768]{1,0:T(8,128)(2,1)S(1)}, u32[]{:S(2)}, u32[]{:S(2)}) collective-permute-start(bf16[512,768]{1,0:T(8,128)(2,1)S(1)} %get-tuple-element.20.refs_3_), channel_id=1, source_target_pairs={{0,2},{2,0},{1,3},{3,1},{4,6},{6,4},{5,7},{7,5},{8,10},{10,8},{9,1... | collective-permute-start | bytes 2359304 | tf_op jit(solution)/shard_map/ppermute | solution.py:352
  41.0 3.3 %collective-permute-start.1 = (bf16[512,768]{1,0:T(8,128)(2,1)S(1)}, bf16[512,768]{1,0:T(8,128)(2,1)}, u32[]{:S(2)}, u32[]{:S(2)}) collective-permute-start(bf16[512,768]{1,0:T(8,128)(2,1)S(1)} %collective-permute-done.refs_0_.refs_4_), channel_id=1, source_target_pairs={{0,4},{4,8},{8,12},{6,2},{10,6},{14,10},{1,5},{5,9},{9,13},{7,3},{... | collective-permute-start | bytes 2359304 | tf_op jit(solution)/shard_map/ppermute | solution.py:358
  44.3 9.1 %all-to-all-done.2.in_ref = bf16[4,48,768]{2,1,0:T(8,128)(2,1)S(1)} async-done(((bf16[4,48,768]{2,1,0:T(8,128)(2,1)}), bf16[4,48,768]{2,1,0:T(8,128)(2,1)S(1)}, u32[]{:S(2)}, u32[]{:S(2)}) %all-to-all-start.2) | async-done | bytes 294944 | tf_op jit(solution)/shard_map/all_to_all | solution.py:386
  53.4 7.5 %collective-permute-start.4 = (bf16[4,48,768]{2,1,0:T(8,128)(2,1)S(1)}, bf16[4,48,768]{2,1,0:T(8,128)(2,1)S(1)}, u32[]{:S(2)}, u32[]{:S(2)}) collective-permute-start(bf16[4,48,768]{2,1,0:T(8,128)(2,1)S(1)} %once.4), channel_id=1, source_target_pairs={{0,64},{32,96},{64,0},{96,32},{1,65},{33,97},{65,1},{97,33},{2,66}... | collective-permute-start | bytes 884744 | tf_op jit(solution)/shard_map/ppermute | solution.py:363
  60.9 2.5 %collective-permute-start.3 = (bf16[512,768]{1,0:T(8,128)(2,1)S(1)}, bf16[512,768]{1,0:T(8,128)(2,1)S(1)}, u32[]{:S(2)}, u32[]{:S(2)}) collective-permute-start(bf16[512,768]{1,0:T(8,128)(2,1)S(1)} %collective-permute-done.2.refs_1_.refs_5_), channel_id=1, source_target_pairs={{0,4},{4,8},{8,12},{6,2},{10,6},{14,10},{1,5},{5,9},{9,13},{7,3},{... | collective-permute-start | bytes 2359304 | tf_op jit(solution)/shard_map/ppermute | solution.py:358
  63.4 9.0 %collective-permute-done.4 = bf16[4,48,768]{2,1,0:T(8,128)(2,1)S(1)} collective-permute-done((bf16[4,48,768]{2,1,0:T(8,128)(2,1)S(1)}, bf16[4,48,768]{2,1,0:T(8,128)(2,1)S(1)}, u32[]{:S(2)}, u32[]{:S(2)}) %collective-permute-start.4) | collective-permute-done | bytes 294944 | tf_op jit(solution)/shard_map/ppermute | solution.py:363
  73.2 1.9 %collective-permute-start.5 = (bf16[2,4,48,768]{3,2,1,0:T(8,128)(2,1)S(1)}, bf16[2,4,48,768]{3,2,1,0:T(8,128)(2,1)S(1)}, u32[]{:S(2)}, u32[]{:S(2)}) collective-permute-start(bf16[2,4,48,768]{3,2,1,0:T(8,128)(2,1)S(1)} %once.5.refs_7_), channel_id=1, source_target_pairs={{0,32},{32,0},{64,96},{96,64},{1,33},{33,1},{65,97},{97,65},{2,34}... | collective-permute-start | bytes 1769480 | tf_op jit(solution)/shard_map/ppermute | solution.py:363
  75.1 1.9 %collective-permute-start.6 = (bf16[2,4,48,768]{3,2,1,0:T(8,128)(2,1)S(1)}, bf16[2,4,48,768]{3,2,1,0:T(8,128)(2,1)}, u32[]{:S(2)}, u32[]{:S(2)}) collective-permute-start(bf16[2,4,48,768]{3,2,1,0:T(8,128)(2,1)S(1)} %once.5.refs_7_), channel_id=1, source_target_pairs={{0,1},{1,0},{2,3},{3,2},{4,5},{5,4},{6,7},{7,6},{8,9},{9,8},{10,11... | collective-permute-start | bytes 1769480 | tf_op jit(solution)/shard_map/ppermute | solution.py:367
  78.0 10.6 %collective-permute-done.5.in_ref = bf16[2,4,48,768]{3,2,1,0:T(8,128)(2,1)S(1)} collective-permute-done((bf16[2,4,48,768]{3,2,1,0:T(8,128)(2,1)S(1)}, bf16[2,4,48,768]{3,2,1,0:T(8,128)(2,1)S(1)}, u32[]{:S(2)}, u32[]{:S(2)}) %collective-permute-start.5) | collective-permute-done | bytes 589856 | tf_op jit(solution)/shard_map/ppermute | solution.py:363
  88.7 1.9 %collective-permute-start.7 = (bf16[2,4,48,768]{3,2,1,0:T(8,128)(2,1)S(1)}, bf16[2,4,48,768]{3,2,1,0:T(8,128)(2,1)S(1)}, u32[]{:S(2)}, u32[]{:S(2)}) collective-permute-start(bf16[2,4,48,768]{3,2,1,0:T(8,128)(2,1)S(1)} %once.6.refs_8_), channel_id=1, source_target_pairs={{0,1},{1,0},{2,3},{3,2},{4,5},{5,4},{6,7},{7,6},{8,9},{9,8},{10,11... | collective-permute-start | bytes 1769480 | tf_op jit(solution)/shard_map/ppermute | solution.py:367
  93.4 12.1 %forward.1 = (bf16[2,512,384]{2,1,0:T(8,128)(2,1)S(1)}, f32[4,3,48,768]{3,2,1,0:T(8,128)}, bf16[4,3,48,768]{3,2,1,0:T(8,128)(2,1)}, bf16[3,768,384]{2,1,0:T(8,128)(2,1)S(1)}) custom-call(s32[2]{0:T(128)S(1)} %pad_add_fusion.at_ref, bf16[512,768]{1,0:T(8,128)(2,1)} %collective-permute-done.1.refs_0_, bf16[512,768]{1,0:T(8,128)(2,1)} %copy-done.6, ...), custom_call_target="tpu_custom_call" | custom-call | flops 4227858432 | bytes 12582912 | tf_op jit(solution)/shard_map/forward/pallas_call | solution.py:294
  106.7 2.0 %collective-permute-start.9 = (bf16[4,3,48,768]{3,2,1,0:T(8,128)(2,1)}, bf16[4,3,48,768]{3,2,1,0:T(8,128)(2,1)S(1)}, u32[]{:S(2)}, u32[]{:S(2)}) collective-permute-start(bf16[4,3,48,768]{3,2,1,0:T(8,128)(2,1)} %get-tuple-element.22), channel_id=1, source_target_pairs={{0,1},{1,0},{2,3},{3,2},{4,5},{5,4},{6,7},{7,6},{8,9},{9,8},{10,11... | collective-permute-start | bytes 2654216 | tf_op jit(solution)/shard_map/ppermute | solution.py:367
  108.8 3.9 %collective-permute-start.8 = (bf16[2,512,384]{2,1,0:T(8,128)(2,1)S(1)}, bf16[2,512,384]{2,1,0:T(8,128)(2,1)S(1)}, u32[]{:S(2)}, u32[]{:S(2)}) collective-permute-start(bf16[2,512,384]{2,1,0:T(8,128)(2,1)S(1)} %get-tuple-element.21.pre_ref), channel_id=1, source_target_pairs={{0,2},{2,0},{1,3},{3,1},{4,6},{6,4},{5,7},{7,5},{8,10},{10,8},{9,1... | collective-permute-start | bytes 2359304 | tf_op jit(solution)/shard_map/ppermute | solution.py:352
  112.6 17.9 %conditional.1 = (bf16[4,3,48,768]{3,2,1,0:T(8,128)(2,1)S(1)}) conditional(s32[]{:T(128)} %convert_element_type.9, () %tuple.14, (bf16[4,3,48,768]{3,2,1,0:T(8,128)(2,1)S(1)}, f32[4,3,48,768]{3,2,1,0:T(8,128)}) %tuple.15), branch_computations={%region_0.0_spmd, %region_1.0_spmd} | conditional | flops 1327104 | bytes 5308424 | solution.py:94
  114.3 16.3 %all_to_all.24 = bf16[4,3,48,768]{3,2,1,0:T(8,128)(2,1)S(1)} all-to-all(bf16[4,3,48,768]{3,2,1,0:T(8,128)(2,1)S(1)} %add_convert_fusion), channel_id=1, replica_groups=mesh['zh'=4,'zl'=4,'yl'=2,'x'=4,'yh'=2,'core'=2] {'x'}, dimensions={0} | all-to-all | bytes 1769472 | tf_op jit(solution)/shard_map/cond/branch_1_fun/all_to_all | solution.py:402
  131.7 6.0 %all-to-all-start.3 = ((bf16[16,3,24,128]{3,2,1,0:T(8,128)(2,1)}), bf16[16,3,24,128]{3,2,1,0:T(8,128)(2,1)S(1)}, u32[]{:S(2)}, u32[]{:S(2)}) async-start(bf16[16,3,24,128]{3,2,1,0:T(8,128)(2,1)} %by_channel.1), calls=%async_computation.3 | async-start | bytes 589824 | tf_op jit(solution)/shard_map/all_to_all | solution.py:409
  137.8 2.5 %collective-permute-start.10 = (bf16[2,512,384]{2,1,0:T(8,128)(2,1)S(1)}, bf16[2,512,384]{2,1,0:T(8,128)(2,1)S(1)}, u32[]{:S(2)}, u32[]{:S(2)}) collective-permute-start(bf16[2,512,384]{2,1,0:T(8,128)(2,1)S(1)} %once.7), channel_id=1, source_target_pairs={{0,4},{4,8},{8,12},{6,2},{10,6},{14,10},{1,5},{5,9},{9,13},{7,3},{... | collective-permute-start | bytes 2359304 | tf_op jit(solution)/shard_map/ppermute | solution.py:358
  140.3 16.1 %all-to-all-done.3.in_ref = bf16[16,3,24,128]{3,2,1,0:T(8,128)(2,1)S(1)} async-done(((bf16[16,3,24,128]{3,2,1,0:T(8,128)(2,1)}), bf16[16,3,24,128]{3,2,1,0:T(8,128)(2,1)S(1)}, u32[]{:S(2)}, u32[]{:S(2)}) %all-to-all-start.3) | async-done | bytes 294944 | tf_op jit(solution)/shard_map/all_to_all | solution.py:409
  157.1 5.2 %all-to-all-start.4 = ((bf16[4,24,128]{2,1,0:T(8,128)(2,1)}), bf16[4,24,128]{2,1,0:T(8,128)(2,1)S(1)}, u32[]{:S(2)}, u32[]{:S(2)}) async-start(bf16[4,24,128]{2,1,0:T(8,128)(2,1)} %add_parts.1), calls=%async_computation.4 | async-start | bytes 49152 | tf_op jit(solution)/shard_map/all_to_all | solution.py:414
  162.3 8.0 %backward.1 = (bf16[2,512,768]{2,1,0:T(8,128)(2,1)}, f32[8,128]{1,0:T(8,128)S(1)}) custom-call(bf16[2,512,768]{2,1,0:T(8,128)(2,1)} %in_ref.3, bf16[2,512,768]{2,1,0:T(8,128)(2,1)} %cot_ref.1, bf16[2,512,384]{2,1,0:T(8,128)(2,1)S(1)} %collective-permute-done.8.in_ref.partner_ref, bf16[2,512,384]{2,1,0:T(8,128)(2,1)S(1)} %get-tuple-element.21.pre_ref, ...), custom_call_target="tpu_custom_call" | custom-call | flops 1811939328 | bytes 12582912 | tf_op jit(solution)/shard_map/backward/pallas_call | solution.py:339
  (40 shorter events, 11.9 us)
Async XLA Ops:
  18.7 53.7 %copy-start.3 = (bf16[512,768]{1,0:T(8,128)(2,1)}, bf16[512,768]{1,0:T(8,128)(2,1)S(1)}, u32[]{:S(2)}) copy-start(bf16[512,768]{1,0:T(8,128)(2,1)S(1)} %get-tuple-element.19.refs_2_) | copy-start | bytes 2359300
  18.8 53.7 %copy-start.4 = (bf16[512,768]{1,0:T(8,128)(2,1)}, bf16[512,768]{1,0:T(8,128)(2,1)S(1)}, u32[]{:S(2)}) copy-start(bf16[512,768]{1,0:T(8,128)(2,1)S(1)} %get-tuple-element.20.refs_3_) | copy-start | bytes 2359300
  18.8 22.2 %collective-permute-start = (bf16[512,768]{1,0:T(8,128)(2,1)S(1)}, bf16[512,768]{1,0:T(8,128)(2,1)S(1)}, u32[]{:S(2)}, u32[]{:S(2)}) collective-permute-start(bf16[512,768]{1,0:T(8,128)(2,1)S(1)} %get-tuple-element.19.refs_2_), channel_id=1, source_target_pairs={{0,2},{2,0},{1,3},{3,1},{4,6},{6,4},{5,7},{7,5},{8,10},{10,8},{9,1... | collective-permute-start | bytes 2359304 | tf_op jit(solution)/shard_map/ppermute | solution.py:352
  23.1 30.2 %all-to-all-start.2 = ((bf16[4,48,768]{2,1,0:T(8,128)(2,1)}), bf16[4,48,768]{2,1,0:T(8,128)(2,1)S(1)}, u32[]{:S(2)}, u32[]{:S(2)}) async-start(bf16[4,48,768]{2,1,0:T(8,128)(2,1)} %assemble.1), calls=%async_computation.2 | async-start | bytes 589824 | tf_op jit(solution)/shard_map/all_to_all | solution.py:386
  37.1 23.7 %collective-permute-start.2 = (bf16[512,768]{1,0:T(8,128)(2,1)S(1)}, bf16[512,768]{1,0:T(8,128)(2,1)S(1)}, u32[]{:S(2)}, u32[]{:S(2)}) collective-permute-start(bf16[512,768]{1,0:T(8,128)(2,1)S(1)} %get-tuple-element.20.refs_3_), channel_id=1, source_target_pairs={{0,2},{2,0},{1,3},{3,1},{4,6},{6,4},{5,7},{7,5},{8,10},{10,8},{9,1... | collective-permute-start | bytes 2359304 | tf_op jit(solution)/shard_map/ppermute | solution.py:352
  41.0 32.2 %copy-start.1 = (bf16[512,768]{1,0:T(8,128)(2,1)}, bf16[512,768]{1,0:T(8,128)(2,1)S(1)}, u32[]{:S(2)}) copy-start(bf16[512,768]{1,0:T(8,128)(2,1)S(1)} %collective-permute-done.refs_0_.refs_4_) | copy-start | bytes 2359300
  41.0 31.4 %collective-permute-start.1 = (bf16[512,768]{1,0:T(8,128)(2,1)S(1)}, bf16[512,768]{1,0:T(8,128)(2,1)}, u32[]{:S(2)}, u32[]{:S(2)}) collective-permute-start(bf16[512,768]{1,0:T(8,128)(2,1)S(1)} %collective-permute-done.refs_0_.refs_4_), channel_id=1, source_target_pairs={{0,4},{4,8},{8,12},{6,2},{10,6},{14,10},{1,5},{5,9},{9,13},{7,3},{... | collective-permute-start | bytes 2359304 | tf_op jit(solution)/shard_map/ppermute | solution.py:358
  53.4 19.0 %collective-permute-start.4 = (bf16[4,48,768]{2,1,0:T(8,128)(2,1)S(1)}, bf16[4,48,768]{2,1,0:T(8,128)(2,1)S(1)}, u32[]{:S(2)}, u32[]{:S(2)}) collective-permute-start(bf16[4,48,768]{2,1,0:T(8,128)(2,1)S(1)} %once.4), channel_id=1, source_target_pairs={{0,64},{32,96},{64,0},{96,32},{1,65},{33,97},{65,1},{97,33},{2,66}... | collective-permute-start | bytes 884744 | tf_op jit(solution)/shard_map/ppermute | solution.py:363
  60.9 27.8 %copy-start.2 = (bf16[512,768]{1,0:T(8,128)(2,1)}, bf16[512,768]{1,0:T(8,128)(2,1)S(1)}, u32[]{:S(2)}) copy-start(bf16[512,768]{1,0:T(8,128)(2,1)S(1)} %collective-permute-done.2.refs_1_.refs_5_) | copy-start | bytes 2359300
  60.9 17.2 %collective-permute-start.3 = (bf16[512,768]{1,0:T(8,128)(2,1)S(1)}, bf16[512,768]{1,0:T(8,128)(2,1)S(1)}, u32[]{:S(2)}, u32[]{:S(2)}) collective-permute-start(bf16[512,768]{1,0:T(8,128)(2,1)S(1)} %collective-permute-done.2.refs_1_.refs_5_), channel_id=1, source_target_pairs={{0,4},{4,8},{8,12},{6,2},{10,6},{14,10},{1,5},{5,9},{9,13},{7,3},{... | collective-permute-start | bytes 2359304 | tf_op jit(solution)/shard_map/ppermute | solution.py:358
  73.2 15.4 %collective-permute-start.5 = (bf16[2,4,48,768]{3,2,1,0:T(8,128)(2,1)S(1)}, bf16[2,4,48,768]{3,2,1,0:T(8,128)(2,1)S(1)}, u32[]{:S(2)}, u32[]{:S(2)}) collective-permute-start(bf16[2,4,48,768]{3,2,1,0:T(8,128)(2,1)S(1)} %once.5.refs_7_), channel_id=1, source_target_pairs={{0,32},{32,0},{64,96},{96,64},{1,33},{33,1},{65,97},{97,65},{2,34}... | collective-permute-start | bytes 1769480 | tf_op jit(solution)/shard_map/ppermute | solution.py:363
  75.1 15.6 %collective-permute-start.6 = (bf16[2,4,48,768]{3,2,1,0:T(8,128)(2,1)S(1)}, bf16[2,4,48,768]{3,2,1,0:T(8,128)(2,1)}, u32[]{:S(2)}, u32[]{:S(2)}) collective-permute-start(bf16[2,4,48,768]{3,2,1,0:T(8,128)(2,1)S(1)} %once.5.refs_7_), channel_id=1, source_target_pairs={{0,1},{1,0},{2,3},{3,2},{4,5},{5,4},{6,7},{7,6},{8,9},{9,8},{10,11... | collective-permute-start | bytes 1769480 | tf_op jit(solution)/shard_map/ppermute | solution.py:367
  78.0 12.6 %copy-start.6 = (bf16[512,768]{1,0:T(8,128)(2,1)}, bf16[512,768]{1,0:T(8,128)(2,1)S(1)}, u32[]{:S(2)}) copy-start(bf16[512,768]{1,0:T(8,128)(2,1)S(1)} %collective-permute-done.3.refs_1_) | copy-start | bytes 2359300
  88.7 3.9 %collective-permute-start.7 = (bf16[2,4,48,768]{3,2,1,0:T(8,128)(2,1)S(1)}, bf16[2,4,48,768]{3,2,1,0:T(8,128)(2,1)S(1)}, u32[]{:S(2)}, u32[]{:S(2)}) collective-permute-start(bf16[2,4,48,768]{3,2,1,0:T(8,128)(2,1)S(1)} %once.6.refs_8_), channel_id=1, source_target_pairs={{0,1},{1,0},{2,3},{3,2},{4,5},{5,4},{6,7},{7,6},{8,9},{9,8},{10,11... | collective-permute-start | bytes 1769480 | tf_op jit(solution)/shard_map/ppermute | solution.py:367
  92.6 0.8 copy-start.7
  105.5 1.2 copy-start
  106.7 5.9 %collective-permute-start.9 = (bf16[4,3,48,768]{3,2,1,0:T(8,128)(2,1)}, bf16[4,3,48,768]{3,2,1,0:T(8,128)(2,1)S(1)}, u32[]{:S(2)}, u32[]{:S(2)}) collective-permute-start(bf16[4,3,48,768]{3,2,1,0:T(8,128)(2,1)} %get-tuple-element.22), channel_id=1, source_target_pairs={{0,1},{1,0},{2,3},{3,2},{4,5},{5,4},{6,7},{7,6},{8,9},{9,8},{10,11... | collective-permute-start | bytes 2654216 | tf_op jit(solution)/shard_map/ppermute | solution.py:367
  108.8 28.9 %collective-permute-start.8 = (bf16[2,512,384]{2,1,0:T(8,128)(2,1)S(1)}, bf16[2,512,384]{2,1,0:T(8,128)(2,1)S(1)}, u32[]{:S(2)}, u32[]{:S(2)}) collective-permute-start(bf16[2,512,384]{2,1,0:T(8,128)(2,1)S(1)} %get-tuple-element.21.pre_ref), channel_id=1, source_target_pairs={{0,2},{2,0},{1,3},{3,1},{4,6},{6,4},{5,7},{7,5},{8,10},{10,8},{9,1... | collective-permute-start | bytes 2359304 | tf_op jit(solution)/shard_map/ppermute | solution.py:352
  130.6 7.1 %copy-start.5 = (bf16[4,3,48,768]{3,2,1,0:T(8,128)(2,1)}, bf16[4,3,48,768]{3,2,1,0:T(8,128)(2,1)S(1)}, u32[]{:S(2)}) copy-start(bf16[4,3,48,768]{3,2,1,0:T(8,128)(2,1)S(1)} %get-tuple-element.27.refs_0_.in_ref) | copy-start | bytes 2654212
  131.7 24.7 %all-to-all-start.3 = ((bf16[16,3,24,128]{3,2,1,0:T(8,128)(2,1)}), bf16[16,3,24,128]{3,2,1,0:T(8,128)(2,1)S(1)}, u32[]{:S(2)}, u32[]{:S(2)}) async-start(bf16[16,3,24,128]{3,2,1,0:T(8,128)(2,1)} %by_channel.1), calls=%async_computation.3 | async-start | bytes 589824 | tf_op jit(solution)/shard_map/all_to_all | solution.py:409
  137.8 24.6 %collective-permute-start.10 = (bf16[2,512,384]{2,1,0:T(8,128)(2,1)S(1)}, bf16[2,512,384]{2,1,0:T(8,128)(2,1)S(1)}, u32[]{:S(2)}, u32[]{:S(2)}) collective-permute-start(bf16[2,512,384]{2,1,0:T(8,128)(2,1)S(1)} %once.7), channel_id=1, source_target_pairs={{0,4},{4,8},{8,12},{6,2},{10,6},{14,10},{1,5},{5,9},{9,13},{7,3},{... | collective-permute-start | bytes 2359304 | tf_op jit(solution)/shard_map/ppermute | solution.py:358
  157.1 13.2 %all-to-all-start.4 = ((bf16[4,24,128]{2,1,0:T(8,128)(2,1)}), bf16[4,24,128]{2,1,0:T(8,128)(2,1)S(1)}, u32[]{:S(2)}, u32[]{:S(2)}) async-start(bf16[4,24,128]{2,1,0:T(8,128)(2,1)} %add_parts.1), calls=%async_computation.4 | async-start | bytes 49152 | tf_op jit(solution)/shard_map/all_to_all | solution.py:414

commit v9 on v8

--- a/solution.py
+++ b/solution.py
@@ -248,7 +248,8 @@
 def forward_kernel(scale, samples, at_ref, *refs):
     count = 3 * samples + 1
     far_refs, packed, refs = refs[:count], refs[count : count + 4], refs[count + 4 :]
-    pre_ref, own_out, other_out, weights_out, acts, cot, weights, point, turned, sems = refs
+    pre_ref, own_out, other_out, weights_out, refs = *refs[:4], refs[4:]
+    acts, cot, weights, point, turned, own, other, sems = refs
     _, bins, width = cot.shape
     half = weights.shape[2] // CORES
     near_refs = [acts.at[i] for i in range(3 * samples)] + [cot]
@@ -265,24 +266,31 @@
     keep = pltpu.make_async_copy(weights, weights_out, sems.at[count])
     keep.start()
     for sample in range(samples):
-        for role in range(3):
-            copies[role * samples + sample].wait()
+        handed, mid, partner = [acts.at[role * samples + sample] for role in range(3)]
+        copies[sample].wait()
+        shifted = dot(handed[...], weights[0], 1, 0).astype(jnp.bfloat16).astype(jnp.float32)
+        copies[2 * samples + sample].wait()
+        shifted += dot(partner[...], weights[2], 1, 0).astype(jnp.bfloat16).astype(jnp.float32)
+        copies[samples + sample].wait()
+        preact = shifted + dot(mid[...], weights[1], 1, 0)
         if sample == 0:
             copies[count - 1].wait()
-        handed, mid, partner = [acts[role * samples + sample] for role in range(3)]
-        shifted = dot(handed, weights[0], 1, 0).astype(jnp.bfloat16).astype(jnp.float32)
-        shifted += dot(partner, weights[2], 1, 0).astype(jnp.bfloat16).astype(jnp.float32)
-        preact = shifted + dot(mid, weights[1], 1, 0)
         grad_inner = dot(cot[sample], point[...], 1, 0)
         grad_pre = grad_inner * gelu_slope(preact)
         pre_ref[sample] = grad_pre.astype(jnp.bfloat16)
         turned[:, pl.ds(sample * bins, bins)] = grad_pre.T.astype(jnp.bfloat16)
+    sends = []
     for role, tap in enumerate(roles(at_ref[0])):
         block = acts[pl.ds(role * samples, samples)].reshape(samples * bins, width)
         term = dot(turned[...], block, 1, 0) * scale
-        own_out[:, tap] = term[:half].reshape(own_out.shape[0], -1, width)
-        other = term[half:].astype(jnp.bfloat16)
-        other_out[:, tap] = other.reshape(other_out.shape[0], -1, width)
+        own[role] = term[:half].reshape(own.shape[1:])
+        other[role] = term[half:].astype(jnp.bfloat16).reshape(other.shape[1:])
+        for near_ref, far_ref in ((own, own_out), (other, other_out)):
+            sem = sems.at[count + 1 + len(sends)]
+            sends.append(pltpu.make_async_copy(near_ref.at[role], far_ref.at[:, tap], sem))
+            sends[-1].start()
+    for send in sends:
+        send.wait()
     keep.wait()
 
 
@@ -294,7 +302,7 @@
     return pl.pallas_call(
         functools.partial(forward_kernel, scale, samples),
         in_specs=[IN_SMEM] + [IN_HBM] * (count + 1) + [IN_VMEM] * 4,
-        out_specs=[IN_VMEM] * 3 + [IN_HBM],
+        out_specs=[IN_VMEM] + [ANYWHERE] * 3,
         out_shape=[
             struct((samples, bins, hidden), jnp.bfloat16),
             struct(half, jnp.float32),
@@ -307,7 +315,9 @@
             pltpu.VMEM((3, width, hidden), jnp.bfloat16),
             pltpu.VMEM((width, hidden), jnp.bfloat16),
             pltpu.VMEM((hidden, samples * bins), jnp.bfloat16),
-            pltpu.SemaphoreType.DMA((count + 2,)),
+            pltpu.VMEM((3,) + half[:1] + half[2:], jnp.float32),
+            pltpu.VMEM((3,) + half[:1] + half[2:], jnp.bfloat16),
+            pltpu.SemaphoreType.DMA((count + 2 + 6,)),
         ],
         compiler_params=params(30),
         cost_estimate=cost(14 * samples * bins * width * hidden, 16 * samples * bins * width),
@@ -345,7 +355,7 @@
         compiler_params=params(24),
         cost_estimate=cost(6 * samples * bins * width * hidden, 16 * samples * bins * width),
         name="backward",
-    )(in_hbm(inputs), in_hbm(cotangent), partner, grad_pre, handed, in_hbm(weights))
+    )(in_hbm(inputs), in_hbm(cotangent), partner, grad_pre, handed, weights)
 
 
 def exchanged(array):
@@ -404,7 +414,7 @@
     other = other_core(other)
     grad_partner = exchanged(grad_pre)
     parts = held(first_sums, own, other)
-    grad_handed = handed_on(once(grad_partner, parts))
+    grad_handed = handed_on(once(grad_partner, corner(parts[0, 0])))
 
     parts = lax.all_to_all(by_channel(parts, depth), ("zh", "zl"), 0, 0)
     input_grad, token = backward(

time: 172 us -> 174 us (1.012)
  Pallas kernels: 27.1 us -> 29.1 us
  transfers between devices with their start and end apart: 14 -> 14, of which waited for: 6 -> 6; matrix products, arithmetic and copies ran while one was open for 1% -> 2% of each run, Pallas kernels for 6% -> 7%
where the time goes in v9:
time: 174 us; the launch traced here: 173 us
  starting transfers between devices  61 us (35%)
  waiting for transfers between devices  46.1 us (26%)
  blocking collectives  31.7 us (18%)
  Pallas kernels  29.1 us (17%)
  local copies, waits for them, and re-layouts  2.67 us (2%)
  other arithmetic  1.8 us (1%)
    ppermute x2, waiting for transfers between devices, z_pair(): return lax.ppermute(array, 'zl', [(i, i ^ bit) for i in range(near)])  19.6 us
    all_to_all x1, blocking collectives, first_sums(): return lax.all_to_all(pair.astype(jnp.bfloat16), 'x', 0, 0)  17 us
    all_to_all x1, blocking collectives, body(): pieces = lax.all_to_all(packed, ('x', 'yh', 'yl'), 0, 0)  14.6 us
    all_to_all x1, waiting for transfers between devices, body(): parts = lax.all_to_all(by_channel(parts, depth), ('zh', 'zl'), 0, 0)  14.5 us
    all_to_all x1, starting transfers between devices, body(): part = lax.all_to_all(assemble(pieces, f_part, taps + 1)[:far], 'zh', 0, 0)  14 us
    pallas_call x1, Pallas kernels, forward(): pl.pallas_call(functools.partial(forward_kernel, scale, samples), in_spec...  12.4 us
    ppermute x3, starting transfers between devices, exchanged(): return lax.ppermute(array, 'yh', [(0, 1), (1, 0)])  11.2 us
    ppermute x2, starting transfers between devices, z_pair(): return lax.ppermute(array, 'zl', [(i, i ^ bit) for i in range(near)])  9.39 us
  transfers between devices with their start and end apart: 14, of which 6 were waited for; matrix products, arithmetic and copies ran while one was open for 2% of the time, Pallas kernels for 7%

profile of v9, /device:TPU:8, one launch (start us, length us, event | category | flops | bytes accessed | tf_op | source)
XLA Modules:
  0.0 173.2 jit_solution(6362579351722842797)
XLA Ops:
  1.5 14.6 %all_to_all.25._.in_ref = bf16[16,24,128]{2,1,0:T(8,128)(2,1)S(1)} all-to-all(bf16[16,24,128]{2,1,0:T(8,128)(2,1)S(1)} %pack.1), channel_id=1, replica_groups=mesh['zh'=4,'zl'=4,'yl'=2,'x'=4,'yh'=2,'core'=2] {'x','yh','yl'}, dimensions={0} | all-to-all | bytes 196608 | tf_op jit(solution)/shard_map/all_to_all | solution.py:391
  16.1 2.6 %activate.1 = (bf16[512,768]{1,0:T(8,128)(2,1)S(1)}, bf16[512,768]{1,0:T(8,128)(2,1)S(1)}) custom-call(bf16[2,512,768]{2,1,0:T(8,128)(2,1)} %in_ref.3, bf16[16,24,128]{2,1,0:T(8,128)(2,1)S(1)} %all_to_all.25._.in_ref), custom_call_target="tpu_custom_call" | custom-call | flops 15728640 | bytes 3145728 | tf_op jit(solution)/shard_map/activate/pallas_call | solution.py:216
  18.8 3.5 %collective-permute-start = (bf16[512,768]{1,0:T(8,128)(2,1)S(1)}, bf16[512,768]{1,0:T(8,128)(2,1)S(1)}, u32[]{:S(2)}, u32[]{:S(2)}) collective-permute-start(bf16[512,768]{1,0:T(8,128)(2,1)S(1)} %get-tuple-element.20.refs_2_), channel_id=1, source_target_pairs={{0,2},{2,0},{1,3},{3,1},{4,6},{6,4},{5,7},{7,5},{8,10},{10,8},{9,1... | collective-permute-start | bytes 2359304 | tf_op jit(solution)/shard_map/ppermute | solution.py:362
  23.1 14.0 %all-to-all-start.2 = ((bf16[4,48,768]{2,1,0:T(8,128)(2,1)}), bf16[4,48,768]{2,1,0:T(8,128)(2,1)S(1)}, u32[]{:S(2)}, u32[]{:S(2)}) async-start(bf16[4,48,768]{2,1,0:T(8,128)(2,1)} %assemble.1), calls=%async_computation.2 | async-start | bytes 589824 | tf_op jit(solution)/shard_map/all_to_all | solution.py:396
  37.1 3.8 %collective-permute-start.2 = (bf16[512,768]{1,0:T(8,128)(2,1)S(1)}, bf16[512,768]{1,0:T(8,128)(2,1)S(1)}, u32[]{:S(2)}, u32[]{:S(2)}) collective-permute-start(bf16[512,768]{1,0:T(8,128)(2,1)S(1)} %get-tuple-element.21.refs_3_), channel_id=1, source_target_pairs={{0,2},{2,0},{1,3},{3,1},{4,6},{6,4},{5,7},{7,5},{8,10},{10,8},{9,1... | collective-permute-start | bytes 2359304 | tf_op jit(solution)/shard_map/ppermute | solution.py:362
  41.0 3.3 %collective-permute-start.1 = (bf16[512,768]{1,0:T(8,128)(2,1)S(1)}, bf16[512,768]{1,0:T(8,128)(2,1)}, u32[]{:S(2)}, u32[]{:S(2)}) collective-permute-start(bf16[512,768]{1,0:T(8,128)(2,1)S(1)} %collective-permute-done.refs_0_.refs_4_), channel_id=1, source_target_pairs={{0,4},{4,8},{8,12},{6,2},{10,6},{14,10},{1,5},{5,9},{9,13},{7,3},{... | collective-permute-start | bytes 2359304 | tf_op jit(solution)/shard_map/ppermute | solution.py:368
  44.3 9.0 %all-to-all-done.2.in_ref = bf16[4,48,768]{2,1,0:T(8,128)(2,1)S(1)} async-done(((bf16[4,48,768]{2,1,0:T(8,128)(2,1)}), bf16[4,48,768]{2,1,0:T(8,128)(2,1)S(1)}, u32[]{:S(2)}, u32[]{:S(2)}) %all-to-all-start.2) | async-done | bytes 294944 | tf_op jit(solution)/shard_map/all_to_all | solution.py:396
  53.4 7.5 %collective-permute-start.4 = (bf16[4,48,768]{2,1,0:T(8,128)(2,1)S(1)}, bf16[4,48,768]{2,1,0:T(8,128)(2,1)S(1)}, u32[]{:S(2)}, u32[]{:S(2)}) collective-permute-start(bf16[4,48,768]{2,1,0:T(8,128)(2,1)S(1)} %once.4), channel_id=1, source_target_pairs={{0,64},{32,96},{64,0},{96,32},{1,65},{33,97},{65,1},{97,33},{2,66}... | collective-permute-start | bytes 884744 | tf_op jit(solution)/shard_map/ppermute | solution.py:373
  60.9 2.5 %collective-permute-start.3 = (bf16[512,768]{1,0:T(8,128)(2,1)S(1)}, bf16[512,768]{1,0:T(8,128)(2,1)S(1)}, u32[]{:S(2)}, u32[]{:S(2)}) collective-permute-start(bf16[512,768]{1,0:T(8,128)(2,1)S(1)} %collective-permute-done.2.refs_1_.refs_5_), channel_id=1, source_target_pairs={{0,4},{4,8},{8,12},{6,2},{10,6},{14,10},{1,5},{5,9},{9,13},{7,3},{... | collective-permute-start | bytes 2359304 | tf_op jit(solution)/shard_map/ppermute | solution.py:368
  63.4 9.0 %collective-permute-done.4 = bf16[4,48,768]{2,1,0:T(8,128)(2,1)S(1)} collective-permute-done((bf16[4,48,768]{2,1,0:T(8,128)(2,1)S(1)}, bf16[4,48,768]{2,1,0:T(8,128)(2,1)S(1)}, u32[]{:S(2)}, u32[]{:S(2)}) %collective-permute-start.4) | collective-permute-done | bytes 294944 | tf_op jit(solution)/shard_map/ppermute | solution.py:373
  78.0 10.6 %collective-permute-done.5.in_ref = bf16[2,4,48,768]{3,2,1,0:T(8,128)(2,1)S(1)} collective-permute-done((bf16[2,4,48,768]{3,2,1,0:T(8,128)(2,1)S(1)}, bf16[2,4,48,768]{3,2,1,0:T(8,128)(2,1)S(1)}, u32[]{:S(2)}, u32[]{:S(2)}) %collective-permute-start.5) | collective-permute-done | bytes 589856 | tf_op jit(solution)/shard_map/ppermute | solution.py:373
  88.7 1.9 %collective-permute-start.7 = (bf16[2,4,48,768]{3,2,1,0:T(8,128)(2,1)S(1)}, bf16[2,4,48,768]{3,2,1,0:T(8,128)(2,1)}, u32[]{:S(2)}, u32[]{:S(2)}) collective-permute-start(bf16[2,4,48,768]{3,2,1,0:T(8,128)(2,1)S(1)} %once.6.refs_8_), channel_id=1, source_target_pairs={{0,1},{1,0},{2,3},{3,2},{4,5},{5,4},{6,7},{7,6},{8,9},{9,8},{10,11... | collective-permute-start | bytes 1769480 | tf_op jit(solution)/shard_map/ppermute | solution.py:377
  90.7 2.0 %collective-permute-done.7.refs_10_ = bf16[2,4,48,768]{3,2,1,0:T(8,128)(2,1)} collective-permute-done((bf16[2,4,48,768]{3,2,1,0:T(8,128)(2,1)S(1)}, bf16[2,4,48,768]{3,2,1,0:T(8,128)(2,1)}, u32[]{:S(2)}, u32[]{:S(2)}) %collective-permute-start.7) | collective-permute-done | bytes 589856 | tf_op jit(solution)/shard_map/ppermute | solution.py:377
  93.8 12.4 %forward.1 = (bf16[2,512,384]{2,1,0:T(8,128)(2,1)}, f32[4,3,48,768]{3,2,1,0:T(8,128)}, bf16[4,3,48,768]{3,2,1,0:T(8,128)(2,1)}, bf16[3,768,384]{2,1,0:T(8,128)(2,1)S(1)}) custom-call(s32[2]{0:T(128)S(1)} %pad_add_fusion.at_ref, bf16[512,768]{1,0:T(8,128)(2,1)} %collective-permute-done.1.refs_0_, bf16[512,768]{1,0:T(8,128)(2,1)} %copy-done.6, ...), custom_call_target="tpu_custom_call" | custom-call | flops 4227858432 | bytes 12582912 | tf_op jit(solution)/shard_map/forward/pallas_call | solution.py:302
  106.2 2.0 %collective-permute-start.9 = (bf16[4,3,48,768]{3,2,1,0:T(8,128)(2,1)}, bf16[4,3,48,768]{3,2,1,0:T(8,128)(2,1)S(1)}, u32[]{:S(2)}, u32[]{:S(2)}) collective-permute-start(bf16[4,3,48,768]{3,2,1,0:T(8,128)(2,1)} %get-tuple-element.23), channel_id=1, source_target_pairs={{0,1},{1,0},{2,3},{3,2},{4,5},{5,4},{6,7},{7,6},{8,9},{9,8},{10,11... | collective-permute-start | bytes 2654216 | tf_op jit(solution)/shard_map/ppermute | solution.py:377
  108.2 3.9 %collective-permute-start.8 = (bf16[2,512,384]{2,1,0:T(8,128)(2,1)}, bf16[2,512,384]{2,1,0:T(8,128)(2,1)S(1)}, u32[]{:S(2)}, u32[]{:S(2)}) collective-permute-start(bf16[2,512,384]{2,1,0:T(8,128)(2,1)} %get-tuple-element.22.pre_ref), channel_id=1, source_target_pairs={{0,2},{2,0},{1,3},{3,1},{4,6},{6,4},{5,7},{7,5},{8,10},{10,8},{9,1... | collective-permute-start | bytes 2359304 | tf_op jit(solution)/shard_map/ppermute | solution.py:362
  112.1 19.6 %conditional.1 = (bf16[4,3,48,768]{3,2,1,0:T(8,128)(2,1)}, bf16[16,128]{1,0:T(8,128)(2,1)S(1)}) conditional(s32[]{:T(128)} %convert_element_type.9, () %tuple.18, (bf16[4,3,48,768]{3,2,1,0:T(8,128)(2,1)S(1)}, f32[4,3,48,768]{3,2,1,0:T(8,128)}) %tuple.19), branch_computations={%region_0.0_spmd, %region_1.0_spmd} | conditional | flops 1327104 | bytes 5464080 | solution.py:94
  113.8 17.0 %all_to_all.24 = bf16[4,3,48,768]{3,2,1,0:T(8,128)(2,1)} all-to-all(bf16[4,3,48,768]{3,2,1,0:T(8,128)(2,1)S(1)} %add_convert_fusion), channel_id=1, replica_groups=mesh['zh'=4,'zl'=4,'yl'=2,'x'=4,'yh'=2,'core'=2] {'x'}, dimensions={0} | all-to-all | bytes 1769472 | tf_op jit(solution)/shard_map/cond/branch_1_fun/all_to_all | solution.py:412
  131.7 2.3 %by_channel.1 = bf16[16,3,24,128]{3,2,1,0:T(8,128)(2,1)} custom-call(bf16[4,3,48,768]{3,2,1,0:T(8,128)(2,1)} %get-tuple-element.28.in_ref), custom_call_target="tpu_custom_call" | custom-call | bytes 1769472 | tf_op jit(solution)/shard_map/by_channel/pallas_call | solution.py:160
  134.0 6.0 %all-to-all-start.3 = ((bf16[16,3,24,128]{3,2,1,0:T(8,128)(2,1)}), bf16[16,3,24,128]{3,2,1,0:T(8,128)(2,1)S(1)}, u32[]{:S(2)}, u32[]{:S(2)}) async-start(bf16[16,3,24,128]{3,2,1,0:T(8,128)(2,1)} %by_channel.1), calls=%async_computation.3 | async-start | bytes 589824 | tf_op jit(solution)/shard_map/all_to_all | solution.py:419
  140.9 3.4 %collective-permute-start.10 = (bf16[2,512,384]{2,1,0:T(8,128)(2,1)}, bf16[2,512,384]{2,1,0:T(8,128)(2,1)}, u32[]{:S(2)}, u32[]{:S(2)}) collective-permute-start(bf16[2,512,384]{2,1,0:T(8,128)(2,1)} %once.7), channel_id=1, source_target_pairs={{0,4},{4,8},{8,12},{6,2},{10,6},{14,10},{1,5},{5,9},{9,13},{7,3},{... | collective-permute-start | bytes 2359304 | tf_op jit(solution)/shard_map/ppermute | solution.py:368
  144.3 14.5 %all-to-all-done.3.in_ref = bf16[16,3,24,128]{3,2,1,0:T(8,128)(2,1)S(1)} async-done(((bf16[16,3,24,128]{3,2,1,0:T(8,128)(2,1)}), bf16[16,3,24,128]{3,2,1,0:T(8,128)(2,1)S(1)}, u32[]{:S(2)}, u32[]{:S(2)}) %all-to-all-start.3) | async-done | bytes 294944 | tf_op jit(solution)/shard_map/all_to_all | solution.py:419
  159.5 5.4 %all-to-all-start.4 = ((bf16[4,24,128]{2,1,0:T(8,128)(2,1)}), bf16[4,24,128]{2,1,0:T(8,128)(2,1)S(1)}, u32[]{:S(2)}, u32[]{:S(2)}) async-start(bf16[4,24,128]{2,1,0:T(8,128)(2,1)} %add_parts.1), calls=%async_computation.4 | async-start | bytes 49152 | tf_op jit(solution)/shard_map/all_to_all | solution.py:424
  164.9 7.6 %backward.1 = (bf16[2,512,768]{2,1,0:T(8,128)(2,1)}, f32[8,128]{1,0:T(8,128)S(1)}) custom-call(bf16[2,512,768]{2,1,0:T(8,128)(2,1)} %in_ref.3, bf16[2,512,768]{2,1,0:T(8,128)(2,1)} %cot_ref.1, bf16[2,512,384]{2,1,0:T(8,128)(2,1)S(1)} %collective-permute-done.8.in_ref.partner_ref, bf16[2,512,384]{2,1,0:T(8,128)(2,1)} %get-tuple-element.22.pre_ref, ...), custom_call_target="tpu_custom_call" | custom-call | flops 1811939328 | bytes 12582912 | tf_op jit(solution)/shard_map/backward/pallas_call | solution.py:349
  (40 shorter events, 13.6 us)
Async XLA Ops:
  18.7 53.7 %copy-start.4 = (bf16[512,768]{1,0:T(8,128)(2,1)}, bf16[512,768]{1,0:T(8,128)(2,1)S(1)}, u32[]{:S(2)}) copy-start(bf16[512,768]{1,0:T(8,128)(2,1)S(1)} %get-tuple-element.20.refs_2_) | copy-start | bytes 2359300
  18.8 53.7 %copy-start.5 = (bf16[512,768]{1,0:T(8,128)(2,1)}, bf16[512,768]{1,0:T(8,128)(2,1)S(1)}, u32[]{:S(2)}) copy-start(bf16[512,768]{1,0:T(8,128)(2,1)S(1)} %get-tuple-element.21.refs_3_) | copy-start | bytes 2359300
  18.8 22.2 %collective-permute-start = (bf16[512,768]{1,0:T(8,128)(2,1)S(1)}, bf16[512,768]{1,0:T(8,128)(2,1)S(1)}, u32[]{:S(2)}, u32[]{:S(2)}) collective-permute-start(bf16[512,768]{1,0:T(8,128)(2,1)S(1)} %get-tuple-element.20.refs_2_), channel_id=1, source_target_pairs={{0,2},{2,0},{1,3},{3,1},{4,6},{6,4},{5,7},{7,5},{8,10},{10,8},{9,1... | collective-permute-start | bytes 2359304 | tf_op jit(solution)/shard_map/ppermute | solution.py:362
  23.1 30.2 %all-to-all-start.2 = ((bf16[4,48,768]{2,1,0:T(8,128)(2,1)}), bf16[4,48,768]{2,1,0:T(8,128)(2,1)S(1)}, u32[]{:S(2)}, u32[]{:S(2)}) async-start(bf16[4,48,768]{2,1,0:T(8,128)(2,1)} %assemble.1), calls=%async_computation.2 | async-start | bytes 589824 | tf_op jit(solution)/shard_map/all_to_all | solution.py:396
  37.1 23.7 %collective-permute-start.2 = (bf16[512,768]{1,0:T(8,128)(2,1)S(1)}, bf16[512,768]{1,0:T(8,128)(2,1)S(1)}, u32[]{:S(2)}, u32[]{:S(2)}) collective-permute-start(bf16[512,768]{1,0:T(8,128)(2,1)S(1)} %get-tuple-element.21.refs_3_), channel_id=1, source_target_pairs={{0,2},{2,0},{1,3},{3,1},{4,6},{6,4},{5,7},{7,5},{8,10},{10,8},{9,1... | collective-permute-start | bytes 2359304 | tf_op jit(solution)/shard_map/ppermute | solution.py:362
  41.0 32.2 %copy-start = (bf16[512,768]{1,0:T(8,128)(2,1)}, bf16[512,768]{1,0:T(8,128)(2,1)S(1)}, u32[]{:S(2)}) copy-start(bf16[512,768]{1,0:T(8,128)(2,1)S(1)} %collective-permute-done.refs_0_.refs_4_) | copy-start | bytes 2359300
  41.0 31.4 %collective-permute-start.1 = (bf16[512,768]{1,0:T(8,128)(2,1)S(1)}, bf16[512,768]{1,0:T(8,128)(2,1)}, u32[]{:S(2)}, u32[]{:S(2)}) collective-permute-start(bf16[512,768]{1,0:T(8,128)(2,1)S(1)} %collective-permute-done.refs_0_.refs_4_), channel_id=1, source_target_pairs={{0,4},{4,8},{8,12},{6,2},{10,6},{14,10},{1,5},{5,9},{9,13},{7,3},{... | collective-permute-start | bytes 2359304 | tf_op jit(solution)/shard_map/ppermute | solution.py:368
  53.4 19.0 %collective-permute-start.4 = (bf16[4,48,768]{2,1,0:T(8,128)(2,1)S(1)}, bf16[4,48,768]{2,1,0:T(8,128)(2,1)S(1)}, u32[]{:S(2)}, u32[]{:S(2)}) collective-permute-start(bf16[4,48,768]{2,1,0:T(8,128)(2,1)S(1)} %once.4), channel_id=1, source_target_pairs={{0,64},{32,96},{64,0},{96,32},{1,65},{33,97},{65,1},{97,33},{2,66}... | collective-permute-start | bytes 884744 | tf_op jit(solution)/shard_map/ppermute | solution.py:373
  60.9 27.8 %copy-start.1 = (bf16[512,768]{1,0:T(8,128)(2,1)}, bf16[512,768]{1,0:T(8,128)(2,1)S(1)}, u32[]{:S(2)}) copy-start(bf16[512,768]{1,0:T(8,128)(2,1)S(1)} %collective-permute-done.2.refs_1_.refs_5_) | copy-start | bytes 2359300
  60.9 17.2 %collective-permute-start.3 = (bf16[512,768]{1,0:T(8,128)(2,1)S(1)}, bf16[512,768]{1,0:T(8,128)(2,1)S(1)}, u32[]{:S(2)}, u32[]{:S(2)}) collective-permute-start(bf16[512,768]{1,0:T(8,128)(2,1)S(1)} %collective-permute-done.2.refs_1_.refs_5_), channel_id=1, source_target_pairs={{0,4},{4,8},{8,12},{6,2},{10,6},{14,10},{1,5},{5,9},{9,13},{7,3},{... | collective-permute-start | bytes 2359304 | tf_op jit(solution)/shard_map/ppermute | solution.py:368
  73.2 17.5 %copy-start.2 = (bf16[2,4,48,768]{3,2,1,0:T(8,128)(2,1)}, bf16[2,4,48,768]{3,2,1,0:T(8,128)(2,1)S(1)}, u32[]{:S(2)}) copy-start(bf16[2,4,48,768]{3,2,1,0:T(8,128)(2,1)S(1)} %once.5.refs_7_) | copy-start | bytes 1769476
  73.2 15.4 %collective-permute-start.5 = (bf16[2,4,48,768]{3,2,1,0:T(8,128)(2,1)S(1)}, bf16[2,4,48,768]{3,2,1,0:T(8,128)(2,1)S(1)}, u32[]{:S(2)}, u32[]{:S(2)}) collective-permute-start(bf16[2,4,48,768]{3,2,1,0:T(8,128)(2,1)S(1)} %once.5.refs_7_), channel_id=1, source_target_pairs={{0,32},{32,0},{64,96},{96,64},{1,33},{33,1},{65,97},{97,65},{2,34}... | collective-permute-start | bytes 1769480 | tf_op jit(solution)/shard_map/ppermute | solution.py:373
  75.1 15.6 %collective-permute-start.6 = (bf16[2,4,48,768]{3,2,1,0:T(8,128)(2,1)S(1)}, bf16[2,4,48,768]{3,2,1,0:T(8,128)(2,1)S(1)}, u32[]{:S(2)}, u32[]{:S(2)}) collective-permute-start(bf16[2,4,48,768]{3,2,1,0:T(8,128)(2,1)S(1)} %once.5.refs_7_), channel_id=1, source_target_pairs={{0,1},{1,0},{2,3},{3,2},{4,5},{5,4},{6,7},{7,6},{8,9},{9,8},{10,11... | collective-permute-start | bytes 1769480 | tf_op jit(solution)/shard_map/ppermute | solution.py:377
  78.0 12.6 %copy-start.6 = (bf16[512,768]{1,0:T(8,128)(2,1)}, bf16[512,768]{1,0:T(8,128)(2,1)S(1)}, u32[]{:S(2)}) copy-start(bf16[512,768]{1,0:T(8,128)(2,1)S(1)} %collective-permute-done.3.refs_1_) | copy-start | bytes 2359300
  88.7 4.0 %collective-permute-start.7 = (bf16[2,4,48,768]{3,2,1,0:T(8,128)(2,1)S(1)}, bf16[2,4,48,768]{3,2,1,0:T(8,128)(2,1)}, u32[]{:S(2)}, u32[]{:S(2)}) collective-permute-start(bf16[2,4,48,768]{3,2,1,0:T(8,128)(2,1)S(1)} %once.6.refs_8_), channel_id=1, source_target_pairs={{0,1},{1,0},{2,3},{3,2},{4,5},{5,4},{6,7},{7,6},{8,9},{9,8},{10,11... | collective-permute-start | bytes 1769480 | tf_op jit(solution)/shard_map/ppermute | solution.py:377
  92.7 1.1 copy-start.3
  106.2 5.9 %collective-permute-start.9 = (bf16[4,3,48,768]{3,2,1,0:T(8,128)(2,1)}, bf16[4,3,48,768]{3,2,1,0:T(8,128)(2,1)S(1)}, u32[]{:S(2)}, u32[]{:S(2)}) collective-permute-start(bf16[4,3,48,768]{3,2,1,0:T(8,128)(2,1)} %get-tuple-element.23), channel_id=1, source_target_pairs={{0,1},{1,0},{2,3},{3,2},{4,5},{5,4},{6,7},{7,6},{8,9},{9,8},{10,11... | collective-permute-start | bytes 2654216 | tf_op jit(solution)/shard_map/ppermute | solution.py:377
  108.2 31.7 %collective-permute-start.8 = (bf16[2,512,384]{2,1,0:T(8,128)(2,1)}, bf16[2,512,384]{2,1,0:T(8,128)(2,1)S(1)}, u32[]{:S(2)}, u32[]{:S(2)}) collective-permute-start(bf16[2,512,384]{2,1,0:T(8,128)(2,1)} %get-tuple-element.22.pre_ref), channel_id=1, source_target_pairs={{0,2},{2,0},{1,3},{3,1},{4,6},{6,4},{5,7},{7,5},{8,10},{10,8},{9,1... | collective-permute-start | bytes 2359304 | tf_op jit(solution)/shard_map/ppermute | solution.py:362
  134.0 24.8 %all-to-all-start.3 = ((bf16[16,3,24,128]{3,2,1,0:T(8,128)(2,1)}), bf16[16,3,24,128]{3,2,1,0:T(8,128)(2,1)S(1)}, u32[]{:S(2)}, u32[]{:S(2)}) async-start(bf16[16,3,24,128]{3,2,1,0:T(8,128)(2,1)} %by_channel.1), calls=%async_computation.3 | async-start | bytes 589824 | tf_op jit(solution)/shard_map/all_to_all | solution.py:419
  140.9 24.0 %collective-permute-start.10 = (bf16[2,512,384]{2,1,0:T(8,128)(2,1)}, bf16[2,512,384]{2,1,0:T(8,128)(2,1)}, u32[]{:S(2)}, u32[]{:S(2)}) collective-permute-start(bf16[2,512,384]{2,1,0:T(8,128)(2,1)} %once.7), channel_id=1, source_target_pairs={{0,4},{4,8},{8,12},{6,2},{10,6},{14,10},{1,5},{5,9},{9,13},{7,3},{... | collective-permute-start | bytes 2359304 | tf_op jit(solution)/shard_map/ppermute | solution.py:368
  159.5 13.0 %all-to-all-start.4 = ((bf16[4,24,128]{2,1,0:T(8,128)(2,1)}), bf16[4,24,128]{2,1,0:T(8,128)(2,1)S(1)}, u32[]{:S(2)}, u32[]{:S(2)}) async-start(bf16[4,24,128]{2,1,0:T(8,128)(2,1)} %add_parts.1), calls=%async_computation.4 | async-start | bytes 49152 | tf_op jit(solution)/shard_map/all_to_all | solution.py:424

commit v10 on v8

--- a/solution.py
+++ b/solution.py
@@ -345,7 +345,7 @@
         compiler_params=params(24),
         cost_estimate=cost(6 * samples * bins * width * hidden, 16 * samples * bins * width),
         name="backward",
-    )(in_hbm(inputs), in_hbm(cotangent), partner, grad_pre, handed, in_hbm(weights))
+    )(in_hbm(inputs), in_hbm(cotangent), partner, grad_pre, handed, weights)
 
 
 def exchanged(array):
@@ -391,19 +391,18 @@
     other_two = other_core(two)
     last = once(z_pair(two, 1), corner(handed[1]))
 
-    packed = (two, last, other_two, in_hbm(other_core(last)))
+    packed = (two, last, in_hbm(other_two), in_hbm(other_core(last)))
 
     grad_pre, own, other, weights = forward(
         at, handed + mids + partners, cotangent, packed[:2], packed[2:], grad_scale
     )
 
     def first_sums(own, other):
-        pair = own + other.astype(jnp.float32)
-        return lax.all_to_all(pair.astype(jnp.bfloat16), "x", 0, 0)
+        return (own + other.astype(jnp.float32)).astype(jnp.bfloat16)
 
     other = other_core(other)
     grad_partner = exchanged(grad_pre)
-    parts = held(first_sums, own, other)
+    parts = lax.all_to_all(held(first_sums, own, other), "x", 0, 0)
     grad_handed = handed_on(once(grad_partner, parts))
 
     parts = lax.all_to_all(by_channel(parts, depth), ("zh", "zl"), 0, 0)

time: 172 us -> 175 us (1.017)
  blocking collectives: 30.9 us -> 14.6 us
  waiting for transfers between devices: 47.6 us -> 58.1 us
  starting transfers between devices: 59.9 us -> 64.2 us
  local copies, waits for them, and re-layouts: 2.71 us -> 6.17 us
    all_to_all x1 -> x0, blocking collectives: 16.3 us -> none  [first_sums(): return lax.all_to_all(pair.astype(jnp.bfloat16), 'x', 0, 0)]
    all_to_all x0 -> x1, waiting for transfers between devices: none -> 10 us  [body(): parts = lax.all_to_all(held(first_sums, own, other), 'x', 0, 0)]
    all_to_all x1, waiting for transfers between devices: 16.1 us -> 12.6 us  [body(): parts = lax.all_to_all(by_channel(parts, depth), ('zh', 'zl'), 0, 0)]
    all_to_all x0 -> x1, starting transfers between devices: none -> 3.5 us  [body(): parts = lax.all_to_all(held(first_sums, own, other), 'x', 0, 0)]
    unnamed x16 -> x22, local copies, waits for them, and re-layouts: 2.02 us -> 5.49 us
    ppermute x3, waiting for transfers between devices: 0.01 us -> 2.32 us  [exchanged(): return lax.ppermute(array, 'yh', [(0, 1), (1, 0)])]
  transfers between devices with their start and end apart: 14 -> 15, of which waited for: 6 -> 9; matrix products, arithmetic and copies ran while one was open for 1% -> 0% of each run, Pallas kernels for 6% -> 6%
where the time goes in v10:
time: 175 us; the launch traced here: 174 us
  starting transfers between devices  64.2 us (37%)
  waiting for transfers between devices  58.1 us (33%)
  Pallas kernels  27.4 us (16%)
  blocking collectives  14.6 us (8%)
  local copies, waits for them, and re-layouts  6.17 us (4%)
  other arithmetic  2.94 us (2%)
    ppermute x2, waiting for transfers between devices, z_pair(): return lax.ppermute(array, 'zl', [(i, i ^ bit) for i in range(near)])  19.5 us
    all_to_all x1, blocking collectives, body(): pieces = lax.all_to_all(packed, ('x', 'yh', 'yl'), 0, 0)  14.6 us
    all_to_all x1, starting transfers between devices, body(): part = lax.all_to_all(assemble(pieces, f_part, taps + 1)[:far], 'zh', 0, 0)  14 us
    all_to_all x1, waiting for transfers between devices, body(): parts = lax.all_to_all(by_channel(parts, depth), ('zh', 'zl'), 0, 0)  12.6 us
    pallas_call x1, Pallas kernels, forward(): pl.pallas_call(functools.partial(forward_kernel, scale, samples), in_spec...  11.9 us
    ppermute x3, starting transfers between devices, exchanged(): return lax.ppermute(array, 'yh', [(0, 1), (1, 0)])  11.2 us
    all_to_all x1, waiting for transfers between devices, body(): parts = lax.all_to_all(held(first_sums, own, other), 'x', 0, 0)  10 us
    ppermute x3, starting transfers between devices, handed_on(): return lax.ppermute(array, ('x', 'yh'), lower + higher)  9.41 us
  transfers between devices with their start and end apart: 15, of which 9 were waited for; matrix products, arithmetic and copies ran while one was open for 0% of the time, Pallas kernels for 6%

profile of v10, /device:TPU:8, one launch (start us, length us, event | category | flops | bytes accessed | tf_op | source)
XLA Modules:
  0.0 174.4 jit_solution(1687843714135180358)
XLA Ops:
  1.5 14.6 %all_to_all.25._.in_ref = bf16[16,24,128]{2,1,0:T(8,128)(2,1)S(1)} all-to-all(bf16[16,24,128]{2,1,0:T(8,128)(2,1)S(1)} %pack.1), channel_id=1, replica_groups=mesh['zh'=4,'zl'=4,'yl'=2,'x'=4,'yh'=2,'core'=2] {'x','yh','yl'}, dimensions={0} | all-to-all | bytes 196608 | tf_op jit(solution)/shard_map/all_to_all | solution.py:381
  16.1 2.6 %activate.1 = (bf16[512,768]{1,0:T(8,128)(2,1)S(1)}, bf16[512,768]{1,0:T(8,128)(2,1)S(1)}) custom-call(bf16[2,512,768]{2,1,0:T(8,128)(2,1)} %in_ref.3, bf16[16,24,128]{2,1,0:T(8,128)(2,1)S(1)} %all_to_all.25._.in_ref), custom_call_target="tpu_custom_call" | custom-call | flops 15728640 | bytes 3145728 | tf_op jit(solution)/shard_map/activate/pallas_call | solution.py:216
  19.6 3.5 %collective-permute-start = (bf16[512,768]{1,0:T(8,128)(2,1)S(1)}, bf16[512,768]{1,0:T(8,128)(2,1)S(1)}, u32[]{:S(2)}, u32[]{:S(2)}) collective-permute-start(bf16[512,768]{1,0:T(8,128)(2,1)S(1)} %get-tuple-element.19.refs_2_), channel_id=1, source_target_pairs={{0,2},{2,0},{1,3},{3,1},{4,6},{6,4},{5,7},{7,5},{8,10},{10,8},{9,1... | collective-permute-start | bytes 2359304 | tf_op jit(solution)/shard_map/ppermute | solution.py:352
  24.0 14.0 %all-to-all-start.1 = ((bf16[4,48,768]{2,1,0:T(8,128)(2,1)}), bf16[4,48,768]{2,1,0:T(8,128)(2,1)S(1)}, u32[]{:S(2)}, u32[]{:S(2)}) async-start(bf16[4,48,768]{2,1,0:T(8,128)(2,1)} %assemble.1), calls=%async_computation.1 | async-start | bytes 589824 | tf_op jit(solution)/shard_map/all_to_all | solution.py:386
  38.0 3.8 %collective-permute-start.2 = (bf16[512,768]{1,0:T(8,128)(2,1)}, bf16[512,768]{1,0:T(8,128)(2,1)S(1)}, u32[]{:S(2)}, u32[]{:S(2)}) collective-permute-start(bf16[512,768]{1,0:T(8,128)(2,1)} %copy-done.8), channel_id=1, source_target_pairs={{0,2},{2,0},{1,3},{3,1},{4,6},{6,4},{5,7},{7,5},{8,10},{10,8},{9,1... | collective-permute-start | bytes 2359304 | tf_op jit(solution)/shard_map/ppermute | solution.py:352
  41.8 3.3 %collective-permute-start.1 = (bf16[512,768]{1,0:T(8,128)(2,1)S(1)}, bf16[512,768]{1,0:T(8,128)(2,1)}, u32[]{:S(2)}, u32[]{:S(2)}) collective-permute-start(bf16[512,768]{1,0:T(8,128)(2,1)S(1)} %collective-permute-done.refs_0_.refs_4_), channel_id=1, source_target_pairs={{0,4},{4,8},{8,12},{6,2},{10,6},{14,10},{1,5},{5,9},{9,13},{7,3},{... | collective-permute-start | bytes 2359304 | tf_op jit(solution)/shard_map/ppermute | solution.py:358
  45.1 9.0 %all-to-all-done.1.in_ref = bf16[4,48,768]{2,1,0:T(8,128)(2,1)S(1)} async-done(((bf16[4,48,768]{2,1,0:T(8,128)(2,1)}), bf16[4,48,768]{2,1,0:T(8,128)(2,1)S(1)}, u32[]{:S(2)}, u32[]{:S(2)}) %all-to-all-start.1) | async-done | bytes 294944 | tf_op jit(solution)/shard_map/all_to_all | solution.py:386
  54.2 7.5 %collective-permute-start.4 = (bf16[4,48,768]{2,1,0:T(8,128)(2,1)S(1)}, bf16[4,48,768]{2,1,0:T(8,128)(2,1)S(1)}, u32[]{:S(2)}, u32[]{:S(2)}) collective-permute-start(bf16[4,48,768]{2,1,0:T(8,128)(2,1)S(1)} %once.4), channel_id=1, source_target_pairs={{0,64},{32,96},{64,0},{96,32},{1,65},{33,97},{65,1},{97,33},{2,66}... | collective-permute-start | bytes 884744 | tf_op jit(solution)/shard_map/ppermute | solution.py:363
  61.7 2.5 %collective-permute-start.3 = (bf16[512,768]{1,0:T(8,128)(2,1)S(1)}, bf16[512,768]{1,0:T(8,128)(2,1)S(1)}, u32[]{:S(2)}, u32[]{:S(2)}) collective-permute-start(bf16[512,768]{1,0:T(8,128)(2,1)S(1)} %collective-permute-done.2.refs_1_.refs_5_), channel_id=1, source_target_pairs={{0,4},{4,8},{8,12},{6,2},{10,6},{14,10},{1,5},{5,9},{9,13},{7,3},{... | collective-permute-start | bytes 2359304 | tf_op jit(solution)/shard_map/ppermute | solution.py:358
  64.2 9.0 %collective-permute-done.4 = bf16[4,48,768]{2,1,0:T(8,128)(2,1)S(1)} collective-permute-done((bf16[4,48,768]{2,1,0:T(8,128)(2,1)S(1)}, bf16[4,48,768]{2,1,0:T(8,128)(2,1)S(1)}, u32[]{:S(2)}, u32[]{:S(2)}) %collective-permute-start.4) | collective-permute-done | bytes 294944 | tf_op jit(solution)/shard_map/ppermute | solution.py:363
  78.9 10.6 %collective-permute-done.5.in_ref = bf16[2,4,48,768]{3,2,1,0:T(8,128)(2,1)S(1)} collective-permute-done((bf16[2,4,48,768]{3,2,1,0:T(8,128)(2,1)S(1)}, bf16[2,4,48,768]{3,2,1,0:T(8,128)(2,1)S(1)}, u32[]{:S(2)}, u32[]{:S(2)}) %collective-permute-start.5) | collective-permute-done | bytes 589856 | tf_op jit(solution)/shard_map/ppermute | solution.py:363
  94.6 11.9 %forward.1 = (bf16[2,512,384]{2,1,0:T(8,128)(2,1)S(1)}, f32[4,3,48,768]{3,2,1,0:T(8,128)}, bf16[4,3,48,768]{3,2,1,0:T(8,128)(2,1)S(1)}, bf16[3,768,384]{2,1,0:T(8,128)(2,1)S(1)}) custom-call(s32[2]{0:T(128)S(1)} %pad_add_fusion.at_ref, bf16[512,768]{1,0:T(8,128)(2,1)} %collective-permute-done.1.refs_0_, bf16[512,768]{1,0:T(8,128)(2,1)} %copy-done.9, ...), custom_call_target="tpu_custom_call" | custom-call | flops 4227858432 | bytes 12582912 | tf_op jit(solution)/shard_map/forward/pallas_call | solution.py:294
  109.4 2.4 %collective-permute-done.9 = bf16[4,3,48,768]{3,2,1,0:T(8,128)(2,1)} collective-permute-done((bf16[4,3,48,768]{3,2,1,0:T(8,128)(2,1)S(1)}, bf16[4,3,48,768]{3,2,1,0:T(8,128)(2,1)}, u32[]{:S(2)}, u32[]{:S(2)}) %collective-permute-start.9) | collective-permute-done | bytes 884768 | tf_op jit(solution)/shard_map/ppermute | solution.py:367
  111.8 2.8 %conditional.1 = (bf16[4,3,48,768]{3,2,1,0:T(8,128)(2,1)}) conditional(s32[]{:T(128)} %convert_element_type.9, () %tuple.14, (bf16[4,3,48,768]{3,2,1,0:T(8,128)(2,1)}, f32[4,3,48,768]{3,2,1,0:T(8,128)}) %tuple.15), branch_computations={%region_0.0_spmd, %region_1.0_spmd} | conditional | flops 1327104 | bytes 3538952 | solution.py:94
  111.8 2.8 %add_convert_fusion = bf16[4,3,48,768]{3,2,1,0:T(8,128)(2,1)} fusion(f32[4,3,48,768]{3,2,1,0:T(8,128)} %get-tuple-element.4, bf16[4,3,48,768]{3,2,1,0:T(8,128)(2,1)} %get-tuple-element.8), kind=kLoop, calls=%fused_computation | loop fusion | flops 1327104 | bytes 3538944 | tf_op jit(solution)/shard_map/cond/branch_1_fun/convert_element_type | solution.py:401
  114.6 3.5 %all-to-all-start.2 = ((bf16[4,3,48,768]{3,2,1,0:T(8,128)(2,1)}), bf16[4,3,48,768]{3,2,1,0:T(8,128)(2,1)S(1)}, u32[]{:S(2)}, u32[]{:S(2)}) async-start(bf16[4,3,48,768]{3,2,1,0:T(8,128)(2,1)} %get-tuple-element.27), calls=%async_computation.2 | async-start | bytes 1769472 | tf_op jit(solution)/shard_map/all_to_all | solution.py:405
  118.1 3.8 %collective-permute-start.8 = (bf16[2,512,384]{2,1,0:T(8,128)(2,1)}, bf16[2,512,384]{2,1,0:T(8,128)(2,1)S(1)}, u32[]{:S(2)}, u32[]{:S(2)}) collective-permute-start(bf16[2,512,384]{2,1,0:T(8,128)(2,1)} %copy-done.1), channel_id=1, source_target_pairs={{0,2},{2,0},{1,3},{3,1},{4,6},{6,4},{5,7},{7,5},{8,10},{10,8},{9,1... | collective-permute-start | bytes 2359304 | tf_op jit(solution)/shard_map/ppermute | solution.py:352
  122.0 10.0 %all-to-all-done.2.refs_0_.in_ref = bf16[4,3,48,768]{3,2,1,0:T(8,128)(2,1)S(1)} async-done(((bf16[4,3,48,768]{3,2,1,0:T(8,128)(2,1)}), bf16[4,3,48,768]{3,2,1,0:T(8,128)(2,1)S(1)}, u32[]{:S(2)}, u32[]{:S(2)}) %all-to-all-start.2) | async-done | bytes 884768 | tf_op jit(solution)/shard_map/all_to_all | solution.py:405
  133.1 5.9 %all-to-all-start.3 = ((bf16[16,3,24,128]{3,2,1,0:T(8,128)(2,1)}), bf16[16,3,24,128]{3,2,1,0:T(8,128)(2,1)}, u32[]{:S(2)}, u32[]{:S(2)}) async-start(bf16[16,3,24,128]{3,2,1,0:T(8,128)(2,1)} %copy-done), calls=%async_computation.3 | async-start | bytes 589824 | tf_op jit(solution)/shard_map/all_to_all | solution.py:408
  139.0 2.3 %collective-permute-done.8.in_ref.partner_ref = bf16[2,512,384]{2,1,0:T(8,128)(2,1)S(1)} collective-permute-done((bf16[2,512,384]{2,1,0:T(8,128)(2,1)}, bf16[2,512,384]{2,1,0:T(8,128)(2,1)S(1)}, u32[]{:S(2)}, u32[]{:S(2)}) %collective-permute-start.8) | collective-permute-done | bytes 786464 | tf_op jit(solution)/shard_map/ppermute | solution.py:352
  142.3 3.6 %collective-permute-start.10 = (bf16[2,512,384]{2,1,0:T(8,128)(2,1)}, bf16[2,512,384]{2,1,0:T(8,128)(2,1)S(1)}, u32[]{:S(2)}, u32[]{:S(2)}) collective-permute-start(bf16[2,512,384]{2,1,0:T(8,128)(2,1)} %once.7), channel_id=1, source_target_pairs={{0,4},{4,8},{8,12},{6,2},{10,6},{14,10},{1,5},{5,9},{9,13},{7,3},{... | collective-permute-start | bytes 2359304 | tf_op jit(solution)/shard_map/ppermute | solution.py:358
  145.9 12.6 %all-to-all-done.3.in_ref = bf16[16,3,24,128]{3,2,1,0:T(8,128)(2,1)} async-done(((bf16[16,3,24,128]{3,2,1,0:T(8,128)(2,1)}), bf16[16,3,24,128]{3,2,1,0:T(8,128)(2,1)}, u32[]{:S(2)}, u32[]{:S(2)}) %all-to-all-start.3) | async-done | bytes 294944 | tf_op jit(solution)/shard_map/all_to_all | solution.py:408
  160.2 5.0 %all-to-all-start.4 = ((bf16[4,24,128]{2,1,0:T(8,128)(2,1)}), bf16[4,24,128]{2,1,0:T(8,128)(2,1)S(1)}, u32[]{:S(2)}, u32[]{:S(2)}) async-start(bf16[4,24,128]{2,1,0:T(8,128)(2,1)} %add_parts.1), calls=%async_computation.4 | async-start | bytes 49152 | tf_op jit(solution)/shard_map/all_to_all | solution.py:413
  166.4 7.3 %backward.1 = (bf16[2,512,768]{2,1,0:T(8,128)(2,1)}, f32[8,128]{1,0:T(8,128)S(1)}) custom-call(bf16[2,512,768]{2,1,0:T(8,128)(2,1)} %in_ref.3, bf16[2,512,768]{2,1,0:T(8,128)(2,1)} %cot_ref.1, bf16[2,512,384]{2,1,0:T(8,128)(2,1)S(1)} %collective-permute-done.8.in_ref.partner_ref, bf16[2,512,384]{2,1,0:T(8,128)(2,1)S(1)} %copy-done.2, ...), custom_call_target="tpu_custom_call" | custom-call | flops 1811939328 | bytes 12582912 | tf_op jit(solution)/shard_map/backward/pallas_call | solution.py:339
  (47 shorter events, 21.8 us)
Async XLA Ops:
  18.7 0.9 copy-start.8
  19.6 53.6 %copy-start.7 = (bf16[512,768]{1,0:T(8,128)(2,1)}, bf16[512,768]{1,0:T(8,128)(2,1)S(1)}, u32[]{:S(2)}) copy-start(bf16[512,768]{1,0:T(8,128)(2,1)S(1)} %get-tuple-element.19.refs_2_) | copy-start | bytes 2359300
  19.6 22.2 %collective-permute-start = (bf16[512,768]{1,0:T(8,128)(2,1)S(1)}, bf16[512,768]{1,0:T(8,128)(2,1)S(1)}, u32[]{:S(2)}, u32[]{:S(2)}) collective-permute-start(bf16[512,768]{1,0:T(8,128)(2,1)S(1)} %get-tuple-element.19.refs_2_), channel_id=1, source_target_pairs={{0,2},{2,0},{1,3},{3,1},{4,6},{6,4},{5,7},{7,5},{8,10},{10,8},{9,1... | collective-permute-start | bytes 2359304 | tf_op jit(solution)/shard_map/ppermute | solution.py:352
  24.0 30.2 %all-to-all-start.1 = ((bf16[4,48,768]{2,1,0:T(8,128)(2,1)}), bf16[4,48,768]{2,1,0:T(8,128)(2,1)S(1)}, u32[]{:S(2)}, u32[]{:S(2)}) async-start(bf16[4,48,768]{2,1,0:T(8,128)(2,1)} %assemble.1), calls=%async_computation.1 | async-start | bytes 589824 | tf_op jit(solution)/shard_map/all_to_all | solution.py:386
  38.0 23.7 %collective-permute-start.2 = (bf16[512,768]{1,0:T(8,128)(2,1)}, bf16[512,768]{1,0:T(8,128)(2,1)S(1)}, u32[]{:S(2)}, u32[]{:S(2)}) collective-permute-start(bf16[512,768]{1,0:T(8,128)(2,1)} %copy-done.8), channel_id=1, source_target_pairs={{0,2},{2,0},{1,3},{3,1},{4,6},{6,4},{5,7},{7,5},{8,10},{10,8},{9,1... | collective-permute-start | bytes 2359304 | tf_op jit(solution)/shard_map/ppermute | solution.py:352
  41.8 32.1 %copy-start.3 = (bf16[512,768]{1,0:T(8,128)(2,1)}, bf16[512,768]{1,0:T(8,128)(2,1)S(1)}, u32[]{:S(2)}) copy-start(bf16[512,768]{1,0:T(8,128)(2,1)S(1)} %collective-permute-done.refs_0_.refs_4_) | copy-start | bytes 2359300
  41.8 31.4 %collective-permute-start.1 = (bf16[512,768]{1,0:T(8,128)(2,1)S(1)}, bf16[512,768]{1,0:T(8,128)(2,1)}, u32[]{:S(2)}, u32[]{:S(2)}) collective-permute-start(bf16[512,768]{1,0:T(8,128)(2,1)S(1)} %collective-permute-done.refs_0_.refs_4_), channel_id=1, source_target_pairs={{0,4},{4,8},{8,12},{6,2},{10,6},{14,10},{1,5},{5,9},{9,13},{7,3},{... | collective-permute-start | bytes 2359304 | tf_op jit(solution)/shard_map/ppermute | solution.py:358
  54.2 19.0 %collective-permute-start.4 = (bf16[4,48,768]{2,1,0:T(8,128)(2,1)S(1)}, bf16[4,48,768]{2,1,0:T(8,128)(2,1)S(1)}, u32[]{:S(2)}, u32[]{:S(2)}) collective-permute-start(bf16[4,48,768]{2,1,0:T(8,128)(2,1)S(1)} %once.4), channel_id=1, source_target_pairs={{0,64},{32,96},{64,0},{96,32},{1,65},{33,97},{65,1},{97,33},{2,66}... | collective-permute-start | bytes 884744 | tf_op jit(solution)/shard_map/ppermute | solution.py:363
  61.7 27.8 %copy-start.4 = (bf16[512,768]{1,0:T(8,128)(2,1)}, bf16[512,768]{1,0:T(8,128)(2,1)S(1)}, u32[]{:S(2)}) copy-start(bf16[512,768]{1,0:T(8,128)(2,1)S(1)} %collective-permute-done.2.refs_1_.refs_5_) | copy-start | bytes 2359300
  61.7 17.2 %collective-permute-start.3 = (bf16[512,768]{1,0:T(8,128)(2,1)S(1)}, bf16[512,768]{1,0:T(8,128)(2,1)S(1)}, u32[]{:S(2)}, u32[]{:S(2)}) collective-permute-start(bf16[512,768]{1,0:T(8,128)(2,1)S(1)} %collective-permute-done.2.refs_1_.refs_5_), channel_id=1, source_target_pairs={{0,4},{4,8},{8,12},{6,2},{10,6},{14,10},{1,5},{5,9},{9,13},{7,3},{... | collective-permute-start | bytes 2359304 | tf_op jit(solution)/shard_map/ppermute | solution.py:358
  74.0 17.5 %copy-start.5 = (bf16[2,4,48,768]{3,2,1,0:T(8,128)(2,1)}, bf16[2,4,48,768]{3,2,1,0:T(8,128)(2,1)S(1)}, u32[]{:S(2)}) copy-start(bf16[2,4,48,768]{3,2,1,0:T(8,128)(2,1)S(1)} %once.5.refs_7_) | copy-start | bytes 1769476
  74.0 15.4 %collective-permute-start.5 = (bf16[2,4,48,768]{3,2,1,0:T(8,128)(2,1)S(1)}, bf16[2,4,48,768]{3,2,1,0:T(8,128)(2,1)S(1)}, u32[]{:S(2)}, u32[]{:S(2)}) collective-permute-start(bf16[2,4,48,768]{3,2,1,0:T(8,128)(2,1)S(1)} %once.5.refs_7_), channel_id=1, source_target_pairs={{0,32},{32,0},{64,96},{96,64},{1,33},{33,1},{65,97},{97,65},{2,34}... | collective-permute-start | bytes 1769480 | tf_op jit(solution)/shard_map/ppermute | solution.py:363
  75.9 15.6 %collective-permute-start.6 = (bf16[2,4,48,768]{3,2,1,0:T(8,128)(2,1)S(1)}, bf16[2,4,48,768]{3,2,1,0:T(8,128)(2,1)S(1)}, u32[]{:S(2)}, u32[]{:S(2)}) collective-permute-start(bf16[2,4,48,768]{3,2,1,0:T(8,128)(2,1)S(1)} %once.5.refs_7_), channel_id=1, source_target_pairs={{0,1},{1,0},{2,3},{3,2},{4,5},{5,4},{6,7},{7,6},{8,9},{9,8},{10,11... | collective-permute-start | bytes 1769480 | tf_op jit(solution)/shard_map/ppermute | solution.py:367
  78.9 12.6 %copy-start.9 = (bf16[512,768]{1,0:T(8,128)(2,1)}, bf16[512,768]{1,0:T(8,128)(2,1)S(1)}, u32[]{:S(2)}) copy-start(bf16[512,768]{1,0:T(8,128)(2,1)S(1)} %collective-permute-done.3.refs_1_) | copy-start | bytes 2359300
  89.5 4.0 %collective-permute-start.7 = (bf16[2,4,48,768]{3,2,1,0:T(8,128)(2,1)S(1)}, bf16[2,4,48,768]{3,2,1,0:T(8,128)(2,1)}, u32[]{:S(2)}, u32[]{:S(2)}) collective-permute-start(bf16[2,4,48,768]{3,2,1,0:T(8,128)(2,1)S(1)} %once.6.refs_8_), channel_id=1, source_target_pairs={{0,1},{1,0},{2,3},{3,2},{4,5},{5,4},{6,7},{7,6},{8,9},{9,8},{10,11... | collective-permute-start | bytes 1769480 | tf_op jit(solution)/shard_map/ppermute | solution.py:367
  93.5 1.1 copy-start.6
  106.5 0.9 copy-start.1
  107.4 4.4 %collective-permute-start.9 = (bf16[4,3,48,768]{3,2,1,0:T(8,128)(2,1)S(1)}, bf16[4,3,48,768]{3,2,1,0:T(8,128)(2,1)}, u32[]{:S(2)}, u32[]{:S(2)}) collective-permute-start(bf16[4,3,48,768]{3,2,1,0:T(8,128)(2,1)S(1)} %get-tuple-element.22), channel_id=1, source_target_pairs={{0,1},{1,0},{2,3},{3,2},{4,5},{5,4},{6,7},{7,6},{8,9},{9,8},{10,11... | collective-permute-start | bytes 2654216 | tf_op jit(solution)/shard_map/ppermute | solution.py:367
  114.6 17.4 %all-to-all-start.2 = ((bf16[4,3,48,768]{3,2,1,0:T(8,128)(2,1)}), bf16[4,3,48,768]{3,2,1,0:T(8,128)(2,1)S(1)}, u32[]{:S(2)}, u32[]{:S(2)}) async-start(bf16[4,3,48,768]{3,2,1,0:T(8,128)(2,1)} %get-tuple-element.27), calls=%async_computation.2 | async-start | bytes 1769472 | tf_op jit(solution)/shard_map/all_to_all | solution.py:405
  118.1 23.2 %collective-permute-start.8 = (bf16[2,512,384]{2,1,0:T(8,128)(2,1)}, bf16[2,512,384]{2,1,0:T(8,128)(2,1)S(1)}, u32[]{:S(2)}, u32[]{:S(2)}) collective-permute-start(bf16[2,512,384]{2,1,0:T(8,128)(2,1)} %copy-done.1), channel_id=1, source_target_pairs={{0,2},{2,0},{1,3},{3,1},{4,6},{6,4},{5,7},{7,5},{8,10},{10,8},{9,1... | collective-permute-start | bytes 2359304 | tf_op jit(solution)/shard_map/ppermute | solution.py:352
  133.1 25.4 %all-to-all-start.3 = ((bf16[16,3,24,128]{3,2,1,0:T(8,128)(2,1)}), bf16[16,3,24,128]{3,2,1,0:T(8,128)(2,1)}, u32[]{:S(2)}, u32[]{:S(2)}) async-start(bf16[16,3,24,128]{3,2,1,0:T(8,128)(2,1)} %copy-done), calls=%async_computation.3 | async-start | bytes 589824 | tf_op jit(solution)/shard_map/all_to_all | solution.py:408
  142.3 23.0 %collective-permute-start.10 = (bf16[2,512,384]{2,1,0:T(8,128)(2,1)}, bf16[2,512,384]{2,1,0:T(8,128)(2,1)S(1)}, u32[]{:S(2)}, u32[]{:S(2)}) collective-permute-start(bf16[2,512,384]{2,1,0:T(8,128)(2,1)} %once.7), channel_id=1, source_target_pairs={{0,4},{4,8},{8,12},{6,2},{10,6},{14,10},{1,5},{5,9},{9,13},{7,3},{... | collective-permute-start | bytes 2359304 | tf_op jit(solution)/shard_map/ppermute | solution.py:358
  160.2 13.5 %all-to-all-start.4 = ((bf16[4,24,128]{2,1,0:T(8,128)(2,1)}), bf16[4,24,128]{2,1,0:T(8,128)(2,1)S(1)}, u32[]{:S(2)}, u32[]{:S(2)}) async-start(bf16[4,24,128]{2,1,0:T(8,128)(2,1)} %add_parts.1), calls=%async_computation.4 | async-start | bytes 49152 | tf_op jit(solution)/shard_map/all_to_all | solution.py:413
  165.2 1.1 copy-start.2
  (2 other events, 1.5 us)

commit v11 on v8

--- a/solution.py
+++ b/solution.py
@@ -345,7 +345,7 @@
         compiler_params=params(24),
         cost_estimate=cost(6 * samples * bins * width * hidden, 16 * samples * bins * width),
         name="backward",
-    )(in_hbm(inputs), in_hbm(cotangent), partner, grad_pre, handed, in_hbm(weights))
+    )(in_hbm(inputs), in_hbm(cotangent), partner, grad_pre, handed, weights)
 
 
 def exchanged(array):

time: 172 us -> 171 us (level)
    all_to_all x1, waiting for transfers between devices: 16.1 us -> 14.4 us  [body(): parts = lax.all_to_all(by_channel(parts, depth), ('zh', 'zl'), 0, 0)]
  transfers between devices with their start and end apart: 14 -> 14, of which waited for: 6 -> 6; matrix products, arithmetic and copies ran while one was open for 1% -> 1% of each run, Pallas kernels for 6% -> 7%
where the time goes in v11:
time: 171 us; the launch traced here: 170 us
  starting transfers between devices  60.6 us (35%)
  waiting for transfers between devices  46 us (27%)
  blocking collectives  30.9 us (18%)
  Pallas kernels  27.8 us (16%)
  other arithmetic  1.8 us (1%)
  local copies, waits for them, and re-layouts  1.77 us (1%)
    ppermute x2, waiting for transfers between devices, z_pair(): return lax.ppermute(array, 'zl', [(i, i ^ bit) for i in range(near)])  19.6 us
    all_to_all x1, blocking collectives, first_sums(): return lax.all_to_all(pair.astype(jnp.bfloat16), 'x', 0, 0)  16.3 us
    all_to_all x1, blocking collectives, body(): pieces = lax.all_to_all(packed, ('x', 'yh', 'yl'), 0, 0)  14.6 us
    all_to_all x1, waiting for transfers between devices, body(): parts = lax.all_to_all(by_channel(parts, depth), ('zh', 'zl'), 0, 0)  14.4 us
    all_to_all x1, starting transfers between devices, body(): part = lax.all_to_all(assemble(pieces, f_part, taps + 1)[:far], 'zh', 0, 0)  14 us
    pallas_call x1, Pallas kernels, forward(): pl.pallas_call(functools.partial(forward_kernel, scale, samples), in_spec...  12.2 us
    ppermute x3, starting transfers between devices, exchanged(): return lax.ppermute(array, 'yh', [(0, 1), (1, 0)])  11.2 us
    ppermute x2, starting transfers between devices, z_pair(): return lax.ppermute(array, 'zl', [(i, i ^ bit) for i in range(near)])  9.39 us
  transfers between devices with their start and end apart: 14, of which 6 were waited for; matrix products, arithmetic and copies ran while one was open for 1% of the time, Pallas kernels for 7%

profile of v11, /device:TPU:8, one launch (start us, length us, event | category | flops | bytes accessed | tf_op | source)
XLA Modules:
  0.0 169.7 jit_solution(4709418330577427358)
XLA Ops:
  1.5 14.6 %all_to_all.25._.in_ref = bf16[16,24,128]{2,1,0:T(8,128)(2,1)S(1)} all-to-all(bf16[16,24,128]{2,1,0:T(8,128)(2,1)S(1)} %pack.1), channel_id=1, replica_groups=mesh['zh'=4,'zl'=4,'yl'=2,'x'=4,'yh'=2,'core'=2] {'x','yh','yl'}, dimensions={0} | all-to-all | bytes 196608 | tf_op jit(solution)/shard_map/all_to_all | solution.py:381
  16.1 2.6 %activate.1 = (bf16[512,768]{1,0:T(8,128)(2,1)S(1)}, bf16[512,768]{1,0:T(8,128)(2,1)S(1)}) custom-call(bf16[2,512,768]{2,1,0:T(8,128)(2,1)} %in_ref.3, bf16[16,24,128]{2,1,0:T(8,128)(2,1)S(1)} %all_to_all.25._.in_ref), custom_call_target="tpu_custom_call" | custom-call | flops 15728640 | bytes 3145728 | tf_op jit(solution)/shard_map/activate/pallas_call | solution.py:216
  18.8 3.5 %collective-permute-start = (bf16[512,768]{1,0:T(8,128)(2,1)S(1)}, bf16[512,768]{1,0:T(8,128)(2,1)S(1)}, u32[]{:S(2)}, u32[]{:S(2)}) collective-permute-start(bf16[512,768]{1,0:T(8,128)(2,1)S(1)} %get-tuple-element.19.refs_2_), channel_id=1, source_target_pairs={{0,2},{2,0},{1,3},{3,1},{4,6},{6,4},{5,7},{7,5},{8,10},{10,8},{9,1... | collective-permute-start | bytes 2359304 | tf_op jit(solution)/shard_map/ppermute | solution.py:352
  23.1 14.0 %all-to-all-start.2 = ((bf16[4,48,768]{2,1,0:T(8,128)(2,1)}), bf16[4,48,768]{2,1,0:T(8,128)(2,1)S(1)}, u32[]{:S(2)}, u32[]{:S(2)}) async-start(bf16[4,48,768]{2,1,0:T(8,128)(2,1)} %assemble.1), calls=%async_computation.2 | async-start | bytes 589824 | tf_op jit(solution)/shard_map/all_to_all | solution.py:386
  37.1 3.8 %collective-permute-start.2 = (bf16[512,768]{1,0:T(8,128)(2,1)S(1)}, bf16[512,768]{1,0:T(8,128)(2,1)S(1)}, u32[]{:S(2)}, u32[]{:S(2)}) collective-permute-start(bf16[512,768]{1,0:T(8,128)(2,1)S(1)} %get-tuple-element.20.refs_3_), channel_id=1, source_target_pairs={{0,2},{2,0},{1,3},{3,1},{4,6},{6,4},{5,7},{7,5},{8,10},{10,8},{9,1... | collective-permute-start | bytes 2359304 | tf_op jit(solution)/shard_map/ppermute | solution.py:352
  41.0 3.3 %collective-permute-start.1 = (bf16[512,768]{1,0:T(8,128)(2,1)S(1)}, bf16[512,768]{1,0:T(8,128)(2,1)}, u32[]{:S(2)}, u32[]{:S(2)}) collective-permute-start(bf16[512,768]{1,0:T(8,128)(2,1)S(1)} %collective-permute-done.refs_0_.refs_4_), channel_id=1, source_target_pairs={{0,4},{4,8},{8,12},{6,2},{10,6},{14,10},{1,5},{5,9},{9,13},{7,3},{... | collective-permute-start | bytes 2359304 | tf_op jit(solution)/shard_map/ppermute | solution.py:358
  44.3 9.0 %all-to-all-done.2.in_ref = bf16[4,48,768]{2,1,0:T(8,128)(2,1)S(1)} async-done(((bf16[4,48,768]{2,1,0:T(8,128)(2,1)}), bf16[4,48,768]{2,1,0:T(8,128)(2,1)S(1)}, u32[]{:S(2)}, u32[]{:S(2)}) %all-to-all-start.2) | async-done | bytes 294944 | tf_op jit(solution)/shard_map/all_to_all | solution.py:386
  53.4 7.5 %collective-permute-start.4 = (bf16[4,48,768]{2,1,0:T(8,128)(2,1)S(1)}, bf16[4,48,768]{2,1,0:T(8,128)(2,1)S(1)}, u32[]{:S(2)}, u32[]{:S(2)}) collective-permute-start(bf16[4,48,768]{2,1,0:T(8,128)(2,1)S(1)} %once.4), channel_id=1, source_target_pairs={{0,64},{32,96},{64,0},{96,32},{1,65},{33,97},{65,1},{97,33},{2,66}... | collective-permute-start | bytes 884744 | tf_op jit(solution)/shard_map/ppermute | solution.py:363
  60.9 2.5 %collective-permute-start.3 = (bf16[512,768]{1,0:T(8,128)(2,1)S(1)}, bf16[512,768]{1,0:T(8,128)(2,1)S(1)}, u32[]{:S(2)}, u32[]{:S(2)}) collective-permute-start(bf16[512,768]{1,0:T(8,128)(2,1)S(1)} %collective-permute-done.2.refs_1_.refs_5_), channel_id=1, source_target_pairs={{0,4},{4,8},{8,12},{6,2},{10,6},{14,10},{1,5},{5,9},{9,13},{7,3},{... | collective-permute-start | bytes 2359304 | tf_op jit(solution)/shard_map/ppermute | solution.py:358
  63.4 9.0 %collective-permute-done.4 = bf16[4,48,768]{2,1,0:T(8,128)(2,1)S(1)} collective-permute-done((bf16[4,48,768]{2,1,0:T(8,128)(2,1)S(1)}, bf16[4,48,768]{2,1,0:T(8,128)(2,1)S(1)}, u32[]{:S(2)}, u32[]{:S(2)}) %collective-permute-start.4) | collective-permute-done | bytes 294944 | tf_op jit(solution)/shard_map/ppermute | solution.py:363
  75.1 1.9 %collective-permute-start.6 = (bf16[2,4,48,768]{3,2,1,0:T(8,128)(2,1)S(1)}, bf16[2,4,48,768]{3,2,1,0:T(8,128)(2,1)S(1)}, u32[]{:S(2)}, u32[]{:S(2)}) collective-permute-start(bf16[2,4,48,768]{3,2,1,0:T(8,128)(2,1)S(1)} %once.5.refs_7_), channel_id=1, source_target_pairs={{0,1},{1,0},{2,3},{3,2},{4,5},{5,4},{6,7},{7,6},{8,9},{9,8},{10,11... | collective-permute-start | bytes 1769480 | tf_op jit(solution)/shard_map/ppermute | solution.py:367
  78.0 10.6 %collective-permute-done.5.in_ref = bf16[2,4,48,768]{3,2,1,0:T(8,128)(2,1)S(1)} collective-permute-done((bf16[2,4,48,768]{3,2,1,0:T(8,128)(2,1)S(1)}, bf16[2,4,48,768]{3,2,1,0:T(8,128)(2,1)S(1)}, u32[]{:S(2)}, u32[]{:S(2)}) %collective-permute-start.5) | collective-permute-done | bytes 589856 | tf_op jit(solution)/shard_map/ppermute | solution.py:363
  88.7 1.9 %collective-permute-start.7 = (bf16[2,4,48,768]{3,2,1,0:T(8,128)(2,1)S(1)}, bf16[2,4,48,768]{3,2,1,0:T(8,128)(2,1)}, u32[]{:S(2)}, u32[]{:S(2)}) collective-permute-start(bf16[2,4,48,768]{3,2,1,0:T(8,128)(2,1)S(1)} %once.6.refs_8_), channel_id=1, source_target_pairs={{0,1},{1,0},{2,3},{3,2},{4,5},{5,4},{6,7},{7,6},{8,9},{9,8},{10,11... | collective-permute-start | bytes 1769480 | tf_op jit(solution)/shard_map/ppermute | solution.py:367
  90.7 2.0 %collective-permute-done.7.refs_10_ = bf16[2,4,48,768]{3,2,1,0:T(8,128)(2,1)} collective-permute-done((bf16[2,4,48,768]{3,2,1,0:T(8,128)(2,1)S(1)}, bf16[2,4,48,768]{3,2,1,0:T(8,128)(2,1)}, u32[]{:S(2)}, u32[]{:S(2)}) %collective-permute-start.7) | collective-permute-done | bytes 589856 | tf_op jit(solution)/shard_map/ppermute | solution.py:367
  93.8 12.2 %forward.1 = (bf16[2,512,384]{2,1,0:T(8,128)(2,1)}, f32[4,3,48,768]{3,2,1,0:T(8,128)}, bf16[4,3,48,768]{3,2,1,0:T(8,128)(2,1)}, bf16[3,768,384]{2,1,0:T(8,128)(2,1)S(1)}) custom-call(s32[2]{0:T(128)S(1)} %pad_add_fusion.at_ref, bf16[512,768]{1,0:T(8,128)(2,1)} %collective-permute-done.1.refs_0_, bf16[512,768]{1,0:T(8,128)(2,1)} %copy-done.7, ...), custom_call_target="tpu_custom_call" | custom-call | flops 4227858432 | bytes 12582912 | tf_op jit(solution)/shard_map/forward/pallas_call | solution.py:294
  106.0 2.0 %collective-permute-start.9 = (bf16[4,3,48,768]{3,2,1,0:T(8,128)(2,1)}, bf16[4,3,48,768]{3,2,1,0:T(8,128)(2,1)S(1)}, u32[]{:S(2)}, u32[]{:S(2)}) collective-permute-start(bf16[4,3,48,768]{3,2,1,0:T(8,128)(2,1)} %get-tuple-element.22), channel_id=1, source_target_pairs={{0,1},{1,0},{2,3},{3,2},{4,5},{5,4},{6,7},{7,6},{8,9},{9,8},{10,11... | collective-permute-start | bytes 2654216 | tf_op jit(solution)/shard_map/ppermute | solution.py:367
  108.0 3.9 %collective-permute-start.8 = (bf16[2,512,384]{2,1,0:T(8,128)(2,1)}, bf16[2,512,384]{2,1,0:T(8,128)(2,1)S(1)}, u32[]{:S(2)}, u32[]{:S(2)}) collective-permute-start(bf16[2,512,384]{2,1,0:T(8,128)(2,1)} %get-tuple-element.21.pre_ref), channel_id=1, source_target_pairs={{0,2},{2,0},{1,3},{3,1},{4,6},{6,4},{5,7},{7,5},{8,10},{10,8},{9,1... | collective-permute-start | bytes 2359304 | tf_op jit(solution)/shard_map/ppermute | solution.py:352
  111.9 18.0 %conditional.1 = (bf16[4,3,48,768]{3,2,1,0:T(8,128)(2,1)S(1)}) conditional(s32[]{:T(128)} %convert_element_type.9, () %tuple.14, (bf16[4,3,48,768]{3,2,1,0:T(8,128)(2,1)S(1)}, f32[4,3,48,768]{3,2,1,0:T(8,128)}) %tuple.15), branch_computations={%region_0.0_spmd, %region_1.0_spmd} | conditional | flops 1327104 | bytes 5308424 | solution.py:94
  113.6 16.3 %all_to_all.24 = bf16[4,3,48,768]{3,2,1,0:T(8,128)(2,1)S(1)} all-to-all(bf16[4,3,48,768]{3,2,1,0:T(8,128)(2,1)S(1)} %add_convert_fusion), channel_id=1, replica_groups=mesh['zh'=4,'zl'=4,'yl'=2,'x'=4,'yh'=2,'core'=2] {'x'}, dimensions={0} | all-to-all | bytes 1769472 | tf_op jit(solution)/shard_map/cond/branch_1_fun/all_to_all | solution.py:402
  131.0 6.0 %all-to-all-start.3 = ((bf16[16,3,24,128]{3,2,1,0:T(8,128)(2,1)}), bf16[16,3,24,128]{3,2,1,0:T(8,128)(2,1)S(1)}, u32[]{:S(2)}, u32[]{:S(2)}) async-start(bf16[16,3,24,128]{3,2,1,0:T(8,128)(2,1)} %by_channel.1), calls=%async_computation.3 | async-start | bytes 589824 | tf_op jit(solution)/shard_map/all_to_all | solution.py:409
  138.0 3.4 %collective-permute-start.10 = (bf16[2,512,384]{2,1,0:T(8,128)(2,1)}, bf16[2,512,384]{2,1,0:T(8,128)(2,1)}, u32[]{:S(2)}, u32[]{:S(2)}) collective-permute-start(bf16[2,512,384]{2,1,0:T(8,128)(2,1)} %once.7), channel_id=1, source_target_pairs={{0,4},{4,8},{8,12},{6,2},{10,6},{14,10},{1,5},{5,9},{9,13},{7,3},{... | collective-permute-start | bytes 2359304 | tf_op jit(solution)/shard_map/ppermute | solution.py:358
  141.3 14.4 %all-to-all-done.3.in_ref = bf16[16,3,24,128]{3,2,1,0:T(8,128)(2,1)S(1)} async-done(((bf16[16,3,24,128]{3,2,1,0:T(8,128)(2,1)}), bf16[16,3,24,128]{3,2,1,0:T(8,128)(2,1)S(1)}, u32[]{:S(2)}, u32[]{:S(2)}) %all-to-all-start.3) | async-done | bytes 294944 | tf_op jit(solution)/shard_map/all_to_all | solution.py:409
  156.4 5.0 %all-to-all-start.4 = ((bf16[4,24,128]{2,1,0:T(8,128)(2,1)}), bf16[4,24,128]{2,1,0:T(8,128)(2,1)S(1)}, u32[]{:S(2)}, u32[]{:S(2)}) async-start(bf16[4,24,128]{2,1,0:T(8,128)(2,1)} %add_parts.1), calls=%async_computation.4 | async-start | bytes 49152 | tf_op jit(solution)/shard_map/all_to_all | solution.py:414
  161.4 7.6 %backward.1 = (bf16[2,512,768]{2,1,0:T(8,128)(2,1)}, f32[8,128]{1,0:T(8,128)S(1)}) custom-call(bf16[2,512,768]{2,1,0:T(8,128)(2,1)} %in_ref.3, bf16[2,512,768]{2,1,0:T(8,128)(2,1)} %cot_ref.1, bf16[2,512,384]{2,1,0:T(8,128)(2,1)S(1)} %collective-permute-done.8.in_ref.partner_ref, bf16[2,512,384]{2,1,0:T(8,128)(2,1)} %get-tuple-element.21.pre_ref, ...), custom_call_target="tpu_custom_call" | custom-call | flops 1811939328 | bytes 12582912 | tf_op jit(solution)/shard_map/backward/pallas_call | solution.py:339
  (40 shorter events, 11.9 us)
Async XLA Ops:
  18.7 53.7 %copy-start.4 = (bf16[512,768]{1,0:T(8,128)(2,1)}, bf16[512,768]{1,0:T(8,128)(2,1)S(1)}, u32[]{:S(2)}) copy-start(bf16[512,768]{1,0:T(8,128)(2,1)S(1)} %get-tuple-element.19.refs_2_) | copy-start | bytes 2359300
  18.8 53.7 %copy-start.5 = (bf16[512,768]{1,0:T(8,128)(2,1)}, bf16[512,768]{1,0:T(8,128)(2,1)S(1)}, u32[]{:S(2)}) copy-start(bf16[512,768]{1,0:T(8,128)(2,1)S(1)} %get-tuple-element.20.refs_3_) | copy-start | bytes 2359300
  18.8 22.2 %collective-permute-start = (bf16[512,768]{1,0:T(8,128)(2,1)S(1)}, bf16[512,768]{1,0:T(8,128)(2,1)S(1)}, u32[]{:S(2)}, u32[]{:S(2)}) collective-permute-start(bf16[512,768]{1,0:T(8,128)(2,1)S(1)} %get-tuple-element.19.refs_2_), channel_id=1, source_target_pairs={{0,2},{2,0},{1,3},{3,1},{4,6},{6,4},{5,7},{7,5},{8,10},{10,8},{9,1... | collective-permute-start | bytes 2359304 | tf_op jit(solution)/shard_map/ppermute | solution.py:352
  23.1 30.2 %all-to-all-start.2 = ((bf16[4,48,768]{2,1,0:T(8,128)(2,1)}), bf16[4,48,768]{2,1,0:T(8,128)(2,1)S(1)}, u32[]{:S(2)}, u32[]{:S(2)}) async-start(bf16[4,48,768]{2,1,0:T(8,128)(2,1)} %assemble.1), calls=%async_computation.2 | async-start | bytes 589824 | tf_op jit(solution)/shard_map/all_to_all | solution.py:386
  37.1 23.7 %collective-permute-start.2 = (bf16[512,768]{1,0:T(8,128)(2,1)S(1)}, bf16[512,768]{1,0:T(8,128)(2,1)S(1)}, u32[]{:S(2)}, u32[]{:S(2)}) collective-permute-start(bf16[512,768]{1,0:T(8,128)(2,1)S(1)} %get-tuple-element.20.refs_3_), channel_id=1, source_target_pairs={{0,2},{2,0},{1,3},{3,1},{4,6},{6,4},{5,7},{7,5},{8,10},{10,8},{9,1... | collective-permute-start | bytes 2359304 | tf_op jit(solution)/shard_map/ppermute | solution.py:352
  41.0 32.2 %copy-start = (bf16[512,768]{1,0:T(8,128)(2,1)}, bf16[512,768]{1,0:T(8,128)(2,1)S(1)}, u32[]{:S(2)}) copy-start(bf16[512,768]{1,0:T(8,128)(2,1)S(1)} %collective-permute-done.refs_0_.refs_4_) | copy-start | bytes 2359300
  41.0 31.4 %collective-permute-start.1 = (bf16[512,768]{1,0:T(8,128)(2,1)S(1)}, bf16[512,768]{1,0:T(8,128)(2,1)}, u32[]{:S(2)}, u32[]{:S(2)}) collective-permute-start(bf16[512,768]{1,0:T(8,128)(2,1)S(1)} %collective-permute-done.refs_0_.refs_4_), channel_id=1, source_target_pairs={{0,4},{4,8},{8,12},{6,2},{10,6},{14,10},{1,5},{5,9},{9,13},{7,3},{... | collective-permute-start | bytes 2359304 | tf_op jit(solution)/shard_map/ppermute | solution.py:358
  53.4 19.0 %collective-permute-start.4 = (bf16[4,48,768]{2,1,0:T(8,128)(2,1)S(1)}, bf16[4,48,768]{2,1,0:T(8,128)(2,1)S(1)}, u32[]{:S(2)}, u32[]{:S(2)}) collective-permute-start(bf16[4,48,768]{2,1,0:T(8,128)(2,1)S(1)} %once.4), channel_id=1, source_target_pairs={{0,64},{32,96},{64,0},{96,32},{1,65},{33,97},{65,1},{97,33},{2,66}... | collective-permute-start | bytes 884744 | tf_op jit(solution)/shard_map/ppermute | solution.py:363
  60.9 27.8 %copy-start.1 = (bf16[512,768]{1,0:T(8,128)(2,1)}, bf16[512,768]{1,0:T(8,128)(2,1)S(1)}, u32[]{:S(2)}) copy-start(bf16[512,768]{1,0:T(8,128)(2,1)S(1)} %collective-permute-done.2.refs_1_.refs_5_) | copy-start | bytes 2359300
  60.9 17.2 %collective-permute-start.3 = (bf16[512,768]{1,0:T(8,128)(2,1)S(1)}, bf16[512,768]{1,0:T(8,128)(2,1)S(1)}, u32[]{:S(2)}, u32[]{:S(2)}) collective-permute-start(bf16[512,768]{1,0:T(8,128)(2,1)S(1)} %collective-permute-done.2.refs_1_.refs_5_), channel_id=1, source_target_pairs={{0,4},{4,8},{8,12},{6,2},{10,6},{14,10},{1,5},{5,9},{9,13},{7,3},{... | collective-permute-start | bytes 2359304 | tf_op jit(solution)/shard_map/ppermute | solution.py:358
  73.2 17.5 %copy-start.2 = (bf16[2,4,48,768]{3,2,1,0:T(8,128)(2,1)}, bf16[2,4,48,768]{3,2,1,0:T(8,128)(2,1)S(1)}, u32[]{:S(2)}) copy-start(bf16[2,4,48,768]{3,2,1,0:T(8,128)(2,1)S(1)} %once.5.refs_7_) | copy-start | bytes 1769476
  73.2 15.4 %collective-permute-start.5 = (bf16[2,4,48,768]{3,2,1,0:T(8,128)(2,1)S(1)}, bf16[2,4,48,768]{3,2,1,0:T(8,128)(2,1)S(1)}, u32[]{:S(2)}, u32[]{:S(2)}) collective-permute-start(bf16[2,4,48,768]{3,2,1,0:T(8,128)(2,1)S(1)} %once.5.refs_7_), channel_id=1, source_target_pairs={{0,32},{32,0},{64,96},{96,64},{1,33},{33,1},{65,97},{97,65},{2,34}... | collective-permute-start | bytes 1769480 | tf_op jit(solution)/shard_map/ppermute | solution.py:363
  75.1 15.6 %collective-permute-start.6 = (bf16[2,4,48,768]{3,2,1,0:T(8,128)(2,1)S(1)}, bf16[2,4,48,768]{3,2,1,0:T(8,128)(2,1)S(1)}, u32[]{:S(2)}, u32[]{:S(2)}) collective-permute-start(bf16[2,4,48,768]{3,2,1,0:T(8,128)(2,1)S(1)} %once.5.refs_7_), channel_id=1, source_target_pairs={{0,1},{1,0},{2,3},{3,2},{4,5},{5,4},{6,7},{7,6},{8,9},{9,8},{10,11... | collective-permute-start | bytes 1769480 | tf_op jit(solution)/shard_map/ppermute | solution.py:367
  78.0 12.6 %copy-start.7 = (bf16[512,768]{1,0:T(8,128)(2,1)}, bf16[512,768]{1,0:T(8,128)(2,1)S(1)}, u32[]{:S(2)}) copy-start(bf16[512,768]{1,0:T(8,128)(2,1)S(1)} %collective-permute-done.3.refs_1_) | copy-start | bytes 2359300
  88.7 4.0 %collective-permute-start.7 = (bf16[2,4,48,768]{3,2,1,0:T(8,128)(2,1)S(1)}, bf16[2,4,48,768]{3,2,1,0:T(8,128)(2,1)}, u32[]{:S(2)}, u32[]{:S(2)}) collective-permute-start(bf16[2,4,48,768]{3,2,1,0:T(8,128)(2,1)S(1)} %once.6.refs_8_), channel_id=1, source_target_pairs={{0,1},{1,0},{2,3},{3,2},{4,5},{5,4},{6,7},{7,6},{8,9},{9,8},{10,11... | collective-permute-start | bytes 1769480 | tf_op jit(solution)/shard_map/ppermute | solution.py:367
  92.7 1.1 copy-start.3
  106.0 5.9 %collective-permute-start.9 = (bf16[4,3,48,768]{3,2,1,0:T(8,128)(2,1)}, bf16[4,3,48,768]{3,2,1,0:T(8,128)(2,1)S(1)}, u32[]{:S(2)}, u32[]{:S(2)}) collective-permute-start(bf16[4,3,48,768]{3,2,1,0:T(8,128)(2,1)} %get-tuple-element.22), channel_id=1, source_target_pairs={{0,1},{1,0},{2,3},{3,2},{4,5},{5,4},{6,7},{7,6},{8,9},{9,8},{10,11... | collective-permute-start | bytes 2654216 | tf_op jit(solution)/shard_map/ppermute | solution.py:367
  108.0 28.9 %collective-permute-start.8 = (bf16[2,512,384]{2,1,0:T(8,128)(2,1)}, bf16[2,512,384]{2,1,0:T(8,128)(2,1)S(1)}, u32[]{:S(2)}, u32[]{:S(2)}) collective-permute-start(bf16[2,512,384]{2,1,0:T(8,128)(2,1)} %get-tuple-element.21.pre_ref), channel_id=1, source_target_pairs={{0,2},{2,0},{1,3},{3,1},{4,6},{6,4},{5,7},{7,5},{8,10},{10,8},{9,1... | collective-permute-start | bytes 2359304 | tf_op jit(solution)/shard_map/ppermute | solution.py:352
  129.9 1.1 copy-start.6
  131.0 24.7 %all-to-all-start.3 = ((bf16[16,3,24,128]{3,2,1,0:T(8,128)(2,1)}), bf16[16,3,24,128]{3,2,1,0:T(8,128)(2,1)S(1)}, u32[]{:S(2)}, u32[]{:S(2)}) async-start(bf16[16,3,24,128]{3,2,1,0:T(8,128)(2,1)} %by_channel.1), calls=%async_computation.3 | async-start | bytes 589824 | tf_op jit(solution)/shard_map/all_to_all | solution.py:409
  138.0 23.5 %collective-permute-start.10 = (bf16[2,512,384]{2,1,0:T(8,128)(2,1)}, bf16[2,512,384]{2,1,0:T(8,128)(2,1)}, u32[]{:S(2)}, u32[]{:S(2)}) collective-permute-start(bf16[2,512,384]{2,1,0:T(8,128)(2,1)} %once.7), channel_id=1, source_target_pairs={{0,4},{4,8},{8,12},{6,2},{10,6},{14,10},{1,5},{5,9},{9,13},{7,3},{... | collective-permute-start | bytes 2359304 | tf_op jit(solution)/shard_map/ppermute | solution.py:358
  156.4 12.6 %all-to-all-start.4 = ((bf16[4,24,128]{2,1,0:T(8,128)(2,1)}), bf16[4,24,128]{2,1,0:T(8,128)(2,1)S(1)}, u32[]{:S(2)}, u32[]{:S(2)}) async-start(bf16[4,24,128]{2,1,0:T(8,128)(2,1)} %add_parts.1), calls=%async_computation.4 | async-start | bytes 49152 | tf_op jit(solution)/shard_map/all_to_all | solution.py:414
